TPU v7x, 128 devices: a whole 4x4x4 slice. The times are simulated.
128 devices in a mesh: blk: 16 (over z, y_lo, core), exp: 8 (over y_hi, x).
Axes of the slice: x: 4, y: 4 (y_hi: 2, y_lo: 2; y = y_hi * 2 + y_lo), z: 4, core: 2. Of those that a mesh axis runs over, the one named last changes fastest.
Arguments:
- nodes: bfloat16 [24576, 512], P('blk'), may hold values from -8 to 8
- attention_weights: bfloat16 [3, 256, 512], P(None, 'exp'), may hold values from -1.5 to 1.5
- output_weight: bfloat16 [256, 512], P('exp'), may hold values from -2 to 2
- router_weight: bfloat16 [8, 512], replicated, may hold values from -1.25 to 1.25
- gain_first: float32 [512], replicated, may hold values from 0.1 to 1.9
- gain_second: float32 [512], replicated, may hold values from 0.1 to 1.9
- expert_in: bfloat16 [8, 2048, 512], P('exp', 'blk'), may hold values from -0.25 to 0.25
- expert_out: bfloat16 [8, 2048, 512], P('exp', 'blk'), may hold values from -0.125 to 0.125
- routes: int32 [24576, 2], P(('blk', 'exp')), may hold values from 0 to 7, all different within a row; in each aligned block of 192 rows (0 to 191, 192 to 383, ...) at most 96 rows name the same one
- cotangent: bfloat16 [24576, 512], P(('blk', 'exp')), may hold values from -6 to 6
Outputs:
- layer_out: bfloat16 [24576, 512], P(('blk', 'exp'))
- stream_grad: bfloat16 [24576, 512], P(('blk', 'exp'))
- expert_in_grad: float32 [8, 2048, 512], P('exp', 'blk')
- expert_out_grad: float32 [8, 2048, 512], P('exp', 'blk')
- router_grad: float32 [8, 512], replicated
- gain_grad: float32 [512], replicated
Inputs may be any that keep to these rules, and one draw needn't show every extreme that they name: `routes`: each row names two different experts. Among the rows of one device (aligned blocks of 192 rows) no expert is named by more than 96 rows, and in some block one expert is named by exactly 96 rows.
All inputs are finite; a program needn't handle non-finite values.
Results may differ from a plain program's by a relative error of at most 0.04.
The roundings to bfloat16 on the way count: a program that leaves them out, or rounds other values in their place, can miss the bound.
Values may be sent and summed in bfloat16 or wider, within the bound.
No kernel may reach another device: no remote copies, remote signals or barrier semaphores. Data moves between devices by JAX's collectives and lax.ppermute only.
A program may use at most 64 MiB of HBM per device.

v0:
```python
import math

import jax
import jax.numpy as jnp
from jax import lax
from jax.sharding import PartitionSpec as P

HD = 32


EPSILON = 1e-06
NEG_LARGE = -1e30


def rms_gain(stream, gain):
    return stream * lax.rsqrt(jnp.mean(stream * stream, axis=-1, keepdims=True) + EPSILON) * gain


def gelu_tanh(values):
    return jax.nn.gelu(values, approximate=True)


def to_sources(buffer):
    return lax.all_to_all(buffer, "exp", split_axis=0, concat_axis=0, tiled=True)


def local(
    nodes,
    attention_weights,
    output_weight,
    router_weight,
    gain_first,
    gain_second,
    expert_in,
    expert_out,
    routes,
    cotangent,
):
    exp_count = lax.axis_size("exp")
    blk_count = lax.axis_size("blk")
    block_rows = nodes.shape[0]
    width = nodes.shape[1]
    features = attention_weights.shape[1]
    heads_here = features // HD
    own_rows = block_rows // exp_count
    capacity = 4 * block_rows // (exp_count * exp_count)
    experts = router_weight.shape[0]
    grad_scale = 1.0 / math.sqrt(block_rows * blk_count)
    score_scale = 1.0 / math.sqrt(HD)
    query = jnp.einsum(
        "td,fd->tf", nodes, attention_weights[0], preferred_element_type=jnp.float32
    ).astype(jnp.bfloat16)
    query_heads = query.reshape(block_rows, heads_here, HD).transpose(1, 0, 2)
    keys_values = jnp.einsum(
        "td,cfd->cft", nodes, attention_weights[1:], preferred_element_type=jnp.float32
    ).astype(jnp.bfloat16)
    start_state = (
        jnp.full((heads_here, block_rows), NEG_LARGE, jnp.float32),
        jnp.zeros((heads_here, block_rows), jnp.float32),
        jnp.zeros((heads_here, block_rows, HD), jnp.float32),
    )
    totals = start_state
    shard_piece = lax.all_gather(keys_values, "blk", axis=2, tiled=True)
    length = shard_piece.shape[2]
    key_width = math.gcd(length, 1024)
    key_blocks = shard_piece.reshape(2, heads_here, HD, length // key_width, key_width).transpose(
        3, 0, 1, 2, 4
    )

    def key_step(running, key_block):
        run_max, run_sum, accum = running
        scores = (
            jnp.einsum(
                "htf,hfk->htk", query_heads, key_block[0], preferred_element_type=jnp.float32
            )
            * score_scale
        )
        new_max = jnp.maximum(run_max, jnp.max(scores, axis=-1))
        shrink = jnp.exp(run_max - new_max)
        weights = jnp.exp(scores - new_max[..., None])
        run_sum = run_sum * shrink + jnp.sum(weights, axis=-1)
        update = jnp.einsum(
            "htk,hfk->htf",
            weights.astype(jnp.bfloat16),
            key_block[1],
            preferred_element_type=jnp.float32,
        )
        accum = accum * shrink[..., None] + update
        return ((new_max, run_sum, accum), None)

    totals, _ = lax.scan(key_step, totals, key_blocks)
    run_max, run_sum, accum = totals
    attended = (accum / run_sum[..., None]).astype(jnp.bfloat16)
    by_rows = attended.transpose(1, 0, 2).reshape(block_rows, features)
    attn_out = lax.psum_scatter(
        jnp.dot(by_rows, output_weight, preferred_element_type=jnp.float32).astype(jnp.bfloat16),
        "exp",
        scatter_dimension=0,
        tiled=True,
    ).astype(jnp.float32)
    own_nodes = lax.dynamic_slice_in_dim(
        nodes, lax.axis_index("exp") * own_rows, own_rows, 0
    ).astype(jnp.float32)
    stream = rms_gain(own_nodes + attn_out, gain_first).astype(jnp.bfloat16)
    logits = jnp.dot(stream, router_weight.T, preferred_element_type=jnp.float32)
    flat_routes = routes.reshape(2 * own_rows)
    choose = (flat_routes[:, None] == jnp.arange(experts, dtype=jnp.int32)[None, :]).astype(
        jnp.int32
    )
    before = jnp.cumsum(choose, axis=0) - choose
    slot_index = jnp.sum(before * choose, axis=1)
    position = flat_routes * capacity + slot_index
    dispatch_table = (
        jnp.arange(experts * capacity, dtype=jnp.int32)[:, None] == position[None, :]
    ).astype(jnp.bfloat16)
    selected = choose.reshape(own_rows, 2, experts).astype(jnp.float32)

    def gate_values(values):
        picked = jnp.sum(jax.nn.sigmoid(values)[:, None, :] * selected, axis=-1)
        return picked / jnp.sum(picked, axis=-1, keepdims=True)

    gates, gate_back = jax.vjp(gate_values, logits)
    repeated = jnp.repeat(stream, 2, axis=0)
    outgoing = jnp.dot(dispatch_table, repeated, preferred_element_type=jnp.float32).astype(
        jnp.bfloat16
    )
    outgoing = outgoing.reshape(experts, capacity, width)
    weight_rows_in, weight_rows_out = (
        lax.all_gather(expert_in[0], "blk", axis=0, tiled=True),
        lax.all_gather(expert_out[0], "blk", axis=0, tiled=True),
    )
    arrived = lax.all_to_all(outgoing, "exp", split_axis=0, concat_axis=0, tiled=True)
    pre_act = jnp.einsum("scd,hd->sch", arrived, weight_rows_in, preferred_element_type=jnp.float32)
    expert_hidden = gelu_tanh(pre_act).astype(jnp.bfloat16)
    result = jnp.einsum(
        "sch,hd->scd", expert_hidden, weight_rows_out, preferred_element_type=jnp.float32
    ).astype(jnp.bfloat16)
    received, pre_act, returned = (arrived, pre_act, to_sources(result))
    expert_rows = jnp.einsum(
        "ps,pd->sd",
        dispatch_table,
        returned.reshape(experts * capacity, width),
        preferred_element_type=jnp.float32,
    )
    expert_rows = expert_rows.reshape(own_rows, 2, width)
    mixture = gates[:, 0:1] * expert_rows[:, 0] + gates[:, 1:2] * expert_rows[:, 1]
    stream_two = stream.astype(jnp.float32) + mixture
    normed, norm_back = jax.vjp(rms_gain, stream_two, gain_second)
    layer_out = normed.astype(jnp.bfloat16)
    grad_two, gain_part = norm_back(cotangent.astype(jnp.float32))
    gate_grads = jnp.sum(expert_rows * grad_two[:, None, :], axis=-1)
    assigned_grads = (
        (gates[..., None] * grad_two[:, None, :]).astype(jnp.bfloat16).reshape(2 * own_rows, width)
    )
    grad_outgoing = jnp.dot(
        dispatch_table, assigned_grads, preferred_element_type=jnp.float32
    ).astype(jnp.bfloat16)
    grad_arrived = lax.all_to_all(
        grad_outgoing.reshape(experts, capacity, width),
        "exp",
        split_axis=0,
        concat_axis=0,
        tiled=True,
    )
    again_in, again_out = (
        lax.all_gather(expert_in[0], "blk", axis=0, tiled=True),
        lax.all_gather(expert_out[0], "blk", axis=0, tiled=True),
    )
    hidden_full, gelu_back = jax.vjp(gelu_tanh, pre_act)
    hidden = hidden_full.astype(jnp.bfloat16)
    hidden_grad = jnp.einsum(
        "scd,hd->sch", grad_arrived, again_out, preferred_element_type=jnp.float32
    )
    pre_grad = gelu_back(hidden_grad)[0].astype(jnp.bfloat16)
    term_in = jnp.einsum("sch,scd->hd", pre_grad, received, preferred_element_type=jnp.float32)
    term_out = jnp.einsum("sch,scd->hd", hidden, grad_arrived, preferred_element_type=jnp.float32)
    summed_grads = lax.psum_scatter(
        (jnp.concatenate([term_in, term_out], axis=1) * grad_scale).astype(jnp.bfloat16),
        "blk",
        scatter_dimension=0,
        tiled=True,
    ).astype(jnp.float32)
    expert_in_grad = summed_grads[None, :, :width]
    expert_out_grad = summed_grads[None, :, width:]
    rows_back = jnp.einsum(
        "sch,hd->scd", pre_grad, again_in, preferred_element_type=jnp.float32
    ).astype(jnp.bfloat16)
    back_home = to_sources(rows_back)
    back_rows = jnp.einsum(
        "ps,pd->sd",
        dispatch_table,
        back_home.reshape(experts * capacity, width),
        preferred_element_type=jnp.float32,
    )
    back_rows = back_rows.reshape(own_rows, 2, width)
    logit_grad = gate_back(gate_grads)[0]
    router_part = (
        jnp.dot(logit_grad.T, stream.astype(jnp.float32), precision=lax.Precision.HIGHEST)
        * grad_scale
    )
    router_grad, gain_grad = lax.psum((router_part, gain_part * grad_scale), ("blk", "exp"))
    router_term = jnp.dot(
        logit_grad, router_weight.astype(jnp.float32), precision=lax.Precision.HIGHEST
    )
    stream_grad = (grad_two + (back_rows[:, 0] + back_rows[:, 1]) + router_term).astype(
        jnp.bfloat16
    )
    return (layer_out, stream_grad, expert_in_grad, expert_out_grad, router_grad, gain_grad)


def solution(mesh):
    placed = (
        P("blk", None),
        P(None, "exp", None),
        P("exp", None),
        P(),
        P(),
        P(),
        P("exp", "blk", None),
        P("exp", "blk", None),
        P(("blk", "exp"), None),
        P(("blk", "exp"), None),
    )
    return jax.shard_map(
        local,
        mesh=mesh,
        in_specs=placed,
        out_specs=(
            P(("blk", "exp"), None),
            P(("blk", "exp"), None),
            P("exp", "blk", None),
            P("exp", "blk", None),
            P(),
            P(),
        ),
        check_vma=False,
    )
```

profile of v0, /device:TPU:0, one launch (start us, length us, event | category | flops | bytes accessed | tf_op | source)
XLA Modules:
  0.0 604.2 jit_solution(10231152198393182954)
XLA Ops:
  7.2 2.7 convolution_convert_fusion.1
  12.3 36.6 %all-gather.6.cloned.1.call-done = bf16[2,32,24576]{2,1,0:T(8,128)(2,1)} async-done(((bf16[2,32,1536]{2,1,0:T(8,128)(2,1)}), bf16[2,32,24576]{2,1,0:T(8,128)(2,1)}) %all-gather.6.cloned.1.call-update) | async-done | bytes 3145744 | tf_op jit(solution)/shard_map/all_gather | solution.py:63
  48.8 3.7 copy.60
  52.6 3.4 copy.66
  56.0 231.9 %while.15 = (s32[]{:T(128)}, f32[1,1536]{1,0:T(1,128)S(1)}, f32[1,1536]{1,0:T(1,128)S(1)}, f32[1,1536,32]{1,2,0:T(8,128)S(1)}, bf16[24,2,1,32,1024]{4,3,2,1,0:T(...) while((s32[]{:T(128)}, f32[1,1536]{1,0:T(1,128)S(1)}, ...), condition=%wide.region_3.4_spmd.clone, body=%wide.region_0.3_spmd.clone.sunk | while | flops 214066176 | bytes 44767396 | solution.py:91
  58.0 2.6 copy-done.1
  61.7 4.0 fusion.103
  67.6 2.6 copy-done.1
  71.3 4.0 fusion.103
  77.3 2.6 copy-done.1
  81.0 4.0 fusion.103
  86.9 2.6 copy-done.1
  90.7 4.0 fusion.103
  96.6 2.6 copy-done.1
  100.3 4.0 fusion.103
  106.3 2.6 copy-done.1
  110.0 4.0 fusion.103
  115.9 2.6 copy-done.1
  119.6 4.0 fusion.103
  125.6 2.6 copy-done.1
  129.3 4.0 fusion.103
  135.3 2.6 copy-done.1
  139.0 4.0 fusion.103
  144.9 2.6 copy-done.1
  148.6 4.0 fusion.103
  154.6 2.6 copy-done.1
  158.3 4.0 fusion.103
  164.3 2.6 copy-done.1
  168.0 4.0 fusion.103
  173.9 2.6 copy-done.1
  177.6 4.0 fusion.103
  183.6 2.6 copy-done.1
  187.3 4.0 fusion.103
  193.2 2.6 copy-done.1
  196.9 4.0 fusion.103
  202.9 2.6 copy-done.1
  206.6 4.0 fusion.103
  212.6 2.6 copy-done.1
  216.3 4.0 fusion.103
  222.2 2.6 copy-done.1
  225.9 4.0 fusion.103
  231.9 2.6 copy-done.1
  235.6 4.0 fusion.103
  245.3 4.0 fusion.103
  254.9 4.0 fusion.103
  264.6 4.0 fusion.103
  274.3 4.0 fusion.103
  283.9 4.0 fusion.103
  292.8 71.2 %reduce-scatter.5.cloned.1.call-done = bf16[192,512]{1,0:T(8,128)(2,1)} async-done(((bf16[1536,512]{1,0:T(8,128)(2,1)}), bf16[192,512]{1,0:T(8,128)(2,1)}) %reduce-scatter.5.cloned.1.call-update) | async-done | bytes 196624 | tf_op jit(solution)/shard_map/reduce_scatter | solution.py:95
  368.3 4.3 all-to-all-start
  373.8 30.2 %all-gather.8.cloned.1.call-done = bf16[1,2048,512]{2,1,0:T(8,128)(2,1)} async-done(((bf16[1,128,512]{2,1,0:T(8,128)(2,1)}), bf16[1,2048,512]{2,1,0:T(8,128)(2,1)}) %all-gather.8.cloned.1.call-update) | async-done | bytes 2097168 | tf_op jit(solution)/shard_map/all_gather | solution.py:129
  404.0 6.1 %fusion.32 = f32[8,96,2048]{2,1,0:T(8,128)} fusion(bf16[8,96,512]{2,1,0:T(8,128)(2,1)S(1)} %all-to-all-done, bf16[1,2048,512]{2,1,0:T(8,128)(2,1)} %all-gather.8.cloned.1.call-done), kind=kOutput, calls=%fused_computation.46 | convolution fusion | flops 1610612736 | bytes 9175040 | tf_op jit(solution)/shard_map/scd,hd->sch/dot_general | solution.py:133
  410.1 30.7 %all-gather.10.cloned.1.call-done = bf16[1,2048,512]{2,1,0:T(8,128)(2,1)} async-done(((bf16[1,128,512]{2,1,0:T(8,128)(2,1)}), bf16[1,2048,512]{2,1,0:T(8,128)(2,1)}) %all-gather.10.cloned.1.call-update) | async-done | bytes 2097168 | tf_op jit(solution)/shard_map/all_gather | solution.py:130
  440.8 6.5 %fusion.38 = bf16[8,96,512]{2,1,0:T(8,128)(2,1)} fusion(bf16[1,2048,512]{2,1,0:T(8,128)(2,1)} %all-gather.10.cloned.1.call-done, f32[8,96,2048]{2,1,0:T(8,128)} %fusion.32), kind=kOutput, calls=%fused_computation.50 | convolution fusion | flops 1625161728 | bytes 9175040 | tf_op jit(solution)/shard_map/sch,hd->scd/dot_general | solution.py:135
  447.2 6.2 %all-to-all-start.1 = ((bf16[8,96,512]{2,1,0:T(8,128)(2,1)}), bf16[8,96,512]{2,1,0:T(8,128)(2,1)S(1)}, u32[]{:S(2)}, u32[]{:S(2)}) async-start(bf16[8,96,512]{2,1,0:T(8,128)(2,1)} %fusion.38), calls=%async_computation.2 | async-start | bytes 1572864 | tf_op jit(solution)/shard_map/all_to_all | solution.py:24
  454.0 14.2 %all-to-all-done.1 = bf16[8,96,512]{2,1,0:T(8,128)(2,1)S(1)} async-done(((bf16[8,96,512]{2,1,0:T(8,128)(2,1)}), bf16[8,96,512]{2,1,0:T(8,128)(2,1)S(1)}, u32[]{:S(2)}, u32[]{:S(2)}) %all-to-all-start.1) | async-done | bytes 786464 | tf_op jit(solution)/shard_map/all_to_all | solution.py:24
  474.6 17.2 %all_to_all.20 = bf16[8,96,512]{2,1,0:T(8,128)(2,1)S(1)} all-to-all(bf16[8,96,512]{2,1,0:T(8,128)(2,1)S(1)} %bitcast.131), channel_id=1, replica_groups=mesh['blk'=16,'exp'=8] {'exp'}, dimensions={0} | all-to-all | bytes 1572864 | tf_op jit(solution)/shard_map/all_to_all | solution.py:158
  491.9 7.8 %fusion.25 = bf16[8,96,2048]{2,1,0:T(8,128)(2,1)S(1)} fusion(f32[8,96,2048]{2,1,0:T(8,128)} %fusion.32, bf16[8,96,512]{2,1,0:T(8,128)(2,1)S(1)} %all_to_all.20, bf16[1,2048,512]{2,1,0:T(8,128)(2,1)} %all-gather.10.cloned.1.call-done), kind=kOutput, calls=%fused_computation.32 | convolution fusion | flops 1642070016 | bytes 12320768 | tf_op jit(solution)/shard_map/scd,hd->sch/dot_general | solution.py:171
  499.7 2.9 convolution_bitcast_fusion
  504.5 2.6 fusion.18
  507.1 6.4 %copy.56 = bf16[2048,1024]{1,0:T(8,128)(2,1)} copy(bf16[2048,1024]{0,1:T(8,128)(2,1)} %fusion.18) | data formatting | bytes 8388608
  513.7 5.3 fusion.35
  519.0 3.5 all-to-all-start.3
  522.8 70.5 %all-reduce = (f32[8,512]{1,0:T(8,128)}, f32[512]{0:T(512)}) all-reduce(f32[8,512]{1,0:T(8,128)S(1)} %convolution_multiply_fusion, f32[512]{0:T(512)S(1)} %broadcast_multiply_fusion), channel_id=1, replica_groups=mesh['blk'=16,'exp'=8] {'blk','exp'}, use_global_device_ids=true, to_apply=%region_17.18 | all-reduce | flops 4608 | bytes 36864 | tf_op jit(solution)/shard_map/psum | solution.py:201
  (238 shorter events, 112.0 us)
Async XLA Ops:
  7.2 280.8 %copy-start = (bf16[32,512]{1,0:T(8,128)(2,1)S(1)}, bf16[32,512]{1,0:T(8,128)(2,1)}, u32[]{:S(2)}) copy-start(bf16[32,512]{1,0:T(8,128)(2,1)} %param.14) | copy-start | bytes 98308
  7.2 41.7 %all-gather.6.cloned.1.call-start = ((), (), s32[]{:S(2)}) async-start(), calls=%async_computation.6 | async-start | bytes 3342336 | tf_op jit(solution)/shard_map/all_gather | solution.py:63
  10.0 354.1 %reduce-scatter.5.cloned.1.call-start = ((), (), s32[]{:S(2)}) async-start(), calls=%async_computation.7 | async-start | bytes 1769472 | tf_op jit(solution)/shard_map/reduce_scatter | solution.py:95
  56.0 235.2 %copy-start.5 = (s32[192,2]{0,1:T(2,128)S(1)}, s32[192,2]{0,1:T(2,128)}, u32[]{:S(2)}) copy-start(s32[192,2]{0,1:T(2,128)} %param.20) | copy-start | bytes 4612
  56.0 309.2 %copy-start.7 = (f32[512]{0:T(512)S(1)}, f32[512]{0:T(512)}, u32[]{:S(2)}) copy-start(f32[512]{0:T(512)} %param.16) | copy-start | bytes 6148
  57.9 2.7 copy-start.1
  67.6 2.7 copy-start.1
  77.2 2.7 copy-start.1
  86.9 2.7 copy-start.1
  96.5 2.7 copy-start.1
  106.2 2.7 copy-start.1
  115.9 2.7 copy-start.1
  125.5 2.7 copy-start.1
  135.2 2.7 copy-start.1
  144.9 2.7 copy-start.1
  154.5 2.7 copy-start.1
  164.2 2.7 copy-start.1
  173.9 2.7 copy-start.1
  183.5 2.7 copy-start.1
  193.2 2.7 copy-start.1
  202.8 2.7 copy-start.1
  212.5 2.7 copy-start.1
  222.2 2.7 copy-start.1
  231.8 2.7 copy-start.1
  241.5 2.7 copy-start.1
  251.2 2.7 copy-start.1
  260.8 2.7 copy-start.1
  270.5 2.7 copy-start.1
  280.1 2.7 copy-start.1
  289.8 114.2 %all-gather.8.cloned.1.call-start = ((), (), s32[]{:S(2)}) async-start(), calls=%async_computation.8 | async-start | bytes 2228224 | tf_op jit(solution)/shard_map/all_gather | solution.py:129
  290.6 150.2 %all-gather.10.cloned.1.call-start = ((), (), s32[]{:S(2)}) async-start(), calls=%async_computation.9 | async-start | bytes 2228224 | tf_op jit(solution)/shard_map/all_gather | solution.py:130
  368.3 35.8 %all-to-all-start = ((bf16[8,96,512]{2,1,0:T(8,128)(2,1)}), bf16[8,96,512]{2,1,0:T(8,128)(2,1)S(1)}, u32[]{:S(2)}, u32[]{:S(2)}) async-start(bf16[8,96,512]{2,1,0:T(8,128)(2,1)} %bitcast.8), calls=%async_computation.1 | async-start | bytes 1572864 | tf_op jit(solution)/shard_map/all_to_all | solution.py:132
  410.1 43.4 %copy-start.4 = (bf16[8,512]{1,0:T(8,128)(2,1)S(1)}, bf16[8,512]{1,0:T(8,128)(2,1)}, u32[]{:S(2)}) copy-start(bf16[8,512]{1,0:T(8,128)(2,1)} %param.15) | copy-start | bytes 24580
  410.1 59.9 %copy-start.2 = (bf16[192,512]{1,0:T(8,128)(2,1)S(1)}, bf16[192,512]{1,0:T(8,128)(2,1)}, u32[]{:S(2)}) copy-start(bf16[192,512]{1,0:T(8,128)(2,1)} %param.21) | copy-start | bytes 589828
  410.1 59.9 %copy-start.6 = (f32[512]{0:T(512)S(1)}, f32[512]{0:T(512)}, u32[]{:S(2)}) copy-start(f32[512]{0:T(512)} %param.17) | copy-start | bytes 6148
  447.2 21.0 %all-to-all-start.1 = ((bf16[8,96,512]{2,1,0:T(8,128)(2,1)}), bf16[8,96,512]{2,1,0:T(8,128)(2,1)S(1)}, u32[]{:S(2)}, u32[]{:S(2)}) async-start(bf16[8,96,512]{2,1,0:T(8,128)(2,1)} %fusion.38), calls=%async_computation.2 | async-start | bytes 1572864 | tf_op jit(solution)/shard_map/all_to_all | solution.py:24
  453.4 141.4 %reduce-scatter.7.cloned.1.call-start = ((), (), s32[]{:S(2)}) async-start(), calls=%async_computation.10 | async-start | bytes 4456448
  474.6 25.0 %slice-start = ((s8[6291456]{0:T(1024)(128)(4,1)}), s8[4194304]{0:T(1024)(128)(4,1)S(1)}, s32[]{:S(2)}) async-start(s8[6291456]{0:T(1024)(128)(4,1)} %bitcast.127), calls=%async_computation.11 | async-start | bytes 8388608
  491.9 7.8 %slice-start.1 = ((s8[6291456]{0:T(1024)(128)(4,1)}), s8[2097152]{0:T(1024)(128)(4,1)S(1)}, s32[]{:S(2)}) async-start(s8[6291456]{0:T(1024)(128)(4,1)} %bitcast.127), calls=%async_computation.12 | async-start | bytes 4194304
  499.7 2.9 copy-start.8
  513.7 79.6 %copy-start.3 = (pred[192,2,768]{2,1,0:T(4,128)(4,1)S(1)}, pred[192,2,768]{2,1,0:T(4,128)(4,1)}, u32[]{:S(2)}) copy-start(pred[192,2,768]{2,1,0:T(4,128)(4,1)} %eq.74) | copy-start | bytes 884740
  519.0 74.3 %all-to-all-start.3 = ((bf16[8,96,512]{2,1,0:T(8,128)(2,1)}), bf16[8,96,512]{2,1,0:T(8,128)(2,1)S(1)}, u32[]{:S(2)}, u32[]{:S(2)}) async-start(bf16[8,96,512]{2,1,0:T(8,128)(2,1)} %fusion.35), calls=%async_computation.4 | async-start | bytes 1572864 | tf_op jit(solution)/shard_map/all_to_all | solution.py:24
Sparse Core Ops, SparseCore 0:
  10.2 38.5 all-gather.5
  289.9 74.0 reduce-scatter.4
  365.8 38.2 all-gather.7
  405.6 35.1 all-gather.9
  513.6 73.4 reduce-scatter.6
where the time goes:
time: 607 us; the launch traced here: 604 us
  waiting for transfers between devices  184 us (30%)
  matrix products  183 us (30%)
  blocking collectives  87.7 us (14%)
  local copies, waits for them, and re-layouts  84.3 us (14%)
  other arithmetic  35.3 us (6%)
  starting transfers between devices  14.2 us (2%)
  between operations  14.2 us (2%)
    dot_general x24, matrix products, key_step(): jnp.einsum('htk,hfk->htf', weights.astype(jnp.bfloat16), key_block[1], pr...  95.5 us
    reduce_scatter x1, waiting for transfers between devices, local(): lax.psum_scatter(jnp.dot(by_rows, output_weight, preferred_element_type=j...  71.2 us
    psum x1, blocking collectives, local(): lax.psum((router_part, gain_part * grad_scale), ('blk', 'exp'))  70.5 us
    while x72, local copies, waits for them, and re-layouts  62.5 us
    dot_general x24, matrix products, key_step(): jnp.einsum('htf,hfk->htk', query_heads, key_block[0], preferred_element_t...  45.2 us
    all_gather x1, waiting for transfers between devices, local(): shard_piece = lax.all_gather(keys_values, 'blk', axis=2, tiled=True)  36.6 us
    all_gather x1, waiting for transfers between devices, local(): lax.all_gather(expert_out[0], 'blk', axis=0, tiled=True)  30.7 us
    all_gather x1, waiting for transfers between devices, local(): lax.all_gather(expert_in[0], 'blk', axis=0, tiled=True)  30.2 us
  transfers between devices with their start and end apart: 8, of which 5 were waited for; matrix products, arithmetic and copies ran while one was open for 4% of the time, Pallas kernels for 0%

commit v1 on v0

--- a/solution.py
+++ b/solution.py
@@ -3,13 +3,17 @@
 import jax
 import jax.numpy as jnp
 from jax import lax
+from jax.experimental import pallas as pl
+from jax.experimental.pallas import tpu as pltpu
 from jax.sharding import PartitionSpec as P
 
 HD = 32
 
-
 EPSILON = 1e-06
-NEG_LARGE = -1e30
+LOG2_SCALE = math.log2(math.e) / math.sqrt(HD)
+SHIFT_KEYS = 256
+SUM_LIMIT = 2.0**100
+VMEM_LIMIT = 60 * 2**20
 
 
 def rms_gain(stream, gain):
@@ -22,6 +26,208 @@
 
 def to_sources(buffer):
     return lax.all_to_all(buffer, "exp", split_axis=0, concat_axis=0, tiled=True)
+
+
+def hop(value, axis, target):
+    count = lax.axis_size(axis)
+    return lax.ppermute(value, axis, [(i, target(i) % count) for i in range(count)])
+
+
+def split_terms(value, terms):
+    pieces = []
+    for _ in range(terms):
+        piece = value.astype(jnp.bfloat16)
+        pieces.append(piece)
+        value = value - piece.astype(jnp.float32)
+    return pieces
+
+
+def key_blocks(refs):
+    return [
+        (ref, start) for ref in refs for start in range(0, ref.shape[0], 2 * HD)
+    ]
+
+
+def load_keys(blocks, keys, values):
+    width = blocks[0][0].shape[1]
+    ones = (lax.broadcasted_iota(jnp.int32, (HD, width), 0) < 3).astype(jnp.bfloat16)
+    one = (lax.broadcasted_iota(jnp.int32, (HD // 2, width), 0) < 1).astype(jnp.bfloat16)
+    for index, (ref, start) in enumerate(blocks):
+        block = ref[start : start + HD, :]
+        span = slice(index * width, (index + 1) * width)
+        keys[span, :] = jnp.concatenate([block, block, block, ones], axis=0).T
+        values[:, span] = jnp.concatenate([ref[start + HD : start + 2 * HD, :], one], axis=0)
+
+
+def group_blocks(refs, count):
+    blocks = key_blocks(refs)
+    return [blocks[start : start + count] for start in range(0, len(blocks), count)]
+
+
+def add_blocks(count, width, query, keys, values, total):
+    chunk = width // 2
+
+    def step(index, running):
+        span = pl.ds(pl.multiple_of(index * chunk, chunk), chunk)
+        exponents = jnp.dot(keys[span, :], query, preferred_element_type=jnp.float32)
+        weights = jnp.exp2(exponents).astype(jnp.bfloat16)
+        return running + jnp.dot(values[:, span], weights, preferred_element_type=jnp.float32)
+
+    return lax.fori_loop(0, 2 * count, step, total)
+
+
+def first_keys_kernel(count, query_ref, *refs):
+    blocks, (wide_ref, total_ref, keys, values) = refs[:-4], refs[-4:]
+    load_keys(key_blocks(blocks), keys, values)
+    width = query_ref.shape[1]
+    scaled = query_ref[...].astype(jnp.float32) * LOG2_SCALE
+    pieces = split_terms(scaled, 3)
+    wide_ref[...] = jnp.concatenate(pieces + [jnp.zeros_like(pieces[0])], axis=0)
+    some = jnp.dot(keys[:SHIFT_KEYS, :], wide_ref[...], preferred_element_type=jnp.float32)
+    shift = split_terms(-jnp.max(some, axis=0, keepdims=True), 3)
+    row = lax.broadcasted_iota(jnp.int32, (HD, width), 0)
+    rows = jnp.zeros((HD, width), jnp.float32)
+    for index, piece in enumerate(shift):
+        rows = jnp.where(row == index, piece.astype(jnp.float32), rows)
+    wide_ref[3 * HD :, :] = rows.astype(jnp.bfloat16)
+    total_ref[...] = add_blocks(
+        count, width, wide_ref[...], keys, values, jnp.zeros(total_ref.shape, jnp.float32)
+    )
+
+
+def more_keys_kernel(count, wide_ref, before_ref, *refs):
+    blocks, (total_ref, keys, values) = refs[:-3], refs[-3:]
+    load_keys(key_blocks(blocks), keys, values)
+    total_ref[...] = add_blocks(
+        count, wide_ref.shape[1], wide_ref[...], keys, values, before_ref[...]
+    )
+
+
+def last_keys_kernel(count, fresh, wide_ref, before_ref, query_ref, *refs):
+    blocks, (out_ref, keys, values, total) = refs[:-4], refs[-4:]
+    load_keys(key_blocks(blocks[:fresh]), keys, values)
+    width = wide_ref.shape[1]
+    total[...] = add_blocks(count, width, wide_ref[...], keys, values, before_ref[...])
+    sums = total[HD : HD + 1, :]
+    inside = jnp.logical_and(sums <= SUM_LIMIT, sums >= 1.0 / SUM_LIMIT)
+    outside = jnp.sum(jnp.where(inside, 0, 1))
+
+    @pl.when(outside > 0)
+    def _():
+        query = query_ref[...]
+        query = jnp.concatenate([query, jnp.zeros((3 * HD, width), query.dtype)], axis=0)
+        total[...] = jnp.zeros(total.shape, jnp.float32)
+
+        def step(index, top):
+            span = pl.ds(pl.multiple_of(index * SHIFT_KEYS, SHIFT_KEYS), SHIFT_KEYS)
+            scores = LOG2_SCALE * jnp.dot(
+                keys[span, :], query, preferred_element_type=jnp.float32
+            )
+            new_top = jnp.maximum(top, jnp.max(scores, axis=0, keepdims=True))
+            weights = jnp.exp2(scores - new_top).astype(jnp.bfloat16)
+            total[...] = total[...] * jnp.exp2(top - new_top) + jnp.dot(
+                values[:, span], weights, preferred_element_type=jnp.float32
+            )
+            return new_top
+
+        top = jnp.full((1, width), -1e30, jnp.float32)
+        for group in group_blocks(blocks, count):
+            load_keys(group, keys, values)
+            top = lax.fori_loop(0, len(group) * (width // SHIFT_KEYS), step, top)
+
+    attended = (total[:HD, :] / total[HD : HD + 1, :]).astype(jnp.bfloat16)
+    rows = out_ref.shape[2]
+    for index in range(out_ref.shape[0]):
+        out_ref[index] = attended[:, index * rows : (index + 1) * rows]
+
+
+def block_count(arrays):
+    return sum(array.shape[0] for array in arrays) // (2 * HD)
+
+
+def attention_call(kernel, out_shape, operands, count, width, extra=(), aliases=None):
+    specs = [pl.BlockSpec(memory_space=pltpu.VMEM)]
+    return pl.pallas_call(
+        kernel,
+        out_shape=out_shape,
+        in_specs=specs * len(operands),
+        out_specs=jax.tree.map(lambda _: specs[0], out_shape),
+        scratch_shapes=[
+            pltpu.VMEM((count * width, 4 * HD), jnp.bfloat16),
+            pltpu.VMEM((HD + HD // 2, count * width), jnp.bfloat16),
+            *extra,
+        ],
+        input_output_aliases=aliases or {},
+        compiler_params=pltpu.CompilerParams(vmem_limit_bytes=VMEM_LIMIT),
+        cost_estimate=pl.CostEstimate(
+            flops=count * width * width * 1200,
+            transcendentals=count * width * width,
+            bytes_accessed=count * width * 4 * HD,
+        ),
+    )(*operands)
+
+
+def attention(query, keys_values, owners):
+    width = query.shape[1]
+    partner = hop(keys_values, "blk", lambda i: i ^ 1)
+    near = [
+        hop(keys_values, "blk", lambda i: i ^ 2),
+        hop(keys_values, "blk", lambda i: i + 4),
+        hop(keys_values, "blk", lambda i: i + 12),
+        hop(keys_values, "blk", lambda i: i + 8),
+    ]
+    beyond = hop(jnp.concatenate(near[1:], axis=0), "blk", lambda i: i ^ 2)
+    near_partner = hop(jnp.concatenate(near, axis=0), "blk", lambda i: i ^ 1)
+    beyond_partner = hop(beyond, "blk", lambda i: i ^ 1)
+    total_shape = jax.ShapeDtypeStruct((HD + HD // 2, width), jnp.float32)
+    wide_shape = jax.ShapeDtypeStruct((4 * HD, width), jnp.bfloat16)
+    first = [keys_values, partner]
+    wide, total = attention_call(
+        lambda *refs: first_keys_kernel(2, *refs), (wide_shape, total_shape), [query, *first], 2, width
+    )
+    for group in (near, [near_partner]):
+        count = block_count(group)
+        total = attention_call(
+            lambda *refs, count=count: more_keys_kernel(count, *refs),
+            total_shape,
+            [wide, total, *group],
+            count,
+            width,
+            aliases={1: 0},
+        )
+    last = [beyond, beyond_partner]
+    count = block_count(last)
+    attended = attention_call(
+        lambda *refs: last_keys_kernel(count, len(last), *refs),
+        jax.ShapeDtypeStruct((owners, HD, width // owners), jnp.bfloat16),
+        [wide, total, query, *last, *first, *near, near_partner],
+        count,
+        width,
+        extra=[pltpu.VMEM(total_shape.shape, jnp.float32)],
+    )
+    return attended, beyond_partner
+
+
+def gather_by_halves(rows, axis):
+    index = lax.axis_index(axis)
+    distance = 1
+    while distance < lax.axis_size(axis):
+        other = hop(rows, axis, lambda i, distance=distance: i ^ distance)
+        upper = (index // distance) % 2 == 1
+        rows = jnp.concatenate(
+            [jnp.where(upper, other, rows), jnp.where(upper, rows, other)], axis=0
+        )
+        distance *= 2
+    return rows
+
+
+def sum_by_halves(value, axes):
+    for axis in axes:
+        distance = 1
+        while distance < lax.axis_size(axis):
+            value = value + hop(value, axis, lambda i, distance=distance: i ^ distance)
+            distance *= 2
+    return value
 
 
 def local(
@@ -41,63 +247,30 @@
     block_rows = nodes.shape[0]
     width = nodes.shape[1]
     features = attention_weights.shape[1]
-    heads_here = features // HD
     own_rows = block_rows // exp_count
     capacity = 4 * block_rows // (exp_count * exp_count)
     experts = router_weight.shape[0]
     grad_scale = 1.0 / math.sqrt(block_rows * blk_count)
-    score_scale = 1.0 / math.sqrt(HD)
+    keys_values = jnp.einsum(
+        "fd,td->ft",
+        attention_weights[1:].reshape(2 * features, width),
+        nodes,
+        preferred_element_type=jnp.float32,
+    ).astype(jnp.bfloat16)
     query = jnp.einsum(
-        "td,fd->tf", nodes, attention_weights[0], preferred_element_type=jnp.float32
-    ).astype(jnp.bfloat16)
-    query_heads = query.reshape(block_rows, heads_here, HD).transpose(1, 0, 2)
-    keys_values = jnp.einsum(
-        "td,cfd->cft", nodes, attention_weights[1:], preferred_element_type=jnp.float32
-    ).astype(jnp.bfloat16)
-    start_state = (
-        jnp.full((heads_here, block_rows), NEG_LARGE, jnp.float32),
-        jnp.zeros((heads_here, block_rows), jnp.float32),
-        jnp.zeros((heads_here, block_rows, HD), jnp.float32),
-    )
-    totals = start_state
-    shard_piece = lax.all_gather(keys_values, "blk", axis=2, tiled=True)
-    length = shard_piece.shape[2]
-    key_width = math.gcd(length, 1024)
-    key_blocks = shard_piece.reshape(2, heads_here, HD, length // key_width, key_width).transpose(
-        3, 0, 1, 2, 4
-    )
-
-    def key_step(running, key_block):
-        run_max, run_sum, accum = running
-        scores = (
-            jnp.einsum(
-                "htf,hfk->htk", query_heads, key_block[0], preferred_element_type=jnp.float32
-            )
-            * score_scale
-        )
-        new_max = jnp.maximum(run_max, jnp.max(scores, axis=-1))
-        shrink = jnp.exp(run_max - new_max)
-        weights = jnp.exp(scores - new_max[..., None])
-        run_sum = run_sum * shrink + jnp.sum(weights, axis=-1)
-        update = jnp.einsum(
-            "htk,hfk->htf",
-            weights.astype(jnp.bfloat16),
-            key_block[1],
-            preferred_element_type=jnp.float32,
-        )
-        accum = accum * shrink[..., None] + update
-        return ((new_max, run_sum, accum), None)
-
-    totals, _ = lax.scan(key_step, totals, key_blocks)
-    run_max, run_sum, accum = totals
-    attended = (accum / run_sum[..., None]).astype(jnp.bfloat16)
-    by_rows = attended.transpose(1, 0, 2).reshape(block_rows, features)
-    attn_out = lax.psum_scatter(
-        jnp.dot(by_rows, output_weight, preferred_element_type=jnp.float32).astype(jnp.bfloat16),
-        "exp",
-        scatter_dimension=0,
-        tiled=True,
-    ).astype(jnp.float32)
+        "fd,td->ft", attention_weights[0], nodes, preferred_element_type=jnp.float32
+    ).astype(jnp.bfloat16)
+    attended, last_arrived = attention(query, keys_values, exp_count)
+    full_output_weight = gather_by_halves(output_weight, "exp")
+    both_weights, _ = lax.optimization_barrier(
+        (jnp.concatenate([expert_in, expert_out], axis=0), last_arrived)
+    )
+    all_weights = lax.all_gather(both_weights, "blk", axis=1, tiled=True)
+    weight_rows_in, weight_rows_out = all_weights[0], all_weights[1]
+    by_feature = to_sources(attended).reshape(exp_count * features, own_rows)
+    attn_out = jnp.einsum(
+        "fr,fd->rd", by_feature, full_output_weight, preferred_element_type=jnp.float32
+    )
     own_nodes = lax.dynamic_slice_in_dim(
         nodes, lax.axis_index("exp") * own_rows, own_rows, 0
     ).astype(jnp.float32)
@@ -125,10 +298,6 @@
         jnp.bfloat16
     )
     outgoing = outgoing.reshape(experts, capacity, width)
-    weight_rows_in, weight_rows_out = (
-        lax.all_gather(expert_in[0], "blk", axis=0, tiled=True),
-        lax.all_gather(expert_out[0], "blk", axis=0, tiled=True),
-    )
     arrived = lax.all_to_all(outgoing, "exp", split_axis=0, concat_axis=0, tiled=True)
     pre_act = jnp.einsum("scd,hd->sch", arrived, weight_rows_in, preferred_element_type=jnp.float32)
     expert_hidden = gelu_tanh(pre_act).astype(jnp.bfloat16)
@@ -149,6 +318,14 @@
     layer_out = normed.astype(jnp.bfloat16)
     grad_two, gain_part = norm_back(cotangent.astype(jnp.float32))
     gate_grads = jnp.sum(expert_rows * grad_two[:, None, :], axis=-1)
+    logit_grad = gate_back(gate_grads)[0]
+    router_part = jnp.dot(
+        logit_grad.T, stream.astype(jnp.float32), precision=lax.Precision.HIGHEST
+    )
+    small_sums = sum_by_halves(
+        jnp.concatenate([router_part, gain_part[None, :]], axis=0) * grad_scale, ("exp", "blk")
+    )
+    router_grad, gain_grad = small_sums[:-1], small_sums[-1]
     assigned_grads = (
         (gates[..., None] * grad_two[:, None, :]).astype(jnp.bfloat16).reshape(2 * own_rows, width)
     )
@@ -162,14 +339,10 @@
         concat_axis=0,
         tiled=True,
     )
-    again_in, again_out = (
-        lax.all_gather(expert_in[0], "blk", axis=0, tiled=True),
-        lax.all_gather(expert_out[0], "blk", axis=0, tiled=True),
-    )
     hidden_full, gelu_back = jax.vjp(gelu_tanh, pre_act)
     hidden = hidden_full.astype(jnp.bfloat16)
     hidden_grad = jnp.einsum(
-        "scd,hd->sch", grad_arrived, again_out, preferred_element_type=jnp.float32
+        "scd,hd->sch", grad_arrived, weight_rows_out, preferred_element_type=jnp.float32
     )
     pre_grad = gelu_back(hidden_grad)[0].astype(jnp.bfloat16)
     term_in = jnp.einsum("sch,scd->hd", pre_grad, received, preferred_element_type=jnp.float32)
@@ -183,7 +356,7 @@
     expert_in_grad = summed_grads[None, :, :width]
     expert_out_grad = summed_grads[None, :, width:]
     rows_back = jnp.einsum(
-        "sch,hd->scd", pre_grad, again_in, preferred_element_type=jnp.float32
+        "sch,hd->scd", pre_grad, weight_rows_in, preferred_element_type=jnp.float32
     ).astype(jnp.bfloat16)
     back_home = to_sources(rows_back)
     back_rows = jnp.einsum(
@@ -193,12 +366,6 @@
         preferred_element_type=jnp.float32,
     )
     back_rows = back_rows.reshape(own_rows, 2, width)
-    logit_grad = gate_back(gate_grads)[0]
-    router_part = (
-        jnp.dot(logit_grad.T, stream.astype(jnp.float32), precision=lax.Precision.HIGHEST)
-        * grad_scale
-    )
-    router_grad, gain_grad = lax.psum((router_part, gain_part * grad_scale), ("blk", "exp"))
     router_term = jnp.dot(
         logit_grad, router_weight.astype(jnp.float32), precision=lax.Precision.HIGHEST
     )

time: 607 us -> 363 us (0.60)
  matrix products: 183 us -> 34.9 us
  Pallas kernels: 0 us -> 116 us
  waiting for transfers between devices: 184 us -> 104 us
  blocking collectives: 87.7 us -> 17.2 us
  local copies, waits for them, and re-layouts: 84.3 us -> 19.3 us
  starting transfers between devices: 14.2 us -> 46.3 us
  other arithmetic: 35.3 us -> 9.68 us
    dot_general x53 -> x5, matrix products: 160 us -> 17.3 us  [the longest x1 7.62 us: local(): jnp.einsum('scd,hd->sch', grad_arrived, weight_rows_out, preferred_elemen...]
    pallas_call x0 -> x4, Pallas kernels: none -> 116 us  [attention_call(): pl.pallas_call(kernel, out_shape=out_shape, in_specs=specs * len(operands...]
    all_gather x3 -> x1, waiting for transfers between devices: 97.4 us -> 0.01 us  [local(): all_weights = lax.all_gather(both_weights, 'blk', axis=1, tiled=True)]
    reduce_scatter x1 -> x0, waiting for transfers between devices: 71.2 us -> none  [local(): lax.psum_scatter(jnp.dot(by_rows, output_weight, preferred_element_type=j...]
    psum x1 -> x0, blocking collectives: 70.5 us -> none  [local(): lax.psum((router_part, gain_part * grad_scale), ('blk', 'exp'))]
    while x72 -> x0, local copies, waits for them, and re-layouts: 62.5 us -> none
    ppermute x0 -> x18, waiting for transfers between devices: none -> 45.8 us  [hop(): lax.ppermute(value, axis, [(i, target(i) % count) for i in range(count)])]
    ppermute x0 -> x18, starting transfers between devices: none -> 31.4 us  [hop(): lax.ppermute(value, axis, [(i, target(i) % count) for i in range(count)])]
  transfers between devices with their start and end apart: 8 -> 24, of which waited for: 5 -> 15; matrix products, arithmetic and copies ran while one was open for 4% -> 6% of each run, Pallas kernels for 0% -> 32%
where the time goes in v1:
time: 363 us; the launch traced here: 362 us
  Pallas kernels  116 us (32%)
  waiting for transfers between devices  104 us (29%)
  starting transfers between devices  46.3 us (13%)
  matrix products  34.9 us (10%)
  local copies, waits for them, and re-layouts  19.3 us (5%)
  blocking collectives  17.2 us (5%)
  between operations  14.6 us (4%)
  other arithmetic  9.68 us (3%)
    pallas_call x4, Pallas kernels, attention_call(): pl.pallas_call(kernel, out_shape=out_shape, in_specs=specs * len(operands...  116 us
    ppermute x18, waiting for transfers between devices, hop(): lax.ppermute(value, axis, [(i, target(i) % count) for i in range(count)])  45.8 us
    ppermute x18, starting transfers between devices, hop(): lax.ppermute(value, axis, [(i, target(i) % count) for i in range(count)])  31.4 us
    unnamed x3, waiting for transfers between devices  25.4 us
    all_to_all x3, waiting for transfers between devices, to_sources(): lax.all_to_all(buffer, 'exp', split_axis=0, concat_axis=0, tiled=True)  20.4 us
    all_to_all x1, blocking collectives, local(): lax.all_to_all(grad_outgoing.reshape(experts, capacity, width), 'exp', sp...  17.2 us
    unnamed x61, local copies, waits for them, and re-layouts  13.5 us
    all_to_all x1, waiting for transfers between devices, local(): lax.all_to_all(outgoing, 'exp', split_axis=0, concat_axis=0, tiled=True)  12.5 us
  transfers between devices with their start and end apart: 24, of which 15 were waited for; matrix products, arithmetic and copies ran while one was open for 6% of the time, Pallas kernels for 32%

profile of v1, /device:TPU:0, one launch (start us, length us, event | category | flops | bytes accessed | tf_op | source)
XLA Modules:
  0.0 361.9 jit_solution(9522217298737395117)
XLA Ops:
  7.2 1.0 slice.49
  8.2 2.0 convolution_convert_fusion.refs_1_.refs_5_
  10.2 4.0 %collective-permute-start.4 = (bf16[64,1536]{1,0:T(8,128)(2,1)S(1)}, bf16[64,1536]{1,0:T(8,128)(2,1)S(1)}, u32[]{:S(2)}, u32[]{:S(2)}) collective-permute-start(bf16[64,1536]{1,0:T(8,128)(2,1)S(1)} %convolution_convert_fusion.refs_1_.refs_5_), channel_id=1, source_target_pairs={{0,64},{8,72},{16,80},{24,88},{32,96},{40,104},{48,112},{56,120},{... | collective-permute-start | bytes 589832 | tf_op jit(solution)/shard_map/ppermute | solution.py:33
  14.3 0.7 collective-permute-start.3
  15.0 1.3 collective-permute-start.2
  16.3 3.7 %collective-permute-done.4.refs_5_.refs_10_ = bf16[64,1536]{1,0:T(8,128)(2,1)S(1)} collective-permute-done((bf16[64,1536]{1,0:T(8,128)(2,1)S(1)}, bf16[64,1536]{1,0:T(8,128)(2,1)S(1)}, u32[]{:S(2)}, u32[]{:S(2)}) %collective-permute-start.4) | collective-permute-done | bytes 196640 | tf_op jit(solution)/shard_map/ppermute | solution.py:33
  20.0 4.2 %collective-permute-done.3.refs_4_.refs_9_ = bf16[64,1536]{1,0:T(8,128)(2,1)S(1)} collective-permute-done((bf16[64,1536]{1,0:T(8,128)(2,1)S(1)}, bf16[64,1536]{1,0:T(8,128)(2,1)S(1)}, u32[]{:S(2)}, u32[]{:S(2)}) %collective-permute-start.3) | collective-permute-done | bytes 196640 | tf_op jit(solution)/shard_map/ppermute | solution.py:33
  24.2 1.7 collective-permute-start.6
  25.9 12.7 %collective-permute-done.6.refs_3_ = bf16[192,1536]{1,0:T(8,128)(2,1)S(1)} collective-permute-done((bf16[192,1536]{1,0:T(8,128)(2,1)S(1)}, bf16[192,1536]{1,0:T(8,128)(2,1)S(1)}, u32[]{:S(2)}, u32[]{:S(2)}) %collective-permute-start.6) | collective-permute-done | bytes 589856 | tf_op jit(solution)/shard_map/ppermute | solution.py:33
  38.5 1.6 collective-permute-start.1
  40.3 1.5 collective-permute-start.8
  41.8 0.8 copy.42
  42.8 1.7 pad_maximum_fusion.2
  44.7 0.9 reduce-window.6
  45.8 2.0 convolution_convert_fusion.1.refs_0_.refs_2_
  47.9 2.8 collective-permute-start.9
  50.7 3.0 collective-permute-done.9
  54.4 2.9 collective-permute-start.10
  57.5 6.8 %shard_map.145 = (bf16[128,1536]{1,0:T(8,128)(2,1)}, f32[48,1536]{1,0:T(8,128)}) custom-call(bf16[32,1536]{1,0:T(8,128)(2,1)} %convolution_convert_fusion.1.refs_0_.refs_2_, bf16[64,1536]{1,0:T(8,128)(2,1)} %copy-done.11, bf16[64,1536]{1,0:T(8,128)(2,1)} %collective-permute-done.refs_2_.refs_6_), custom_call_target="tpu_custom_call" | custom-call | flops 5662310400 | bytes 393216 | tf_op jit(solution)/shard_map/pallas_call | solution.py:150
  64.4 11.9 %shard_map.146.refs_1_ = f32[48,1536]{1,0:T(8,128)} custom-call(bf16[128,1536]{1,0:T(8,128)(2,1)} %get-tuple-element.9.refs_0_, f32[48,1536]{1,0:T(8,128)} %get-tuple-element.10.refs_1_, bf16[64,1536]{1,0:T(8,128)(2,1)} %copy-done.12, bf16[64,1536]{1,0:T(8,128)(2,1)} %copy-done.8, bf16[64,1536]{1,0:T(8,128)(2,1)} %copy-done.7, ...), custom_call_target="tpu_custom_call", output_to_operand_aliasing={{}: (1, {})} | custom-call | flops 11324620800 | bytes 786432 | tf_op jit(solution)/shard_map/pallas_call | solution.py:150
  76.3 11.9 %shard_map.147.refs_1_ = f32[48,1536]{1,0:T(8,128)} custom-call(bf16[128,1536]{1,0:T(8,128)(2,1)} %get-tuple-element.9.refs_0_, f32[48,1536]{1,0:T(8,128)} %shard_map.146.refs_1_, bf16[256,1536]{1,0:T(8,128)(2,1)} %collective-permute-done.5.refs_2_.refs_11_), custom_call_target="tpu_custom_call", output_to_operand_aliasing={{}: (1, {})} | custom-call | flops 11324620800 | bytes 786432 | tf_op jit(solution)/shard_map/pallas_call | solution.py:150
  88.2 85.1 %shard_map.148 = bf16[8,32,192]{2,1,0:T(8,128)(2,1)} custom-call(bf16[128,1536]{1,0:T(8,128)(2,1)} %get-tuple-element.9.refs_0_, f32[48,1536]{1,0:T(8,128)} %shard_map.147.refs_1_, bf16[32,1536]{1,0:T(8,128)(2,1)} %convolution_convert_fusion.1.refs_0_.refs_2_, bf16[192,1536]{1,0:T(8,128)(2,1)} %copy-done.24, ...), custom_call_target="tpu_custom_call" | custom-call | flops 16986931200 | bytes 1179648 | tf_op jit(solution)/shard_map/pallas_call | solution.py:150
  173.3 4.0 %all-to-all-start = ((bf16[8,32,192]{2,1,0:T(8,128)(2,1)}), bf16[8,32,192]{2,1,0:T(8,128)(2,1)S(1)}, u32[]{:S(2)}, u32[]{:S(2)}) async-start(bf16[8,32,192]{2,1,0:T(8,128)(2,1)} %shard_map.148), calls=%async_computation | async-start | bytes 262144 | tf_op jit(solution)/shard_map/all_to_all | solution.py:28
  177.3 1.0 broadcast_select_fusion.1
  178.3 7.1 %all-to-all-done = bf16[8,32,192]{2,1,0:T(8,128)(2,1)S(1)} async-done(((bf16[8,32,192]{2,1,0:T(8,128)(2,1)}), bf16[8,32,192]{2,1,0:T(8,128)(2,1)S(1)}, u32[]{:S(2)}, u32[]{:S(2)}) %all-to-all-start) | async-done | bytes 98336 | tf_op jit(solution)/shard_map/all_to_all | solution.py:28
  186.2 1.5 convolution_convert_fusion.3
  187.7 3.5 all-to-all-start.1
  191.5 1.1 eq.90
  192.6 12.5 %all-to-all-done.1 = bf16[8,96,512]{2,1,0:T(8,128)(2,1)S(1)} async-done(((bf16[8,96,512]{2,1,0:T(8,128)(2,1)}), bf16[8,96,512]{2,1,0:T(8,128)(2,1)S(1)}, u32[]{:S(2)}, u32[]{:S(2)}) %all-to-all-start.1) | async-done | bytes 786464 | tf_op jit(solution)/shard_map/all_to_all | solution.py:301
  205.2 3.6 fusion.9
  208.7 2.7 copy-done.1
  211.4 3.0 fusion.11
  214.4 3.7 %all-to-all-start.2 = ((bf16[8,96,512]{2,1,0:T(8,128)(2,1)}), bf16[8,96,512]{2,1,0:T(8,128)(2,1)S(1)}, u32[]{:S(2)}, u32[]{:S(2)}) async-start(bf16[8,96,512]{2,1,0:T(8,128)(2,1)} %fusion.11), calls=%async_computation.2 | async-start | bytes 1572864 | tf_op jit(solution)/shard_map/all_to_all | solution.py:28
  218.5 0.7 div.76
  219.3 13.3 %all-to-all-done.2 = bf16[8,96,512]{2,1,0:T(8,128)(2,1)S(1)} async-done(((bf16[8,96,512]{2,1,0:T(8,128)(2,1)}), bf16[8,96,512]{2,1,0:T(8,128)(2,1)S(1)}, u32[]{:S(2)}, u32[]{:S(2)}) %all-to-all-start.2) | async-done | bytes 786464 | tf_op jit(solution)/shard_map/all_to_all | solution.py:28
  232.6 1.5 fusion.32
  235.1 0.8 add_add_fusion
  236.8 1.4 convolution_convert_fusion.2
  238.2 17.2 %all_to_all.25 = bf16[8,96,512]{2,1,0:T(8,128)(2,1)S(1)} all-to-all(bf16[8,96,512]{2,1,0:T(8,128)(2,1)S(1)} %bitcast.90), channel_id=1, replica_groups=mesh['blk'=16,'exp'=8] {'exp'}, dimensions={0} | all-to-all | bytes 1572864 | tf_op jit(solution)/shard_map/all_to_all | solution.py:335
  255.4 7.6 %fusion.7 = bf16[8,96,2048]{2,1,0:T(8,128)(2,1)S(1)} fusion(f32[8,96,2048]{2,1,0:T(8,128)} %copy-done.1, bf16[8,96,512]{2,1,0:T(8,128)(2,1)S(1)} %all_to_all.25, bf16[2,2048,512]{2,1,0:T(8,128)(2,1)} %all-gather.2.cloned.1.call-done), kind=kOutput, calls=%fused_computation.10 | convolution fusion | flops 1642070016 | bytes 12320768 | tf_op jit(solution)/shard_map/scd,hd->sch/dot_general | solution.py:344
  263.0 2.9 convolution_bitcast_fusion
  266.0 1.9 convolution_bitcast_fusion.1
  267.9 2.7 fusion
  270.6 6.5 %copy.50 = bf16[2048,1024]{1,0:T(8,128)(2,1)} copy(bf16[2048,1024]{0,1:T(8,128)(2,1)} %fusion) | data formatting | bytes 8388608
  278.0 5.3 %fusion.12 = bf16[8,96,512]{2,1,0:T(8,128)(2,1)} fusion(bf16[8,96,2048]{2,1,0:T(8,128)(2,1)} %copy-done.25, bf16[2,2048,512]{2,1,0:T(8,128)(2,1)} %all-gather.2.cloned.1.call-done), kind=kOutput, calls=%fused_computation.22 | convolution fusion | flops 1611005952 | bytes 6029312 | tf_op jit(solution)/shard_map/sch,hd->scd/dot_general | solution.py:358
  283.3 3.5 all-to-all-start.4
  287.1 2.0 collective-permute-start.11
  289.1 8.3 %collective-permute-done.11 = f32[9,512]{1,0:T(8,128)S(1)} collective-permute-done((f32[9,512]{1,0:T(8,128)S(1)}, f32[9,512]{1,0:T(8,128)S(1)}, u32[]{:S(2)}, u32[]{:S(2)}) %collective-permute-start.11) | collective-permute-done | bytes 18464 | tf_op jit(solution)/shard_map/ppermute | solution.py:33
  297.5 2.8 collective-permute-start.12
  300.2 2.7 collective-permute-done.12
  303.0 3.0 collective-permute-start.13
  306.0 2.5 collective-permute-done.13
  308.4 1.2 collective-permute-done.14
  309.6 0.9 collective-permute-start.15
  310.5 3.7 %collective-permute-done.15 = f32[9,512]{1,0:T(8,128)S(1)} collective-permute-done((f32[9,512]{1,0:T(8,128)S(1)}, f32[9,512]{1,0:T(8,128)S(1)}, u32[]{:S(2)}, u32[]{:S(2)}) %collective-permute-start.15) | collective-permute-done | bytes 18464 | tf_op jit(solution)/shard_map/ppermute | solution.py:33
  314.2 2.1 collective-permute-start.16
  316.3 1.9 collective-permute-done.16
  318.2 3.9 %collective-permute-start.17 = (f32[9,512]{1,0:T(8,128)S(1)}, f32[9,512]{1,0:T(8,128)S(1)}, u32[]{:S(2)}, u32[]{:S(2)}) collective-permute-start(f32[9,512]{1,0:T(8,128)S(1)} %add.119), channel_id=1, source_target_pairs={{0,64},{8,72},{16,80},{24,88},{32,96},{40,104},{48,112},{56,120},{... | collective-permute-start | bytes 55304 | tf_op jit(solution)/shard_map/ppermute | solution.py:33
  322.1 1.9 collective-permute-done.17
  325.7 1.1 fusion.13
  326.7 25.4 %reduce-scatter.4.cloned.1.call-done = bf16[128,1024]{1,0:T(8,128)(2,1)} async-done(((bf16[2048,1024]{1,0:T(8,128)(2,1)}), bf16[128,1024]{1,0:T(8,128)(2,1)}) %reduce-scatter.4.cloned.1.call-update) | async-done | bytes 262160
  352.2 1.1 copy.51
  353.4 0.8 copy.49
  354.2 0.8 copy.48
  (123 shorter events, 8.0 us)
Async XLA Ops:
  7.2 211.0 %copy-start = (bf16[8,512]{1,0:T(8,128)(2,1)S(1)}, bf16[8,512]{1,0:T(8,128)(2,1)}, u32[]{:S(2)}) copy-start(bf16[8,512]{1,0:T(8,128)(2,1)} %param.13) | copy-start | bytes 24580
  7.2 38.6 %copy-start.2 = (bf16[1536,512]{1,0:T(8,128)(2,1)S(1)}, bf16[1536,512]{1,0:T(8,128)(2,1)}, u32[]{:S(2)}) copy-start(bf16[1536,512]{1,0:T(8,128)(2,1)} %param.10) | copy-start | bytes 4718596
  7.2 40.7 %copy-start.13 = (bf16[32,512]{1,0:T(8,128)(2,1)S(1)}, bf16[32,512]{1,0:T(8,128)(2,1)}, u32[]{:S(2)}) copy-start(bf16[32,512]{1,0:T(8,128)(2,1)} %param.12) | copy-start | bytes 98308
  7.2 197.9 %all-gather.2.cloned.1.call-start = ((), (), s32[]{:S(2)}) async-start(), calls=%async_computation.6 | async-start | bytes 4456448 | tf_op jit(solution)/shard_map/all_gather | solution.py:268
  10.2 47.3 %copy-start.11 = (bf16[64,1536]{1,0:T(8,128)(2,1)}, bf16[64,1536]{1,0:T(8,128)(2,1)S(1)}, u32[]{:S(2)}) copy-start(bf16[64,1536]{1,0:T(8,128)(2,1)S(1)} %convolution_convert_fusion.refs_1_.refs_5_) | copy-start | bytes 589828
  10.2 9.8 %collective-permute-start.4 = (bf16[64,1536]{1,0:T(8,128)(2,1)S(1)}, bf16[64,1536]{1,0:T(8,128)(2,1)S(1)}, u32[]{:S(2)}, u32[]{:S(2)}) collective-permute-start(bf16[64,1536]{1,0:T(8,128)(2,1)S(1)} %convolution_convert_fusion.refs_1_.refs_5_), channel_id=1, source_target_pairs={{0,64},{8,72},{16,80},{24,88},{32,96},{40,104},{48,112},{56,120},{... | collective-permute-start | bytes 589832 | tf_op jit(solution)/shard_map/ppermute | solution.py:33
  14.3 9.9 %collective-permute-start.3 = (bf16[64,1536]{1,0:T(8,128)(2,1)S(1)}, bf16[64,1536]{1,0:T(8,128)(2,1)S(1)}, u32[]{:S(2)}, u32[]{:S(2)}) collective-permute-start(bf16[64,1536]{1,0:T(8,128)(2,1)S(1)} %convolution_convert_fusion.refs_1_.refs_5_), channel_id=1, source_target_pairs={{0,96},{8,104},{16,112},{24,120},{32,0},{40,8},{48,16},{56,24},{64... | collective-permute-start | bytes 589832 | tf_op jit(solution)/shard_map/ppermute | solution.py:33
  15.0 9.2 %collective-permute-start.2 = (bf16[64,1536]{1,0:T(8,128)(2,1)S(1)}, bf16[64,1536]{1,0:T(8,128)(2,1)S(1)}, u32[]{:S(2)}, u32[]{:S(2)}) collective-permute-start(bf16[64,1536]{1,0:T(8,128)(2,1)S(1)} %convolution_convert_fusion.refs_1_.refs_5_), channel_id=1, source_target_pairs={{0,32},{8,40},{16,48},{24,56},{32,64},{40,72},{48,80},{56,88},{64,... | collective-permute-start | bytes 589832 | tf_op jit(solution)/shard_map/ppermute | solution.py:33
  20.0 44.4 %copy-start.6 = (bf16[64,1536]{1,0:T(8,128)(2,1)}, bf16[64,1536]{1,0:T(8,128)(2,1)S(1)}, u32[]{:S(2)}) copy-start(bf16[64,1536]{1,0:T(8,128)(2,1)S(1)} %collective-permute-done.4.refs_5_.refs_10_) | copy-start | bytes 589828
  24.1 40.2 %copy-start.7 = (bf16[64,1536]{1,0:T(8,128)(2,1)}, bf16[64,1536]{1,0:T(8,128)(2,1)S(1)}, u32[]{:S(2)}) copy-start(bf16[64,1536]{1,0:T(8,128)(2,1)S(1)} %collective-permute-done.3.refs_4_.refs_9_) | copy-start | bytes 589828
  24.2 40.2 %copy-start.8 = (bf16[64,1536]{1,0:T(8,128)(2,1)}, bf16[64,1536]{1,0:T(8,128)(2,1)S(1)}, u32[]{:S(2)}) copy-start(bf16[64,1536]{1,0:T(8,128)(2,1)S(1)} %collective-permute-done.2.refs_3_.refs_8_) | copy-start | bytes 589828
  24.2 14.3 %collective-permute-start.6 = (bf16[192,1536]{1,0:T(8,128)(2,1)S(1)}, bf16[192,1536]{1,0:T(8,128)(2,1)S(1)}, u32[]{:S(2)}, u32[]{:S(2)}) collective-permute-start(bf16[192,1536]{1,0:T(8,128)(2,1)S(1)} %pad_maximum_fusion.1), channel_id=1, source_target_pairs={{0,16},{8,24},{16,0},{24,8},{32,48},{40,56},{48,32},{56,40},{64,80... | collective-permute-start | bytes 1769480 | tf_op jit(solution)/shard_map/ppermute | solution.py:33
  38.5 6.0 %copy-start.24 = (bf16[192,1536]{1,0:T(8,128)(2,1)}, bf16[192,1536]{1,0:T(8,128)(2,1)S(1)}, u32[]{:S(2)}) copy-start(bf16[192,1536]{1,0:T(8,128)(2,1)S(1)} %collective-permute-done.6.refs_3_) | copy-start | bytes 1769476
  38.5 5.9 %collective-permute-start.7 = (bf16[192,1536]{1,0:T(8,128)(2,1)S(1)}, bf16[192,1536]{1,0:T(8,128)(2,1)}, u32[]{:S(2)}, u32[]{:S(2)}) collective-permute-start(bf16[192,1536]{1,0:T(8,128)(2,1)S(1)} %collective-permute-done.6.refs_3_), channel_id=1, source_target_pairs={{0,8},{8,0},{16,24},{24,16},{32,40},{40,32},{48,56},{56,48},{64,72... | collective-permute-start | bytes 1769480 | tf_op jit(solution)/shard_map/ppermute | solution.py:33
  38.5 18.8 %collective-permute-start.1 = (bf16[64,1536]{1,0:T(8,128)(2,1)S(1)}, bf16[64,1536]{1,0:T(8,128)(2,1)S(1)}, u32[]{:S(2)}, u32[]{:S(2)}) collective-permute-start(bf16[64,1536]{1,0:T(8,128)(2,1)S(1)} %convolution_convert_fusion.refs_1_.refs_5_), channel_id=1, source_target_pairs={{0,16},{8,24},{16,0},{24,8},{32,48},{40,56},{48,32},{56,40},{64,80... | collective-permute-start | bytes 589832 | tf_op jit(solution)/shard_map/ppermute | solution.py:33
  40.1 17.4 %collective-permute-start = (bf16[64,1536]{1,0:T(8,128)(2,1)S(1)}, bf16[64,1536]{1,0:T(8,128)(2,1)}, u32[]{:S(2)}, u32[]{:S(2)}) collective-permute-start(bf16[64,1536]{1,0:T(8,128)(2,1)S(1)} %convolution_convert_fusion.refs_1_.refs_5_), channel_id=1, source_target_pairs={{0,8},{8,0},{16,24},{24,16},{32,40},{40,32},{48,56},{56,48},{64,72... | collective-permute-start | bytes 589832 | tf_op jit(solution)/shard_map/ppermute | solution.py:33
  40.3 7.5 %collective-permute-start.8 = (bf16[32,512]{1,0:T(8,128)(2,1)}, bf16[32,512]{1,0:T(8,128)(2,1)S(1)}, u32[]{:S(2)}, u32[]{:S(2)}) collective-permute-start(bf16[32,512]{1,0:T(8,128)(2,1)} %param.12), channel_id=1, source_target_pairs={{0,1},{1,0},{2,3},{3,2},{4,5},{5,4},{6,7},{7,6},{8,9},{9,8},{10,11... | collective-permute-start | bytes 98312 | tf_op jit(solution)/shard_map/ppermute | solution.py:33
  47.9 5.8 %collective-permute-start.9 = (bf16[64,512]{1,0:T(8,128)(2,1)S(1)}, bf16[64,512]{1,0:T(8,128)(2,1)S(1)}, u32[]{:S(2)}, u32[]{:S(2)}) collective-permute-start(bf16[64,512]{1,0:T(8,128)(2,1)S(1)} %pad_maximum_fusion.4), channel_id=1, source_target_pairs={{0,2},{1,3},{2,0},{3,1},{4,6},{5,7},{6,4},{7,5},{8,10},{9,11},{10,... | collective-permute-start | bytes 196616 | tf_op jit(solution)/shard_map/ppermute | solution.py:33
  50.7 140.6 %copy-start.14 = (s32[384]{0:T(512)}, s32[384]{0:T(512)S(1)}, u32[]{:S(2)}) copy-start(s32[384]{0:T(512)S(1)} %multiply_add_fusion) | copy-start | bytes 4612
  54.4 122.9 %collective-permute-start.10 = (bf16[128,512]{1,0:T(8,128)(2,1)}, bf16[128,512]{1,0:T(8,128)(2,1)}, u32[]{:S(2)}, u32[]{:S(2)}) collective-permute-start(bf16[128,512]{1,0:T(8,128)(2,1)} %pad_maximum_fusion.3), channel_id=1, source_target_pairs={{0,4},{1,5},{2,6},{3,7},{4,0},{5,1},{6,2},{7,3},{8,12},{9,13},{10,... | collective-permute-start | bytes 393224 | tf_op jit(solution)/shard_map/ppermute | solution.py:33
  57.3 7.0 %copy-start.12 = (bf16[64,1536]{1,0:T(8,128)(2,1)}, bf16[64,1536]{1,0:T(8,128)(2,1)S(1)}, u32[]{:S(2)}) copy-start(bf16[64,1536]{1,0:T(8,128)(2,1)S(1)} %collective-permute-done.1.refs_2_.refs_7_) | copy-start | bytes 589828
  57.4 18.9 %collective-permute-start.5 = (bf16[256,1536]{1,0:T(8,128)(2,1)S(1)}, bf16[256,1536]{1,0:T(8,128)(2,1)}, u32[]{:S(2)}, u32[]{:S(2)}) collective-permute-start(bf16[256,1536]{1,0:T(8,128)(2,1)S(1)} %pad_maximum_fusion), channel_id=1, source_target_pairs={{0,8},{8,0},{16,24},{24,16},{32,40},{40,32},{48,56},{56,48},{64,72... | collective-permute-start | bytes 2359304 | tf_op jit(solution)/shard_map/ppermute | solution.py:33
  88.2 97.5 %copy-start.22 = (f32[512]{0:T(512)S(1)}, f32[512]{0:T(512)}, u32[]{:S(2)}) copy-start(f32[512]{0:T(512)} %param.14) | copy-start | bytes 6148
  173.3 12.1 %all-to-all-start = ((bf16[8,32,192]{2,1,0:T(8,128)(2,1)}), bf16[8,32,192]{2,1,0:T(8,128)(2,1)S(1)}, u32[]{:S(2)}, u32[]{:S(2)}) async-start(bf16[8,32,192]{2,1,0:T(8,128)(2,1)} %shard_map.148), calls=%async_computation | async-start | bytes 262144 | tf_op jit(solution)/shard_map/all_to_all | solution.py:28
  185.8 32.3 %copy-start.3 = (bf16[192,512]{1,0:T(8,128)(2,1)}, bf16[192,512]{1,0:T(8,128)(2,1)S(1)}, u32[]{:S(2)}) copy-start(bf16[192,512]{1,0:T(8,128)(2,1)S(1)} %multiply_convert_fusion.4) | copy-start | bytes 589828
  187.7 17.4 %all-to-all-start.1 = ((bf16[8,96,512]{2,1,0:T(8,128)(2,1)}), bf16[8,96,512]{2,1,0:T(8,128)(2,1)S(1)}, u32[]{:S(2)}, u32[]{:S(2)}) async-start(bf16[8,96,512]{2,1,0:T(8,128)(2,1)} %bitcast.6), calls=%async_computation.1 | async-start | bytes 1572864 | tf_op jit(solution)/shard_map/all_to_all | solution.py:301
  205.1 6.3 %copy-start.5 = (bf16[2,2048,512]{2,1,0:T(8,128)(2,1)S(1)}, bf16[2,2048,512]{2,1,0:T(8,128)(2,1)}, u32[]{:S(2)}) copy-start(bf16[2,2048,512]{2,1,0:T(8,128)(2,1)} %all-gather.2.cloned.1.call-done) | copy-start | bytes 12582916
  208.7 2.7 copy-start.1
  211.4 6.9 %copy-start.18 = (s32[192,2]{0,1:T(2,128)S(1)}, s32[192,2]{0,1:T(2,128)}, u32[]{:S(2)}) copy-start(s32[192,2]{0,1:T(2,128)} %param.18) | copy-start | bytes 4612
  214.4 20.0 %copy-start.9 = (bf16[192,512]{1,0:T(8,128)(2,1)S(1)}, bf16[192,512]{1,0:T(8,128)(2,1)}, u32[]{:S(2)}) copy-start(bf16[192,512]{1,0:T(8,128)(2,1)} %param.19) | copy-start | bytes 589828
  214.4 20.0 %copy-start.23 = (f32[512]{0:T(512)S(1)}, f32[512]{0:T(512)}, u32[]{:S(2)}) copy-start(f32[512]{0:T(512)} %param.15) | copy-start | bytes 6148
  214.4 18.1 %all-to-all-start.2 = ((bf16[8,96,512]{2,1,0:T(8,128)(2,1)}), bf16[8,96,512]{2,1,0:T(8,128)(2,1)S(1)}, u32[]{:S(2)}, u32[]{:S(2)}) async-start(bf16[8,96,512]{2,1,0:T(8,128)(2,1)} %fusion.11), calls=%async_computation.2 | async-start | bytes 1572864 | tf_op jit(solution)/shard_map/all_to_all | solution.py:28
  218.1 134.0 %reduce-scatter.4.cloned.1.call-start = ((), (), s32[]{:S(2)}) async-start(), calls=%async_computation.7 | async-start | bytes 4456448
  218.4 17.6 %copy-start.16 = (f32[192,2]{0,1:T(2,128)}, f32[192,2]{0,1:T(2,128)S(1)}, u32[]{:S(2)}) copy-start(f32[192,2]{0,1:T(2,128)S(1)} %get-tuple-element.39) | copy-start | bytes 4612
  218.4 17.6 %copy-start.20 = (f32[192]{0:T(256)}, f32[192]{0:T(256)S(1)}, u32[]{:S(2)}) copy-start(f32[192]{0:T(256)S(1)} %get-tuple-element.38) | copy-start | bytes 2308
  238.2 24.9 %slice-start = ((s8[6291456]{0:T(1024)(128)(4,1)}), s8[4194304]{0:T(1024)(128)(4,1)S(1)}, s32[]{:S(2)}) async-start(s8[6291456]{0:T(1024)(128)(4,1)} %bitcast.88), calls=%async_computation.8 | async-start | bytes 8388608
  255.4 7.6 %slice-start.1 = ((s8[6291456]{0:T(1024)(128)(4,1)}), s8[2097152]{0:T(1024)(128)(4,1)S(1)}, s32[]{:S(2)}) async-start(s8[6291456]{0:T(1024)(128)(4,1)} %bitcast.88), calls=%async_computation.9 | async-start | bytes 4194304
  263.0 2.9 copy-start.25
  277.0 0.7 copy-start.21
  277.0 0.9 copy-start.17
  277.0 0.9 copy-start.19
  278.0 8.9 %copy-start.4 = (bf16[192,512]{1,0:T(8,128)(2,1)S(1)}, bf16[192,512]{1,0:T(8,128)(2,1)}, u32[]{:S(2)}) copy-start(bf16[192,512]{1,0:T(8,128)(2,1)} %copy-done.3) | copy-start | bytes 589828
  278.0 9.1 %copy-start.15 = (f32[512]{0:T(512)S(1)}, f32[512]{0:T(512)}, u32[]{:S(2)}) copy-start(f32[512]{0:T(512)} %get-tuple-element.36) | copy-start | bytes 6148
  278.0 47.2 %copy-start.10 = (pred[192,2,768]{2,1,0:T(4,128)(4,1)S(1)}, pred[192,2,768]{2,1,0:T(4,128)(4,1)}, u32[]{:S(2)}) copy-start(pred[192,2,768]{2,1,0:T(4,128)(4,1)} %eq.90) | copy-start | bytes 884740
  283.3 41.8 %all-to-all-start.4 = ((bf16[8,96,512]{2,1,0:T(8,128)(2,1)}), bf16[8,96,512]{2,1,0:T(8,128)(2,1)S(1)}, u32[]{:S(2)}, u32[]{:S(2)}) async-start(bf16[8,96,512]{2,1,0:T(8,128)(2,1)} %fusion.12), calls=%async_computation.4 | async-start | bytes 1572864 | tf_op jit(solution)/shard_map/all_to_all | solution.py:28
  287.1 10.3 %collective-permute-start.11 = (f32[9,512]{1,0:T(8,128)S(1)}, f32[9,512]{1,0:T(8,128)S(1)}, u32[]{:S(2)}, u32[]{:S(2)}) collective-permute-start(f32[9,512]{1,0:T(8,128)S(1)} %maximum_multiply_fusion.1), channel_id=1, source_target_pairs={{0,1},{1,0},{2,3},{3,2},{4,5},{5,4},{6,7},{7,6},{8,9},{9,8},{10,11... | collective-permute-start | bytes 55304 | tf_op jit(solution)/shard_map/ppermute | solution.py:33
  297.5 5.5 %collective-permute-start.12 = (f32[9,512]{1,0:T(8,128)S(1)}, f32[9,512]{1,0:T(8,128)S(1)}, u32[]{:S(2)}, u32[]{:S(2)}) collective-permute-start(f32[9,512]{1,0:T(8,128)S(1)} %fusion.52), channel_id=1, source_target_pairs={{0,2},{1,3},{2,0},{3,1},{4,6},{5,7},{6,4},{7,5},{8,10},{9,11},{10,... | collective-permute-start | bytes 55304 | tf_op jit(solution)/shard_map/ppermute | solution.py:33
  303.0 5.5 %collective-permute-start.13 = (f32[9,512]{1,0:T(8,128)S(1)}, f32[9,512]{1,0:T(8,128)S(1)}, u32[]{:S(2)}, u32[]{:S(2)}) collective-permute-start(f32[9,512]{1,0:T(8,128)S(1)} %add.115), channel_id=1, source_target_pairs={{0,4},{1,5},{2,6},{3,7},{4,0},{5,1},{6,2},{7,3},{8,12},{9,13},{10,... | collective-permute-start | bytes 55304 | tf_op jit(solution)/shard_map/ppermute | solution.py:33
  308.4 1.2 collective-permute-start.14
  309.6 4.5 %collective-permute-start.15 = (f32[9,512]{1,0:T(8,128)S(1)}, f32[9,512]{1,0:T(8,128)S(1)}, u32[]{:S(2)}, u32[]{:S(2)}) collective-permute-start(f32[9,512]{1,0:T(8,128)S(1)} %add.117), channel_id=1, source_target_pairs={{0,16},{8,24},{16,0},{24,8},{32,48},{40,56},{48,32},{56,40},{64,80... | collective-permute-start | bytes 55304 | tf_op jit(solution)/shard_map/ppermute | solution.py:33
  314.2 4.0 %collective-permute-start.16 = (f32[9,512]{1,0:T(8,128)S(1)}, f32[9,512]{1,0:T(8,128)S(1)}, u32[]{:S(2)}, u32[]{:S(2)}) collective-permute-start(f32[9,512]{1,0:T(8,128)S(1)} %add.118), channel_id=1, source_target_pairs={{0,32},{8,40},{16,48},{24,56},{32,0},{40,8},{48,16},{56,24},{64,96... | collective-permute-start | bytes 55304 | tf_op jit(solution)/shard_map/ppermute | solution.py:33
  318.2 5.8 %collective-permute-start.17 = (f32[9,512]{1,0:T(8,128)S(1)}, f32[9,512]{1,0:T(8,128)S(1)}, u32[]{:S(2)}, u32[]{:S(2)}) collective-permute-start(f32[9,512]{1,0:T(8,128)S(1)} %add.119), channel_id=1, source_target_pairs={{0,64},{8,72},{16,80},{24,88},{32,96},{40,104},{48,112},{56,120},{... | collective-permute-start | bytes 55304 | tf_op jit(solution)/shard_map/ppermute | solution.py:33
Sparse Core Ops, SparseCore 0:
  44.6 41.3 all-gather.1
  277.2 74.9 reduce-scatter.3

commit v2 on v1

--- a/solution.py
+++ b/solution.py
@@ -14,17 +14,15 @@
 SHIFT_KEYS = 256
 SUM_LIMIT = 2.0**100
 VMEM_LIMIT = 60 * 2**20
+TANH_SCALE = math.sqrt(2.0 / math.pi)
+CUBE = 0.044715
 
 
 def rms_gain(stream, gain):
     return stream * lax.rsqrt(jnp.mean(stream * stream, axis=-1, keepdims=True) + EPSILON) * gain
 
 
-def gelu_tanh(values):
-    return jax.nn.gelu(values, approximate=True)
-
-
-def to_sources(buffer):
+def exchange(buffer):
     return lax.all_to_all(buffer, "exp", split_axis=0, concat_axis=0, tiled=True)
 
 
@@ -167,7 +165,15 @@
     )(*operands)
 
 
-def attention(query, keys_values, owners):
+def double_by_exchange(rows, axis, distance):
+    other = hop(rows, axis, lambda i: i ^ distance)
+    upper = (lax.axis_index(axis) // distance) % 2 == 1
+    return jnp.concatenate(
+        [jnp.where(upper, other, rows), jnp.where(upper, rows, other)], axis=0
+    )
+
+
+def attention(query, keys_values, output_weight, expert_weights, owners):
     width = query.shape[1]
     partner = hop(keys_values, "blk", lambda i: i ^ 1)
     near = [
@@ -176,25 +182,42 @@
         hop(keys_values, "blk", lambda i: i + 12),
         hop(keys_values, "blk", lambda i: i + 8),
     ]
-    beyond = hop(jnp.concatenate(near[1:], axis=0), "blk", lambda i: i ^ 2)
-    near_partner = hop(jnp.concatenate(near, axis=0), "blk", lambda i: i ^ 1)
-    beyond_partner = hop(beyond, "blk", lambda i: i ^ 1)
     total_shape = jax.ShapeDtypeStruct((HD + HD // 2, width), jnp.float32)
     wide_shape = jax.ShapeDtypeStruct((4 * HD, width), jnp.bfloat16)
     first = [keys_values, partner]
     wide, total = attention_call(
-        lambda *refs: first_keys_kernel(2, *refs), (wide_shape, total_shape), [query, *first], 2, width
-    )
-    for group in (near, [near_partner]):
+        lambda *refs: first_keys_kernel(2, *refs),
+        (wide_shape, total_shape),
+        [query, *first],
+        2,
+        width,
+    )
+
+    def more(total, group):
         count = block_count(group)
-        total = attention_call(
-            lambda *refs, count=count: more_keys_kernel(count, *refs),
+        return attention_call(
+            lambda *refs: more_keys_kernel(count, *refs),
             total_shape,
             [wide, total, *group],
             count,
             width,
             aliases={1: 0},
         )
+
+    near, output_weight, total = lax.optimization_barrier((near, output_weight, total))
+    beyond = hop(jnp.concatenate(near[1:], axis=0), "blk", lambda i: i ^ 2)
+    near_partner = hop(jnp.concatenate(near, axis=0), "blk", lambda i: i ^ 1)
+    output_weight = double_by_exchange(output_weight, "exp", 1)
+    total = more(total, near)
+    beyond, output_weight, expert_weights, total = lax.optimization_barrier(
+        (beyond, output_weight, expert_weights, total)
+    )
+    beyond_partner = hop(beyond, "blk", lambda i: i ^ 1)
+    output_weight = double_by_exchange(output_weight, "exp", 2)
+    expert_weights = lax.all_gather(expert_weights, "blk", axis=1, tiled=True)
+    total = more(total, [near_partner])
+    output_weight, total = lax.optimization_barrier((output_weight, total))
+    output_weight = double_by_exchange(output_weight, "exp", 4)
     last = [beyond, beyond_partner]
     count = block_count(last)
     attended = attention_call(
@@ -205,29 +228,239 @@
         width,
         extra=[pltpu.VMEM(total_shape.shape, jnp.float32)],
     )
-    return attended, beyond_partner
-
-
-def gather_by_halves(rows, axis):
-    index = lax.axis_index(axis)
-    distance = 1
-    while distance < lax.axis_size(axis):
-        other = hop(rows, axis, lambda i, distance=distance: i ^ distance)
-        upper = (index // distance) % 2 == 1
-        rows = jnp.concatenate(
-            [jnp.where(upper, other, rows), jnp.where(upper, rows, other)], axis=0
-        )
-        distance *= 2
-    return rows
-
-
-def sum_by_halves(value, axes):
-    for axis in axes:
-        distance = 1
-        while distance < lax.axis_size(axis):
-            value = value + hop(value, axis, lambda i, distance=distance: i ^ distance)
-            distance *= 2
-    return value
+    return attended, output_weight, expert_weights
+
+
+def sum_near(value, axis, distance):
+    first, second, both = [
+        hop(value, axis, lambda i, step=step: i ^ step)
+        for step in (distance, 2 * distance, 3 * distance)
+    ]
+    return (value + first) + (second + both)
+
+
+def sum_pair(value, axis, distance):
+    return value + hop(value, axis, lambda i: i ^ distance)
+
+
+def dot_rows(first, second):
+    return lax.dot_general(
+        first, second, (((1,), (1,)), ((), ())), preferred_element_type=jnp.float32
+    )
+
+
+def tanh_part(values):
+    return jnp.tanh(TANH_SCALE * (values + CUBE * (values * values * values)))
+
+
+def expert_forward_kernel(rows_ref, in_ref, out_ref, result_ref, total):
+    step = pl.program_id(0)
+    pre_act = dot_rows(rows_ref[...], in_ref[...])
+    hidden = (pre_act * (0.5 * (1.0 + tanh_part(pre_act)))).astype(jnp.bfloat16)
+    part = jnp.dot(hidden, out_ref[...], preferred_element_type=jnp.float32)
+
+    @pl.when(step == 0)
+    def _():
+        total[...] = part
+
+    @pl.when(step > 0)
+    def _():
+        total[...] += part
+
+    @pl.when(step == pl.num_programs(0) - 1)
+    def _():
+        result_ref[...] = total[...].astype(result_ref.dtype)
+
+
+def expert_forward(rows, weights):
+    count, width = rows.shape
+    hidden = weights.shape[1]
+    tile = 512
+    return pl.pallas_call(
+        expert_forward_kernel,
+        grid=(hidden // tile,),
+        out_shape=jax.ShapeDtypeStruct((count, width), jnp.bfloat16),
+        in_specs=[
+            pl.BlockSpec((count, width), lambda i: (0, 0)),
+            pl.BlockSpec((None, tile, width), lambda i: (0, i, 0)),
+            pl.BlockSpec((None, tile, width), lambda i: (1, i, 0)),
+        ],
+        out_specs=pl.BlockSpec((count, width), lambda i: (0, 0)),
+        scratch_shapes=[pltpu.VMEM((count, width), jnp.float32)],
+        compiler_params=pltpu.CompilerParams(vmem_limit_bytes=VMEM_LIMIT),
+        cost_estimate=pl.CostEstimate(
+            flops=4 * count * width * hidden,
+            transcendentals=count * hidden,
+            bytes_accessed=4 * hidden * width,
+        ),
+    )(rows, weights, weights)
+
+
+def expert_slopes_kernel(place_ref, rows_ref, *refs):
+    ins, outs = refs[:4], refs[4:8]
+    hidden_ref, slope_ref, out_weight_ref, in_weight_ref = refs[8:]
+    weight_in = jnp.concatenate([ref[...] for ref in ins], axis=0)
+    out_weight_ref[...] = jnp.concatenate([ref[...] for ref in outs], axis=0)
+    in_weight_ref[...] = weight_in.T
+    pre_act = dot_rows(weight_in, rows_ref[...])
+    tanh = tanh_part(pre_act)
+    half = 0.5 * (1.0 + tanh)
+    hidden_ref[...] = (pre_act * half).astype(hidden_ref.dtype)
+    slope_ref[...] = half + pre_act * (0.5 * (1.0 - tanh * tanh)) * (
+        TANH_SCALE * (1.0 + 3.0 * CUBE * (pre_act * pre_act))
+    )
+
+
+def expert_slopes(place, rows, weights):
+    count, width = rows.shape
+    hidden = weights.shape[1]
+    share = hidden // 16
+    tile = 4 * share
+
+    def weight_spec(which, quarter):
+        def index(step, place):
+            z = jnp.bitwise_xor(step, place[0])
+            y = jnp.bitwise_xor(quarter // 2, place[1])
+            core = jnp.bitwise_xor(quarter % 2, place[2])
+            return (which, z * 4 + y * 2 + core, 0)
+
+        return pl.BlockSpec((None, share, width), index)
+
+    specs = [weight_spec(which, quarter) for which in range(2) for quarter in range(4)]
+    return pl.pallas_call(
+        expert_slopes_kernel,
+        out_shape=(
+            jax.ShapeDtypeStruct((hidden, count), jnp.bfloat16),
+            jax.ShapeDtypeStruct((hidden, count), jnp.float32),
+            jax.ShapeDtypeStruct((hidden, width), jnp.bfloat16),
+            jax.ShapeDtypeStruct((width, hidden), jnp.bfloat16),
+        ),
+        grid_spec=pltpu.PrefetchScalarGridSpec(
+            num_scalar_prefetch=1,
+            grid=(hidden // tile,),
+            in_specs=[pl.BlockSpec((count, width), lambda i, place: (0, 0)), *specs],
+            out_specs=(
+                pl.BlockSpec((tile, count), lambda i, place: (i, 0)),
+                pl.BlockSpec((tile, count), lambda i, place: (i, 0)),
+                pl.BlockSpec((tile, width), lambda i, place: (i, 0)),
+                pl.BlockSpec((width, tile), lambda i, place: (0, i)),
+            ),
+        ),
+        compiler_params=pltpu.CompilerParams(vmem_limit_bytes=VMEM_LIMIT),
+        cost_estimate=pl.CostEstimate(
+            flops=2 * count * width * hidden,
+            transcendentals=count * hidden,
+            bytes_accessed=6 * count * hidden + 8 * hidden * width,
+        ),
+    )(place, rows, *([weights] * 8))
+
+
+def store_shares(term, mine_ref, theirs_ref):
+    share = mine_ref.shape[2]
+    for y in range(2):
+        start = 2 * y * share
+        mine_ref[0, y] = term[start : start + share]
+        theirs_ref[0, y] = term[start + share : start + 2 * share].astype(theirs_ref.dtype)
+
+
+def expert_out_grad_kernel(scale, hidden_ref, grads_ref, mine_ref, theirs_ref):
+    term = jnp.dot(hidden_ref[...], grads_ref[...], preferred_element_type=jnp.float32)
+    store_shares(term * scale, mine_ref, theirs_ref)
+
+
+def expert_in_grad_kernel(
+    scale,
+    slope_ref,
+    out_weight_ref,
+    in_weight_ref,
+    rows_ref,
+    grads_ref,
+    mine_ref,
+    theirs_ref,
+    back_ref,
+    total,
+):
+    step = pl.program_id(0)
+    hidden_grad = dot_rows(out_weight_ref[...], grads_ref[...])
+    pre_grad = (hidden_grad * slope_ref[...]).astype(jnp.bfloat16)
+    part = jnp.dot(in_weight_ref[...], pre_grad, preferred_element_type=jnp.float32)
+
+    @pl.when(step == 0)
+    def _():
+        total[...] = part
+
+    @pl.when(step > 0)
+    def _():
+        total[...] += part
+
+    term = jnp.dot(pre_grad, rows_ref[...], preferred_element_type=jnp.float32)
+    store_shares(term * scale, mine_ref, theirs_ref)
+
+    @pl.when(step == pl.num_programs(0) - 1)
+    def _():
+        back_ref[...] = total[...].T.astype(back_ref.dtype)
+
+
+def share_shapes(hidden, width):
+    shape = (4, 2, hidden // 16, width)
+    spec = pl.BlockSpec((1, *shape[1:]), lambda i: (i, 0, 0, 0))
+    shapes = (
+        jax.ShapeDtypeStruct(shape, jnp.float32),
+        jax.ShapeDtypeStruct(shape, jnp.bfloat16),
+    )
+    return shapes, (spec, spec)
+
+
+def expert_out_grad(hidden, grads, scale):
+    units, count = hidden.shape
+    width = grads.shape[1]
+    shapes, specs = share_shapes(units, width)
+    return pl.pallas_call(
+        lambda *refs: expert_out_grad_kernel(scale, *refs),
+        grid=(4,),
+        out_shape=shapes,
+        in_specs=[
+            pl.BlockSpec((units // 4, count), lambda i: (i, 0)),
+            pl.BlockSpec((count, width), lambda i: (0, 0)),
+        ],
+        out_specs=specs,
+        compiler_params=pltpu.CompilerParams(vmem_limit_bytes=VMEM_LIMIT),
+        cost_estimate=pl.CostEstimate(
+            flops=2 * units * count * width, transcendentals=0, bytes_accessed=2 * units * count
+        ),
+    )(hidden, grads)
+
+
+def expert_in_grad(slopes, out_weight, in_weight, rows, grads, scale):
+    units, count = slopes.shape
+    width = grads.shape[1]
+    shapes, specs = share_shapes(units, width)
+    return pl.pallas_call(
+        lambda *refs: expert_in_grad_kernel(scale, *refs),
+        grid=(4,),
+        out_shape=(*shapes, jax.ShapeDtypeStruct((count, width), jnp.bfloat16)),
+        in_specs=[
+            pl.BlockSpec((units // 4, count), lambda i: (i, 0)),
+            pl.BlockSpec((units // 4, width), lambda i: (i, 0)),
+            pl.BlockSpec((width, units // 4), lambda i: (0, i)),
+            pl.BlockSpec((count, width), lambda i: (0, 0)),
+            pl.BlockSpec((count, width), lambda i: (0, 0)),
+        ],
+        out_specs=(*specs, pl.BlockSpec((count, width), lambda i: (0, 0))),
+        scratch_shapes=[pltpu.VMEM((width, count), jnp.float32)],
+        compiler_params=pltpu.CompilerParams(vmem_limit_bytes=VMEM_LIMIT),
+        cost_estimate=pl.CostEstimate(
+            flops=6 * units * count * width, transcendentals=0, bytes_accessed=4 * units * count
+        ),
+    )(slopes, out_weight, in_weight, rows, grads)
+
+
+def swap(block, distance):
+    return hop(block.astype(jnp.bfloat16), "blk", lambda i: i ^ distance).astype(jnp.float32)
+
+
+def sum_over_z(blocks):
+    return blocks[0] + (swap(blocks[1], 4) + (swap(blocks[2], 8) + swap(blocks[3], 12)))
 
 
 def local(
@@ -251,6 +484,8 @@
     capacity = 4 * block_rows // (exp_count * exp_count)
     experts = router_weight.shape[0]
     grad_scale = 1.0 / math.sqrt(block_rows * blk_count)
+    block = lax.axis_index("blk")
+    place = jnp.stack([block // 4, (block // 2) % 2, block % 2]).astype(jnp.int32)
     keys_values = jnp.einsum(
         "fd,td->ft",
         attention_weights[1:].reshape(2 * features, width),
@@ -260,14 +495,14 @@
     query = jnp.einsum(
         "fd,td->ft", attention_weights[0], nodes, preferred_element_type=jnp.float32
     ).astype(jnp.bfloat16)
-    attended, last_arrived = attention(query, keys_values, exp_count)
-    full_output_weight = gather_by_halves(output_weight, "exp")
-    both_weights, _ = lax.optimization_barrier(
-        (jnp.concatenate([expert_in, expert_out], axis=0), last_arrived)
-    )
-    all_weights = lax.all_gather(both_weights, "blk", axis=1, tiled=True)
-    weight_rows_in, weight_rows_out = all_weights[0], all_weights[1]
-    by_feature = to_sources(attended).reshape(exp_count * features, own_rows)
+    attended, full_output_weight, all_weights = attention(
+        query,
+        keys_values,
+        output_weight,
+        jnp.concatenate([expert_in, expert_out], axis=0),
+        exp_count,
+    )
+    by_feature = exchange(attended).reshape(exp_count * features, own_rows)
     attn_out = jnp.einsum(
         "fr,fd->rd", by_feature, full_output_weight, preferred_element_type=jnp.float32
     )
@@ -298,13 +533,11 @@
         jnp.bfloat16
     )
     outgoing = outgoing.reshape(experts, capacity, width)
-    arrived = lax.all_to_all(outgoing, "exp", split_axis=0, concat_axis=0, tiled=True)
-    pre_act = jnp.einsum("scd,hd->sch", arrived, weight_rows_in, preferred_element_type=jnp.float32)
-    expert_hidden = gelu_tanh(pre_act).astype(jnp.bfloat16)
-    result = jnp.einsum(
-        "sch,hd->scd", expert_hidden, weight_rows_out, preferred_element_type=jnp.float32
-    ).astype(jnp.bfloat16)
-    received, pre_act, returned = (arrived, pre_act, to_sources(result))
+    arrived = exchange(outgoing).reshape(experts * capacity, width)
+    result = expert_forward(arrived, all_weights)
+    returned = exchange(result.reshape(experts, capacity, width))
+    kept, result = lax.optimization_barrier((arrived, result))
+    hidden, slopes, out_weight, in_weight = expert_slopes(place, kept, all_weights)
     expert_rows = jnp.einsum(
         "ps,pd->sd",
         dispatch_table,
@@ -322,43 +555,29 @@
     router_part = jnp.dot(
         logit_grad.T, stream.astype(jnp.float32), precision=lax.Precision.HIGHEST
     )
-    small_sums = sum_by_halves(
-        jnp.concatenate([router_part, gain_part[None, :]], axis=0) * grad_scale, ("exp", "blk")
-    )
-    router_grad, gain_grad = small_sums[:-1], small_sums[-1]
+    small = jnp.concatenate([router_part, gain_part[None, :]], axis=0) * grad_scale
+    small = sum_pair(sum_near(small, "exp", 1), "exp", 4)
+    small = sum_pair(sum_pair(sum_near(small, "blk", 4), "blk", 2), "blk", 1)
+    router_grad, gain_grad = small[:-1], small[-1]
     assigned_grads = (
         (gates[..., None] * grad_two[:, None, :]).astype(jnp.bfloat16).reshape(2 * own_rows, width)
     )
     grad_outgoing = jnp.dot(
         dispatch_table, assigned_grads, preferred_element_type=jnp.float32
     ).astype(jnp.bfloat16)
-    grad_arrived = lax.all_to_all(
-        grad_outgoing.reshape(experts, capacity, width),
-        "exp",
-        split_axis=0,
-        concat_axis=0,
-        tiled=True,
-    )
-    hidden_full, gelu_back = jax.vjp(gelu_tanh, pre_act)
-    hidden = hidden_full.astype(jnp.bfloat16)
-    hidden_grad = jnp.einsum(
-        "scd,hd->sch", grad_arrived, weight_rows_out, preferred_element_type=jnp.float32
-    )
-    pre_grad = gelu_back(hidden_grad)[0].astype(jnp.bfloat16)
-    term_in = jnp.einsum("sch,scd->hd", pre_grad, received, preferred_element_type=jnp.float32)
-    term_out = jnp.einsum("sch,scd->hd", hidden, grad_arrived, preferred_element_type=jnp.float32)
-    summed_grads = lax.psum_scatter(
-        (jnp.concatenate([term_in, term_out], axis=1) * grad_scale).astype(jnp.bfloat16),
-        "blk",
-        scatter_dimension=0,
-        tiled=True,
-    ).astype(jnp.float32)
-    expert_in_grad = summed_grads[None, :, :width]
-    expert_out_grad = summed_grads[None, :, width:]
-    rows_back = jnp.einsum(
-        "sch,hd->scd", pre_grad, weight_rows_in, preferred_element_type=jnp.float32
-    ).astype(jnp.bfloat16)
-    back_home = to_sources(rows_back)
+    grad_arrived = exchange(grad_outgoing.reshape(experts, capacity, width)).reshape(
+        experts * capacity, width
+    )
+    out_mine, out_theirs = expert_out_grad(hidden, grad_arrived, grad_scale)
+    in_mine, in_theirs, rows_back = expert_in_grad(
+        slopes, out_weight, in_weight, kept, grad_arrived, grad_scale
+    )
+    out_sums = out_mine + swap(out_theirs, 1)
+    out_sums = out_sums[:, 0] + swap(out_sums[:, 1], 2)
+    expert_out_grads = sum_over_z(out_sums)[None]
+    in_sums = sum_over_z(in_mine + swap(in_theirs, 1))
+    expert_in_grads = (in_sums[0] + swap(in_sums[1], 2))[None]
+    back_home = exchange(rows_back.reshape(experts, capacity, width))
     back_rows = jnp.einsum(
         "ps,pd->sd",
         dispatch_table,
@@ -372,7 +591,7 @@
     stream_grad = (grad_two + (back_rows[:, 0] + back_rows[:, 1]) + router_term).astype(
         jnp.bfloat16
     )
-    return (layer_out, stream_grad, expert_in_grad, expert_out_grad, router_grad, gain_grad)
+    return (layer_out, stream_grad, expert_in_grads, expert_out_grads, router_grad, gain_grad)
 
 
 def solution(mesh):

time: 363 us -> 327 us (0.901)
  Pallas kernels: 116 us -> 150 us
  waiting for transfers between devices: 104 us -> 74 us
  matrix products: 34.9 us -> 12.2 us
  blocking collectives: 17.2 us -> 0 us
  local copies, waits for them, and re-layouts: 19.3 us -> 8.15 us
  starting transfers between devices: 46.3 us -> 56.5 us
    pallas_call x0 -> x4, Pallas kernels: none -> 34.9 us  [the longest x1 11.1 us: expert_in_grad(): pl.pallas_call(lambda *refs: expert_in_grad_kernel(scale, *refs), grid=(4...]
    unnamed x3 -> x1, waiting for transfers between devices: 25.4 us -> 0.02 us
    dot_general x6 -> x0, matrix products: 24.3 us -> none  [the longest x1 7.62 us: local(): jnp.einsum('scd,hd->sch', grad_arrived, weight_rows_out, preferred_elemen...]
    all_to_all x1 -> x0, blocking collectives: 17.2 us -> none  [local(): lax.all_to_all(grad_outgoing.reshape(experts, capacity, width), 'exp', sp...]
    unnamed x61 -> x43, local copies, waits for them, and re-layouts: 13.5 us -> 2.75 us
    ppermute x18 -> x30, waiting for transfers between devices: 45.8 us -> 38 us  [hop(): lax.ppermute(value, axis, [(i, target(i) % count) for i in range(count)])]
    ppermute x18 -> x30, starting transfers between devices: 31.4 us -> 37.2 us  [hop(): lax.ppermute(value, axis, [(i, target(i) % count) for i in range(count)])]
    all_to_all x4 -> x5, starting transfers between devices: 14.8 us -> 19.3 us  [exchange(): lax.all_to_all(buffer, 'exp', split_axis=0, concat_axis=0, tiled=True)]
  transfers between devices with their start and end apart: 24 -> 36, of which waited for: 15 -> 16; matrix products, arithmetic and copies ran while one was open for 6% -> 6% of each run, Pallas kernels for 32% -> 40%
where the time goes in v2:
time: 327 us; the launch traced here: 326 us
  Pallas kernels  150 us (46%)
  waiting for transfers between devices  74 us (23%)
  starting transfers between devices  56.5 us (17%)
  between operations  14.7 us (4%)
  matrix products  12.2 us (4%)
  other arithmetic  9.68 us (3%)
  local copies, waits for them, and re-layouts  8.15 us (2%)
    pallas_call x4, Pallas kernels, attention_call(): pl.pallas_call(kernel, out_shape=out_shape, in_specs=specs * len(operands...  116 us
    ppermute x30, waiting for transfers between devices, hop(): lax.ppermute(value, axis, [(i, target(i) % count) for i in range(count)])  38 us
    ppermute x30, starting transfers between devices, hop(): lax.ppermute(value, axis, [(i, target(i) % count) for i in range(count)])  37.2 us
    all_to_all x5, waiting for transfers between devices, exchange(): lax.all_to_all(buffer, 'exp', split_axis=0, concat_axis=0, tiled=True)  35.9 us
    all_to_all x5, starting transfers between devices, exchange(): lax.all_to_all(buffer, 'exp', split_axis=0, concat_axis=0, tiled=True)  19.3 us
    pallas_call x1, Pallas kernels, expert_in_grad(): pl.pallas_call(lambda *refs: expert_in_grad_kernel(scale, *refs), grid=(4...  11.1 us
    pallas_call x1, Pallas kernels, expert_slopes(): pl.pallas_call(expert_slopes_kernel, out_shape=(jax.ShapeDtypeStruct((hid...  10.5 us
    pallas_call x1, Pallas kernels, expert_forward(): pl.pallas_call(expert_forward_kernel, grid=(hidden // tile,), out_shape=j...  7.88 us
  transfers between devices with their start and end apart: 36, of which 16 were waited for; matrix products, arithmetic and copies ran while one was open for 6% of the time, Pallas kernels for 40%

profile of v2, /device:TPU:0, one launch (start us, length us, event | category | flops | bytes accessed | tf_op | source)
XLA Modules:
  0.0 325.6 jit_solution(155994960830709017)
XLA Ops:
  7.3 1.0 slice.81
  8.2 2.0 convolution_convert_fusion.refs_1_.refs_5_
  10.2 4.0 %collective-permute-start.4 = (bf16[64,1536]{1,0:T(8,128)(2,1)S(1)}, bf16[64,1536]{1,0:T(8,128)(2,1)S(1)}, u32[]{:S(2)}, u32[]{:S(2)}) collective-permute-start(bf16[64,1536]{1,0:T(8,128)(2,1)S(1)} %convolution_convert_fusion.refs_1_.refs_5_), channel_id=1, source_target_pairs={{0,64},{8,72},{16,80},{24,88},{32,96},{40,104},{48,112},{56,120},{... | collective-permute-start | bytes 589832 | tf_op jit(solution)/shard_map/ppermute | solution.py:31
  14.3 0.7 collective-permute-start.3
  15.0 1.3 collective-permute-start.2
  16.3 1.6 collective-permute-start.1
  17.9 0.7 pad_maximum_fusion.2
  18.6 2.0 convolution_convert_fusion.1.refs_0_.refs_2_
  21.3 6.8 %shard_map.145 = (bf16[128,1536]{1,0:T(8,128)(2,1)}, f32[48,1536]{1,0:T(8,128)}) custom-call(bf16[32,1536]{1,0:T(8,128)(2,1)} %convolution_convert_fusion.1.refs_0_.refs_2_, bf16[64,1536]{1,0:T(8,128)(2,1)} %copy-done.10, bf16[64,1536]{1,0:T(8,128)(2,1)} %copy-done.20), custom_call_target="tpu_custom_call" | custom-call | flops 5662310400 | bytes 393216 | tf_op jit(solution)/shard_map/pallas_call | solution.py:148
  28.2 1.6 collective-permute-start.6
  30.3 11.9 %shard_map.146.refs_1_ = f32[48,1536]{1,0:T(8,128)} custom-call(bf16[128,1536]{1,0:T(8,128)(2,1)} %get-tuple-element.30.refs_0_, f32[48,1536]{1,0:T(8,128)} %get-tuple-element.36.refs_1_, bf16[64,1536]{1,0:T(8,128)(2,1)} %copy-done.11, bf16[64,1536]{1,0:T(8,128)(2,1)} %copy-done.7, bf16[64,1536]{1,0:T(8,128)(2,1)} %copy-done.6, ...), custom_call_target="tpu_custom_call", output_to_operand_aliasing={{}: (1, {})} | custom-call | flops 11324620800 | bytes 786432 | tf_op jit(solution)/shard_map/pallas_call | solution.py:148
  42.2 3.2 collective-permute-done.5.refs_3_
  45.9 0.9 reduce-window.6
  46.8 1.3 pad_maximum_fusion
  48.5 2.8 collective-permute-start.7
  51.5 3.1 collective-permute-done.7
  54.6 11.9 %shard_map.147.refs_1_ = f32[48,1536]{1,0:T(8,128)} custom-call(bf16[128,1536]{1,0:T(8,128)(2,1)} %get-tuple-element.30.refs_0_, f32[48,1536]{1,0:T(8,128)} %shard_map.146.refs_1_, bf16[256,1536]{1,0:T(8,128)(2,1)} %collective-permute-done.8.refs_2_.refs_11_), custom_call_target="tpu_custom_call", output_to_operand_aliasing={{}: (1, {})} | custom-call | flops 11324620800 | bytes 786432 | tf_op jit(solution)/shard_map/pallas_call | solution.py:148
  66.4 2.9 collective-permute-start.10
  69.3 85.0 %shard_map.148 = bf16[8,32,192]{2,1,0:T(8,128)(2,1)} custom-call(bf16[128,1536]{1,0:T(8,128)(2,1)} %get-tuple-element.30.refs_0_, f32[48,1536]{1,0:T(8,128)} %shard_map.147.refs_1_, bf16[32,1536]{1,0:T(8,128)(2,1)} %convolution_convert_fusion.1.refs_0_.refs_2_, bf16[192,1536]{1,0:T(8,128)(2,1)} %collective-permute-done.5.refs_3_, ...), custom_call_target="tpu_custom_call" | custom-call | flops 16986931200 | bytes 1179648 | tf_op jit(solution)/shard_map/pallas_call | solution.py:148
  154.4 4.2 %all-to-all-start = ((bf16[8,32,192]{2,1,0:T(8,128)(2,1)}), bf16[8,32,192]{2,1,0:T(8,128)(2,1)S(1)}, u32[]{:S(2)}, u32[]{:S(2)}) async-start(bf16[8,32,192]{2,1,0:T(8,128)(2,1)} %shard_map.148), calls=%async_computation | async-start | bytes 262144 | tf_op jit(solution)/shard_map/all_to_all | solution.py:26
  158.6 8.0 %all-to-all-done = bf16[8,32,192]{2,1,0:T(8,128)(2,1)S(1)} async-done(((bf16[8,32,192]{2,1,0:T(8,128)(2,1)}), bf16[8,32,192]{2,1,0:T(8,128)(2,1)S(1)}, u32[]{:S(2)}, u32[]{:S(2)}) %all-to-all-start) | async-done | bytes 98336 | tf_op jit(solution)/shard_map/all_to_all | solution.py:26
  167.5 1.5 convolution_convert_fusion.3
  169.0 3.5 %all-to-all-start.1 = ((bf16[8,96,512]{2,1,0:T(8,128)(2,1)}), bf16[8,96,512]{2,1,0:T(8,128)(2,1)S(1)}, u32[]{:S(2)}, u32[]{:S(2)}) async-start(bf16[8,96,512]{2,1,0:T(8,128)(2,1)} %bitcast.6), calls=%async_computation.1 | async-start | bytes 1572864 | tf_op jit(solution)/shard_map/all_to_all | solution.py:26
  172.9 1.1 eq.92
  174.8 10.8 %all-to-all-done.1 = bf16[8,96,512]{2,1,0:T(8,128)(2,1)S(1)} async-done(((bf16[8,96,512]{2,1,0:T(8,128)(2,1)}), bf16[8,96,512]{2,1,0:T(8,128)(2,1)S(1)}, u32[]{:S(2)}, u32[]{:S(2)}) %all-to-all-start.1) | async-done | bytes 786464 | tf_op jit(solution)/shard_map/all_to_all | solution.py:26
  185.5 1.0 copy-done.2
  186.5 7.9 %shard_map.149 = bf16[768,512]{1,0:T(8,128)(2,1)} custom-call(bf16[768,512]{1,0:T(8,128)(2,1)} %bitcast.109, bf16[2,2048,512]{2,1,0:T(8,128)(2,1)} %all-gather.2.cloned.1.call-done.in_ref.out_ref.refs_0_.refs_1_.refs_2_.refs_3_.refs_4_.refs_5_.refs_6_.refs_7_, ...), custom_call_target="tpu_custom_call" | custom-call | flops 3221225472 | bytes 4194304 | tf_op jit(solution)/shard_map/pallas_call | solution.py:279
  194.4 3.5 %all-to-all-start.2 = ((bf16[8,96,512]{2,1,0:T(8,128)(2,1)}), bf16[8,96,512]{2,1,0:T(8,128)(2,1)S(1)}, u32[]{:S(2)}, u32[]{:S(2)}) async-start(bf16[8,96,512]{2,1,0:T(8,128)(2,1)} %bitcast.116), calls=%async_computation.2 | async-start | bytes 1572864 | tf_op jit(solution)/shard_map/all_to_all | solution.py:26
  198.2 10.5 %shard_map.150 = (bf16[2048,768]{1,0:T(8,128)(2,1)}, f32[2048,768]{1,0:T(8,128)}, bf16[2048,512]{1,0:T(8,128)(2,1)}, bf16[512,2048]{1,0:T(8,128)(2,1)}) custom-call(s32[3]{0:T(128)} %pad_add_fusion.place_ref, bf16[768,512]{1,0:T(8,128)(2,1)} %bitcast.110, ...), custom_call_target="tpu_custom_call" | custom-call | flops 1610612736 | bytes 17825792 | tf_op jit(solution)/shard_map/pallas_call | solution.py:330
  208.7 3.4 %all-to-all-done.2 = bf16[8,96,512]{2,1,0:T(8,128)(2,1)S(1)} async-done(((bf16[8,96,512]{2,1,0:T(8,128)(2,1)}), bf16[8,96,512]{2,1,0:T(8,128)(2,1)S(1)}, u32[]{:S(2)}, u32[]{:S(2)}) %all-to-all-start.2) | async-done | bytes 786464 | tf_op jit(solution)/shard_map/all_to_all | solution.py:26
  212.1 1.6 fusion.22
  214.1 0.8 add_add_fusion
  215.8 1.6 convolution_convert_fusion.2
  217.4 3.8 %all-to-all-start.3 = ((bf16[8,96,512]{2,1,0:T(8,128)(2,1)}), bf16[8,96,512]{2,1,0:T(8,128)(2,1)S(1)}, u32[]{:S(2)}, u32[]{:S(2)}) async-start(bf16[8,96,512]{2,1,0:T(8,128)(2,1)} %bitcast.17), calls=%async_computation.3 | async-start | bytes 1572864 | tf_op jit(solution)/shard_map/all_to_all | solution.py:26
  221.6 13.8 %all-to-all-done.3 = bf16[8,96,512]{2,1,0:T(8,128)(2,1)S(1)} async-done(((bf16[8,96,512]{2,1,0:T(8,128)(2,1)}), bf16[8,96,512]{2,1,0:T(8,128)(2,1)S(1)}, u32[]{:S(2)}, u32[]{:S(2)}) %all-to-all-start.3) | async-done | bytes 786464 | tf_op jit(solution)/shard_map/all_to_all | solution.py:26
  235.4 0.9 copy-done.8
  236.3 11.1 %shard_map.151 = (f32[4,2,128,512]{3,2,1,0:T(8,128)}, bf16[4,2,128,512]{3,2,1,0:T(8,128)(2,1)}, bf16[768,512]{1,0:T(8,128)(2,1)}) custom-call(f32[2048,768]{1,0:T(8,128)} %get-tuple-element.45.refs_0_, bf16[2048,512]{1,0:T(8,128)(2,1)} %get-tuple-element.46.refs_1_, bf16[512,2048]{1,0:T(8,128)(2,1)} %get-tuple-element.47.refs_2_, ...), custom_call_target="tpu_custom_call" | custom-call | flops 4831838208 | bytes 6291456 | tf_op jit(solution)/shard_map/pallas_call | solution.py:438
  247.4 4.2 %all-to-all-start.4 = ((bf16[8,96,512]{2,1,0:T(8,128)(2,1)}), bf16[8,96,512]{2,1,0:T(8,128)(2,1)}, u32[]{:S(2)}, u32[]{:S(2)}) async-start(bf16[8,96,512]{2,1,0:T(8,128)(2,1)} %bitcast.112), calls=%async_computation.4 | async-start | bytes 1572864 | tf_op jit(solution)/shard_map/all_to_all | solution.py:26
  251.8 3.4 %collective-permute-start.22 = (f32[9,512]{1,0:T(8,128)S(1)}, f32[9,512]{1,0:T(8,128)S(1)}, u32[]{:S(2)}, u32[]{:S(2)}) collective-permute-start(f32[9,512]{1,0:T(8,128)S(1)} %maximum_multiply_fusion), channel_id=1, source_target_pairs={{0,2},{1,3},{2,0},{3,1},{4,6},{5,7},{6,4},{7,5},{8,10},{9,11},{10,... | collective-permute-start | bytes 55304 | tf_op jit(solution)/shard_map/ppermute | solution.py:31
  255.2 1.2 collective-permute-start.23
  256.3 8.7 %collective-permute-done.22 = f32[9,512]{1,0:T(8,128)S(1)} collective-permute-done((f32[9,512]{1,0:T(8,128)S(1)}, f32[9,512]{1,0:T(8,128)S(1)}, u32[]{:S(2)}, u32[]{:S(2)}) %collective-permute-start.22) | collective-permute-done | bytes 18464 | tf_op jit(solution)/shard_map/ppermute | solution.py:31
  265.1 3.1 collective-permute-start.24
  268.2 2.4 collective-permute-done.24
  270.6 1.6 collective-permute-start.27
  272.9 1.8 collective-permute-start.25
  274.7 5.4 %shard_map.152 = (f32[4,2,128,512]{3,2,1,0:T(8,128)}, bf16[4,2,128,512]{3,2,1,0:T(8,128)(2,1)}) custom-call(bf16[2048,768]{1,0:T(8,128)(2,1)} %get-tuple-element.51.refs_0_, bf16[768,512]{1,0:T(8,128)(2,1)} %bitcast.114), custom_call_target="tpu_custom_call" | custom-call | flops 1610612736 | bytes 3145728 | tf_op jit(solution)/shard_map/pallas_call | solution.py:418
  280.3 3.8 %collective-permute-done.28 = f32[9,512]{1,0:T(8,128)S(1)} collective-permute-done((f32[9,512]{1,0:T(8,128)S(1)}, f32[9,512]{1,0:T(8,128)S(1)}, u32[]{:S(2)}, u32[]{:S(2)}) %collective-permute-start.28) | collective-permute-done | bytes 18464 | tf_op jit(solution)/shard_map/ppermute | solution.py:31
  284.2 1.2 collective-permute-done.29
  286.6 1.8 fusion.20
  288.4 1.8 fusion.49
  290.6 1.5 collective-permute-start.14
  292.1 2.4 collective-permute-start.13
  295.2 1.1 fusion
  296.3 3.3 collective-permute-done.12
  299.5 6.1 %collective-permute-done.14 = bf16[2,128,512]{2,1,0:T(8,128)(2,1)S(1)} collective-permute-done((bf16[2,128,512]{2,1,0:T(8,128)(2,1)S(1)}, bf16[2,128,512]{2,1,0:T(8,128)(2,1)S(1)}, u32[]{:S(2)}, u32[]{:S(2)}) %collective-permute-start.14) | collective-permute-done | bytes 262176 | tf_op jit(solution)/shard_map/ppermute | solution.py:31
  305.8 0.9 collective-permute-start.15
  306.7 2.0 collective-permute-done.17
  308.9 0.8 collective-permute-start.18
  309.8 1.8 collective-permute-start.20
  311.5 1.6 collective-permute-start.19
  313.1 0.7 fusion.27
  314.3 1.7 collective-permute-done.20
  316.0 2.0 collective-permute-done.19
  318.0 0.8 fusion.25
  (130 shorter events, 10.4 us)
Async XLA Ops:
  7.2 167.4 %copy-start = (bf16[8,512]{1,0:T(8,128)(2,1)S(1)}, bf16[8,512]{1,0:T(8,128)(2,1)}, u32[]{:S(2)}) copy-start(bf16[8,512]{1,0:T(8,128)(2,1)} %param.13) | copy-start | bytes 24580
  7.2 11.4 %copy-start.1 = (bf16[1536,512]{1,0:T(8,128)(2,1)S(1)}, bf16[1536,512]{1,0:T(8,128)(2,1)}, u32[]{:S(2)}) copy-start(bf16[1536,512]{1,0:T(8,128)(2,1)} %param.10) | copy-start | bytes 4718596
  7.2 10.7 %copy-start.12 = (bf16[1,128,512]{2,1,0:T(8,128)(2,1)S(1)}, bf16[1,128,512]{2,1,0:T(8,128)(2,1)}, u32[]{:S(2)}) copy-start(bf16[1,128,512]{2,1,0:T(8,128)(2,1)} %param.17) | copy-start | bytes 393220
  7.2 10.7 %copy-start.13 = (bf16[1,128,512]{2,1,0:T(8,128)(2,1)S(1)}, bf16[1,128,512]{2,1,0:T(8,128)(2,1)}, u32[]{:S(2)}) copy-start(bf16[1,128,512]{2,1,0:T(8,128)(2,1)} %param.16) | copy-start | bytes 393220
  7.2 178.3 %all-gather.2.cloned.1.call-start = ((), (), s32[]{:S(2)}) async-start(), calls=%async_computation.5 | async-start | bytes 4456448 | tf_op jit(solution)/shard_map/all_gather | solution.py:217
  10.2 10.4 %copy-start.10 = (bf16[64,1536]{1,0:T(8,128)(2,1)}, bf16[64,1536]{1,0:T(8,128)(2,1)S(1)}, u32[]{:S(2)}) copy-start(bf16[64,1536]{1,0:T(8,128)(2,1)S(1)} %convolution_convert_fusion.refs_1_.refs_5_) | copy-start | bytes 589828
  10.2 17.9 %collective-permute-start.4 = (bf16[64,1536]{1,0:T(8,128)(2,1)S(1)}, bf16[64,1536]{1,0:T(8,128)(2,1)S(1)}, u32[]{:S(2)}, u32[]{:S(2)}) collective-permute-start(bf16[64,1536]{1,0:T(8,128)(2,1)S(1)} %convolution_convert_fusion.refs_1_.refs_5_), channel_id=1, source_target_pairs={{0,64},{8,72},{16,80},{24,88},{32,96},{40,104},{48,112},{56,120},{... | collective-permute-start | bytes 589832 | tf_op jit(solution)/shard_map/ppermute | solution.py:31
  14.3 13.8 %collective-permute-start.3 = (bf16[64,1536]{1,0:T(8,128)(2,1)S(1)}, bf16[64,1536]{1,0:T(8,128)(2,1)S(1)}, u32[]{:S(2)}, u32[]{:S(2)}) collective-permute-start(bf16[64,1536]{1,0:T(8,128)(2,1)S(1)} %convolution_convert_fusion.refs_1_.refs_5_), channel_id=1, source_target_pairs={{0,96},{8,104},{16,112},{24,120},{32,0},{40,8},{48,16},{56,24},{64... | collective-permute-start | bytes 589832 | tf_op jit(solution)/shard_map/ppermute | solution.py:31
  15.0 13.1 %collective-permute-start.2 = (bf16[64,1536]{1,0:T(8,128)(2,1)S(1)}, bf16[64,1536]{1,0:T(8,128)(2,1)S(1)}, u32[]{:S(2)}, u32[]{:S(2)}) collective-permute-start(bf16[64,1536]{1,0:T(8,128)(2,1)S(1)} %convolution_convert_fusion.refs_1_.refs_5_), channel_id=1, source_target_pairs={{0,32},{8,40},{16,48},{24,56},{32,64},{40,72},{48,80},{56,88},{64,... | collective-permute-start | bytes 589832 | tf_op jit(solution)/shard_map/ppermute | solution.py:31
  16.3 11.8 %collective-permute-start.1 = (bf16[64,1536]{1,0:T(8,128)(2,1)S(1)}, bf16[64,1536]{1,0:T(8,128)(2,1)S(1)}, u32[]{:S(2)}, u32[]{:S(2)}) collective-permute-start(bf16[64,1536]{1,0:T(8,128)(2,1)S(1)} %convolution_convert_fusion.refs_1_.refs_5_), channel_id=1, source_target_pairs={{0,16},{8,24},{16,0},{24,8},{32,48},{40,56},{48,32},{56,40},{64,80... | collective-permute-start | bytes 589832 | tf_op jit(solution)/shard_map/ppermute | solution.py:31
  17.9 2.7 collective-permute-start
  20.6 7.6 %copy-start.16 = (bf16[32,512]{1,0:T(8,128)(2,1)S(1)}, bf16[32,512]{1,0:T(8,128)(2,1)}, u32[]{:S(2)}) copy-start(bf16[32,512]{1,0:T(8,128)(2,1)} %param.12) | copy-start | bytes 98308
  20.6 0.7 copy-start.20
  28.1 2.2 copy-start.5
  28.1 2.2 copy-start.6
  28.1 2.2 copy-start.7
  28.1 2.2 copy-start.11
  28.2 14.0 %collective-permute-start.6 = (bf16[32,512]{1,0:T(8,128)(2,1)S(1)}, bf16[32,512]{1,0:T(8,128)(2,1)S(1)}, u32[]{:S(2)}, u32[]{:S(2)}) collective-permute-start(bf16[32,512]{1,0:T(8,128)(2,1)S(1)} %copy-done.16), channel_id=1, source_target_pairs={{0,1},{1,0},{2,3},{3,2},{4,5},{5,4},{6,7},{7,6},{8,9},{9,8},{10,11... | collective-permute-start | bytes 98312 | tf_op jit(solution)/shard_map/ppermute | solution.py:31
  29.8 15.6 %collective-permute-start.5 = (bf16[192,1536]{1,0:T(8,128)(2,1)S(1)}, bf16[192,1536]{1,0:T(8,128)(2,1)}, u32[]{:S(2)}, u32[]{:S(2)}) collective-permute-start(bf16[192,1536]{1,0:T(8,128)(2,1)S(1)} %pad_maximum_fusion.1), channel_id=1, source_target_pairs={{0,16},{8,24},{16,0},{24,8},{32,48},{40,56},{48,32},{56,40},{64,80... | collective-permute-start | bytes 1769480 | tf_op jit(solution)/shard_map/ppermute | solution.py:31
  30.3 15.1 %copy-start.17 = (s32[192,2]{0,1:T(2,128)S(1)}, s32[192,2]{0,1:T(2,128)}, u32[]{:S(2)}) copy-start(s32[192,2]{0,1:T(2,128)} %param.18) | copy-start | bytes 4612
  48.0 6.6 %collective-permute-start.8 = (bf16[256,1536]{1,0:T(8,128)(2,1)S(1)}, bf16[256,1536]{1,0:T(8,128)(2,1)}, u32[]{:S(2)}, u32[]{:S(2)}) collective-permute-start(bf16[256,1536]{1,0:T(8,128)(2,1)S(1)} %pad_maximum_fusion), channel_id=1, source_target_pairs={{0,8},{8,0},{16,24},{24,16},{32,40},{40,32},{48,56},{56,48},{64,72... | collective-permute-start | bytes 2359304 | tf_op jit(solution)/shard_map/ppermute | solution.py:31
  48.5 6.1 %collective-permute-start.7 = (bf16[64,512]{1,0:T(8,128)(2,1)S(1)}, bf16[64,512]{1,0:T(8,128)(2,1)S(1)}, u32[]{:S(2)}, u32[]{:S(2)}) collective-permute-start(bf16[64,512]{1,0:T(8,128)(2,1)S(1)} %pad_maximum_fusion.4), channel_id=1, source_target_pairs={{0,2},{1,3},{2,0},{3,1},{4,6},{5,7},{6,4},{7,5},{8,10},{9,11},{10,... | collective-permute-start | bytes 196616 | tf_op jit(solution)/shard_map/ppermute | solution.py:31
  51.3 18.1 %collective-permute-start.9 = (bf16[192,1536]{1,0:T(8,128)(2,1)}, bf16[192,1536]{1,0:T(8,128)(2,1)}, u32[]{:S(2)}, u32[]{:S(2)}) collective-permute-start(bf16[192,1536]{1,0:T(8,128)(2,1)} %collective-permute-done.5.refs_3_), channel_id=1, source_target_pairs={{0,8},{8,0},{16,24},{24,16},{32,40},{40,32},{48,56},{56,48},{64,72... | collective-permute-start | bytes 1769480 | tf_op jit(solution)/shard_map/ppermute | solution.py:31
  66.4 92.2 %collective-permute-start.10 = (bf16[128,512]{1,0:T(8,128)(2,1)S(1)}, bf16[128,512]{1,0:T(8,128)(2,1)S(1)}, u32[]{:S(2)}, u32[]{:S(2)}) collective-permute-start(bf16[128,512]{1,0:T(8,128)(2,1)S(1)} %pad_maximum_fusion.3), channel_id=1, source_target_pairs={{0,4},{1,5},{2,6},{3,7},{4,0},{5,1},{6,2},{7,3},{8,12},{9,13},{10,... | collective-permute-start | bytes 393224 | tf_op jit(solution)/shard_map/ppermute | solution.py:31
  154.4 12.6 %copy-start.18 = (f32[512]{0:T(512)S(1)}, f32[512]{0:T(512)}, u32[]{:S(2)}) copy-start(f32[512]{0:T(512)} %param.14) | copy-start | bytes 6148
  154.4 12.3 %all-to-all-start = ((bf16[8,32,192]{2,1,0:T(8,128)(2,1)}), bf16[8,32,192]{2,1,0:T(8,128)(2,1)S(1)}, u32[]{:S(2)}, u32[]{:S(2)}) async-start(bf16[8,32,192]{2,1,0:T(8,128)(2,1)} %shard_map.148), calls=%async_computation | async-start | bytes 262144 | tf_op jit(solution)/shard_map/all_to_all | solution.py:26
  169.0 16.5 %all-to-all-start.1 = ((bf16[8,96,512]{2,1,0:T(8,128)(2,1)}), bf16[8,96,512]{2,1,0:T(8,128)(2,1)S(1)}, u32[]{:S(2)}, u32[]{:S(2)}) async-start(bf16[8,96,512]{2,1,0:T(8,128)(2,1)} %bitcast.6), calls=%async_computation.1 | async-start | bytes 1572864 | tf_op jit(solution)/shard_map/all_to_all | solution.py:26
  185.5 1.0 copy-start.2
  194.4 17.7 %all-to-all-start.2 = ((bf16[8,96,512]{2,1,0:T(8,128)(2,1)}), bf16[8,96,512]{2,1,0:T(8,128)(2,1)S(1)}, u32[]{:S(2)}, u32[]{:S(2)}) async-start(bf16[8,96,512]{2,1,0:T(8,128)(2,1)} %bitcast.116), calls=%async_computation.2 | async-start | bytes 1572864 | tf_op jit(solution)/shard_map/all_to_all | solution.py:26
  212.1 1.9 copy-start.9
  212.1 1.9 copy-start.19
  217.4 18.0 %all-to-all-start.3 = ((bf16[8,96,512]{2,1,0:T(8,128)(2,1)}), bf16[8,96,512]{2,1,0:T(8,128)(2,1)S(1)}, u32[]{:S(2)}, u32[]{:S(2)}) async-start(bf16[8,96,512]{2,1,0:T(8,128)(2,1)} %bitcast.17), calls=%async_computation.3 | async-start | bytes 1572864 | tf_op jit(solution)/shard_map/all_to_all | solution.py:26
  221.4 26.0 %copy-start.14 = (f32[192,8]{0,1:T(8,128)}, f32[192,8]{0,1:T(8,128)S(1)}, u32[]{:S(2)}) copy-start(f32[192,8]{0,1:T(8,128)S(1)} %multiply_reduce_fusion.3) | copy-start | bytes 18436
  235.4 0.9 copy-start.8
  247.4 39.1 %all-to-all-start.4 = ((bf16[8,96,512]{2,1,0:T(8,128)(2,1)}), bf16[8,96,512]{2,1,0:T(8,128)(2,1)}, u32[]{:S(2)}, u32[]{:S(2)}) async-start(bf16[8,96,512]{2,1,0:T(8,128)(2,1)} %bitcast.112), calls=%async_computation.4 | async-start | bytes 1572864 | tf_op jit(solution)/shard_map/all_to_all | solution.py:26
  251.7 36.7 %collective-permute-start.11 = (bf16[4,2,128,512]{3,2,1,0:T(8,128)(2,1)}, bf16[4,2,128,512]{3,2,1,0:T(8,128)(2,1)}, u32[]{:S(2)}, u32[]{:S(2)}) collective-permute-start(bf16[4,2,128,512]{3,2,1,0:T(8,128)(2,1)} %get-tuple-element.50), channel_id=1, source_target_pairs={{0,8},{8,0},{16,24},{24,16},{32,40},{40,32},{48,56},{56,48},{64,72... | collective-permute-start | bytes 3145736 | tf_op jit(solution)/shard_map/ppermute | solution.py:31
  251.8 13.3 %collective-permute-start.22 = (f32[9,512]{1,0:T(8,128)S(1)}, f32[9,512]{1,0:T(8,128)S(1)}, u32[]{:S(2)}, u32[]{:S(2)}) collective-permute-start(f32[9,512]{1,0:T(8,128)S(1)} %maximum_multiply_fusion), channel_id=1, source_target_pairs={{0,2},{1,3},{2,0},{3,1},{4,6},{5,7},{6,4},{7,5},{8,10},{9,11},{10,... | collective-permute-start | bytes 55304 | tf_op jit(solution)/shard_map/ppermute | solution.py:31
  255.2 9.9 %collective-permute-start.23 = (f32[9,512]{1,0:T(8,128)S(1)}, f32[9,512]{1,0:T(8,128)S(1)}, u32[]{:S(2)}, u32[]{:S(2)}) collective-permute-start(f32[9,512]{1,0:T(8,128)S(1)} %maximum_multiply_fusion), channel_id=1, source_target_pairs={{0,3},{1,2},{2,1},{3,0},{4,7},{5,6},{6,5},{7,4},{8,11},{9,10},{10,... | collective-permute-start | bytes 55304 | tf_op jit(solution)/shard_map/ppermute | solution.py:31
  256.3 8.7 %collective-permute-start.21 = (f32[9,512]{1,0:T(8,128)S(1)}, f32[9,512]{1,0:T(8,128)S(1)}, u32[]{:S(2)}, u32[]{:S(2)}) collective-permute-start(f32[9,512]{1,0:T(8,128)S(1)} %maximum_multiply_fusion), channel_id=1, source_target_pairs={{0,1},{1,0},{2,3},{3,2},{4,5},{5,4},{6,7},{7,6},{8,9},{9,8},{10,11... | collective-permute-start | bytes 55304 | tf_op jit(solution)/shard_map/ppermute | solution.py:31
  265.1 5.5 %collective-permute-start.24 = (f32[9,512]{1,0:T(8,128)S(1)}, f32[9,512]{1,0:T(8,128)S(1)}, u32[]{:S(2)}, u32[]{:S(2)}) collective-permute-start(f32[9,512]{1,0:T(8,128)S(1)} %add_add_fusion.2), channel_id=1, source_target_pairs={{0,4},{1,5},{2,6},{3,7},{4,0},{5,1},{6,2},{7,3},{8,12},{9,13},{10,... | collective-permute-start | bytes 55304 | tf_op jit(solution)/shard_map/ppermute | solution.py:31
  270.6 9.5 %collective-permute-start.27 = (f32[9,512]{1,0:T(8,128)S(1)}, f32[9,512]{1,0:T(8,128)S(1)}, u32[]{:S(2)}, u32[]{:S(2)}) collective-permute-start(f32[9,512]{1,0:T(8,128)S(1)} %add.160), channel_id=1, source_target_pairs={{0,96},{8,104},{16,112},{24,120},{32,64},{40,72},{48,80},{56,88},{... | collective-permute-start | bytes 55304 | tf_op jit(solution)/shard_map/ppermute | solution.py:31
  272.2 7.9 %collective-permute-start.26 = (f32[9,512]{1,0:T(8,128)S(1)}, f32[9,512]{1,0:T(8,128)S(1)}, u32[]{:S(2)}, u32[]{:S(2)}) collective-permute-start(f32[9,512]{1,0:T(8,128)S(1)} %add.160), channel_id=1, source_target_pairs={{0,64},{8,72},{16,80},{24,88},{32,96},{40,104},{48,112},{56,120},{... | collective-permute-start | bytes 55304 | tf_op jit(solution)/shard_map/ppermute | solution.py:31
  272.9 7.3 %collective-permute-start.25 = (f32[9,512]{1,0:T(8,128)S(1)}, f32[9,512]{1,0:T(8,128)S(1)}, u32[]{:S(2)}, u32[]{:S(2)}) collective-permute-start(f32[9,512]{1,0:T(8,128)S(1)} %add.160), channel_id=1, source_target_pairs={{0,32},{8,40},{16,48},{24,56},{32,0},{40,8},{48,16},{56,24},{64,96... | collective-permute-start | bytes 55304 | tf_op jit(solution)/shard_map/ppermute | solution.py:31
  280.1 8.3 %copy-start.3 = (f32[4,2,128,512]{3,2,1,0:T(8,128)S(1)}, f32[4,2,128,512]{3,2,1,0:T(8,128)}, u32[]{:S(2)}) copy-start(f32[4,2,128,512]{3,2,1,0:T(8,128)} %get-tuple-element.49) | copy-start | bytes 6291460
  280.1 14.4 %collective-permute-start.16 = (bf16[4,2,128,512]{3,2,1,0:T(8,128)(2,1)}, bf16[4,2,128,512]{3,2,1,0:T(8,128)(2,1)S(1)}, u32[]{:S(2)}, u32[]{:S(2)}) collective-permute-start(bf16[4,2,128,512]{3,2,1,0:T(8,128)(2,1)} %get-tuple-element.53), channel_id=1, source_target_pairs={{0,8},{8,0},{16,24},{24,16},{32,40},{40,32},{48,56},{56,48},{64,72... | collective-permute-start | bytes 3145736 | tf_op jit(solution)/shard_map/ppermute | solution.py:31
  280.2 4.0 %collective-permute-start.28 = (f32[9,512]{1,0:T(8,128)S(1)}, f32[9,512]{1,0:T(8,128)S(1)}, u32[]{:S(2)}, u32[]{:S(2)}) collective-permute-start(f32[9,512]{1,0:T(8,128)S(1)} %add_add_fusion.1), channel_id=1, source_target_pairs={{0,16},{8,24},{16,0},{24,8},{32,48},{40,56},{48,32},{56,40},{64,80... | collective-permute-start | bytes 55304 | tf_op jit(solution)/shard_map/ppermute | solution.py:31
  284.2 1.2 collective-permute-start.29
  288.4 6.1 %copy-start.4 = (f32[4,2,128,512]{3,2,1,0:T(8,128)S(1)}, f32[4,2,128,512]{3,2,1,0:T(8,128)}, u32[]{:S(2)}) copy-start(f32[4,2,128,512]{3,2,1,0:T(8,128)} %get-tuple-element.52) | copy-start | bytes 6291460
  290.3 9.2 %collective-permute-start.12 = (bf16[2,128,512]{2,1,0:T(8,128)(2,1)S(1)}, bf16[2,128,512]{2,1,0:T(8,128)(2,1)S(1)}, u32[]{:S(2)}, u32[]{:S(2)}) collective-permute-start(bf16[2,128,512]{2,1,0:T(8,128)(2,1)S(1)} %get-tuple-element.64), channel_id=1, source_target_pairs={{0,32},{8,40},{16,48},{24,56},{32,0},{40,8},{48,16},{56,24},{64,96... | collective-permute-start | bytes 786440 | tf_op jit(solution)/shard_map/ppermute | solution.py:31
  290.6 15.1 %collective-permute-start.14 = (bf16[2,128,512]{2,1,0:T(8,128)(2,1)S(1)}, bf16[2,128,512]{2,1,0:T(8,128)(2,1)S(1)}, u32[]{:S(2)}, u32[]{:S(2)}) collective-permute-start(bf16[2,128,512]{2,1,0:T(8,128)(2,1)S(1)} %get-tuple-element.65), channel_id=1, source_target_pairs={{0,96},{8,104},{16,112},{24,120},{32,64},{40,72},{48,80},{56,88},{... | collective-permute-start | bytes 786440 | tf_op jit(solution)/shard_map/ppermute | solution.py:31
  292.1 13.6 %collective-permute-start.13 = (bf16[2,128,512]{2,1,0:T(8,128)(2,1)S(1)}, bf16[2,128,512]{2,1,0:T(8,128)(2,1)S(1)}, u32[]{:S(2)}, u32[]{:S(2)}) collective-permute-start(bf16[2,128,512]{2,1,0:T(8,128)(2,1)S(1)} %get-tuple-element.66), channel_id=1, source_target_pairs={{0,64},{8,72},{16,80},{24,88},{32,96},{40,104},{48,112},{56,120},{... | collective-permute-start | bytes 786440 | tf_op jit(solution)/shard_map/ppermute | solution.py:31
  294.5 0.7 copy-start.15
  294.9 13.7 %collective-permute-start.17 = (bf16[4,128,512]{2,1,0:T(8,128)(2,1)S(1)}, bf16[4,128,512]{2,1,0:T(8,128)(2,1)S(1)}, u32[]{:S(2)}, u32[]{:S(2)}) collective-permute-start(bf16[4,128,512]{2,1,0:T(8,128)(2,1)S(1)} %fusion.7), channel_id=1, source_target_pairs={{0,16},{8,24},{16,0},{24,8},{32,48},{40,56},{48,32},{56,40},{64,80... | collective-permute-start | bytes 1572872 | tf_op jit(solution)/shard_map/ppermute | solution.py:31
  305.8 7.3 %collective-permute-start.15 = (bf16[128,512]{1,0:T(8,128)(2,1)S(1)}, bf16[128,512]{1,0:T(8,128)(2,1)S(1)}, u32[]{:S(2)}, u32[]{:S(2)}) collective-permute-start(bf16[128,512]{1,0:T(8,128)(2,1)S(1)} %fusion.31), channel_id=1, source_target_pairs={{0,16},{8,24},{16,0},{24,8},{32,48},{40,56},{48,32},{56,40},{64,80... | collective-permute-start | bytes 393224 | tf_op jit(solution)/shard_map/ppermute | solution.py:31
  308.9 5.4 %collective-permute-start.18 = (bf16[128,512]{1,0:T(8,128)(2,1)S(1)}, bf16[128,512]{1,0:T(8,128)(2,1)S(1)}, u32[]{:S(2)}, u32[]{:S(2)}) collective-permute-start(bf16[128,512]{1,0:T(8,128)(2,1)S(1)} %get-tuple-element.67), channel_id=1, source_target_pairs={{0,32},{8,40},{16,48},{24,56},{32,0},{40,8},{48,16},{56,24},{64,96... | collective-permute-start | bytes 393224 | tf_op jit(solution)/shard_map/ppermute | solution.py:31
  309.8 6.2 %collective-permute-start.20 = (bf16[128,512]{1,0:T(8,128)(2,1)S(1)}, bf16[128,512]{1,0:T(8,128)(2,1)S(1)}, u32[]{:S(2)}, u32[]{:S(2)}) collective-permute-start(bf16[128,512]{1,0:T(8,128)(2,1)S(1)} %get-tuple-element.68), channel_id=1, source_target_pairs={{0,96},{8,104},{16,112},{24,120},{32,64},{40,72},{48,80},{56,88},{... | collective-permute-start | bytes 393224 | tf_op jit(solution)/shard_map/ppermute | solution.py:31
  311.5 6.5 %collective-permute-start.19 = (bf16[128,512]{1,0:T(8,128)(2,1)S(1)}, bf16[128,512]{1,0:T(8,128)(2,1)S(1)}, u32[]{:S(2)}, u32[]{:S(2)}) collective-permute-start(bf16[128,512]{1,0:T(8,128)(2,1)S(1)} %get-tuple-element.69), channel_id=1, source_target_pairs={{0,64},{8,72},{16,80},{24,88},{32,96},{40,104},{48,112},{56,120},{... | collective-permute-start | bytes 393224 | tf_op jit(solution)/shard_map/ppermute | solution.py:31
Sparse Core Ops, SparseCore 0:
  45.6 39.0 all-gather.1

commit v3 on v2

--- a/solution.py
+++ b/solution.py
@@ -44,6 +44,10 @@
     return [
         (ref, start) for ref in refs for start in range(0, ref.shape[0], 2 * HD)
     ]
+
+
+def own_blocks(own_ref):
+    return [(own_ref, HD)]
 
 
 def load_keys(blocks, keys, values):
@@ -57,28 +61,21 @@
         values[:, span] = jnp.concatenate([ref[start + HD : start + 2 * HD, :], one], axis=0)
 
 
-def group_blocks(refs, count):
-    blocks = key_blocks(refs)
-    return [blocks[start : start + count] for start in range(0, len(blocks), count)]
-
-
 def add_blocks(count, width, query, keys, values, total):
-    chunk = width // 2
-
     def step(index, running):
-        span = pl.ds(pl.multiple_of(index * chunk, chunk), chunk)
+        span = pl.ds(pl.multiple_of(index * width, width), width)
         exponents = jnp.dot(keys[span, :], query, preferred_element_type=jnp.float32)
         weights = jnp.exp2(exponents).astype(jnp.bfloat16)
         return running + jnp.dot(values[:, span], weights, preferred_element_type=jnp.float32)
 
-    return lax.fori_loop(0, 2 * count, step, total)
-
-
-def first_keys_kernel(count, query_ref, *refs):
+    return lax.fori_loop(0, count, step, total)
+
+
+def first_keys_kernel(count, own_ref, *refs):
     blocks, (wide_ref, total_ref, keys, values) = refs[:-4], refs[-4:]
-    load_keys(key_blocks(blocks), keys, values)
-    width = query_ref.shape[1]
-    scaled = query_ref[...].astype(jnp.float32) * LOG2_SCALE
+    load_keys(own_blocks(own_ref) + key_blocks(blocks), keys, values)
+    width = own_ref.shape[1]
+    scaled = own_ref[:HD, :].astype(jnp.float32) * LOG2_SCALE
     pieces = split_terms(scaled, 3)
     wide_ref[...] = jnp.concatenate(pieces + [jnp.zeros_like(pieces[0])], axis=0)
     some = jnp.dot(keys[:SHIFT_KEYS, :], wide_ref[...], preferred_element_type=jnp.float32)
@@ -101,7 +98,7 @@
     )
 
 
-def last_keys_kernel(count, fresh, wide_ref, before_ref, query_ref, *refs):
+def last_keys_kernel(count, fresh, wide_ref, before_ref, own_ref, output_weight_ref, *refs):
     blocks, (out_ref, keys, values, total) = refs[:-4], refs[-4:]
     load_keys(key_blocks(blocks[:fresh]), keys, values)
     width = wide_ref.shape[1]
@@ -112,7 +109,7 @@
 
     @pl.when(outside > 0)
     def _():
-        query = query_ref[...]
+        query = own_ref[:HD, :]
         query = jnp.concatenate([query, jnp.zeros((3 * HD, width), query.dtype)], axis=0)
         total[...] = jnp.zeros(total.shape, jnp.float32)
 
@@ -129,14 +126,18 @@
             return new_top
 
         top = jnp.full((1, width), -1e30, jnp.float32)
-        for group in group_blocks(blocks, count):
+        every = own_blocks(own_ref) + key_blocks(blocks)
+        for group in [every[i : i + count] for i in range(0, len(every), count)]:
             load_keys(group, keys, values)
             top = lax.fori_loop(0, len(group) * (width // SHIFT_KEYS), step, top)
 
     attended = (total[:HD, :] / total[HD : HD + 1, :]).astype(jnp.bfloat16)
-    rows = out_ref.shape[2]
+    weight = output_weight_ref[...]
+    features = weight.shape[1]
+    rows = out_ref.shape[2] - features
     for index in range(out_ref.shape[0]):
-        out_ref[index] = attended[:, index * rows : (index + 1) * rows]
+        out_ref[index, :, :features] = weight
+        out_ref[index, :, features:] = attended[:, index * rows : (index + 1) * rows]
 
 
 def block_count(arrays):
@@ -165,30 +166,21 @@
     )(*operands)
 
 
-def double_by_exchange(rows, axis, distance):
-    other = hop(rows, axis, lambda i: i ^ distance)
-    upper = (lax.axis_index(axis) // distance) % 2 == 1
-    return jnp.concatenate(
-        [jnp.where(upper, other, rows), jnp.where(upper, rows, other)], axis=0
-    )
-
-
-def attention(query, keys_values, output_weight, expert_weights, owners):
-    width = query.shape[1]
+def near_hops(value):
+    return [hop(value, "blk", lambda i, step=step: i ^ step) for step in (2, 4, 12, 8)]
+
+
+def attention(projected, output_weight, expert_weights, owners):
+    width = projected.shape[1]
+    keys_values = projected[HD:]
     partner = hop(keys_values, "blk", lambda i: i ^ 1)
-    near = [
-        hop(keys_values, "blk", lambda i: i ^ 2),
-        hop(keys_values, "blk", lambda i: i + 4),
-        hop(keys_values, "blk", lambda i: i + 12),
-        hop(keys_values, "blk", lambda i: i + 8),
-    ]
+    near = near_hops(keys_values)
     total_shape = jax.ShapeDtypeStruct((HD + HD // 2, width), jnp.float32)
     wide_shape = jax.ShapeDtypeStruct((4 * HD, width), jnp.bfloat16)
-    first = [keys_values, partner]
     wide, total = attention_call(
         lambda *refs: first_keys_kernel(2, *refs),
         (wide_shape, total_shape),
-        [query, *first],
+        [projected, partner],
         2,
         width,
     )
@@ -204,31 +196,29 @@
             aliases={1: 0},
         )
 
-    near, output_weight, total = lax.optimization_barrier((near, output_weight, total))
+    near, total = lax.optimization_barrier((near, total))
     beyond = hop(jnp.concatenate(near[1:], axis=0), "blk", lambda i: i ^ 2)
     near_partner = hop(jnp.concatenate(near, axis=0), "blk", lambda i: i ^ 1)
-    output_weight = double_by_exchange(output_weight, "exp", 1)
     total = more(total, near)
-    beyond, output_weight, expert_weights, total = lax.optimization_barrier(
-        (beyond, output_weight, expert_weights, total)
-    )
+    beyond, expert_weights, total = lax.optimization_barrier((beyond, expert_weights, total))
     beyond_partner = hop(beyond, "blk", lambda i: i ^ 1)
-    output_weight = double_by_exchange(output_weight, "exp", 2)
-    expert_weights = lax.all_gather(expert_weights, "blk", axis=1, tiled=True)
+    beside = hop(expert_weights, "blk", lambda i: i ^ 2)
     total = more(total, [near_partner])
-    output_weight, total = lax.optimization_barrier((output_weight, total))
-    output_weight = double_by_exchange(output_weight, "exp", 4)
+    beside, beyond_partner, total = lax.optimization_barrier((beside, beyond_partner, total))
+    pair = jnp.stack([expert_weights, beside])
+    lane = [pair, *[hop(pair, "blk", lambda i, step=step: i ^ step) for step in (4, 8, 12)]]
     last = [beyond, beyond_partner]
     count = block_count(last)
+    features = output_weight.shape[1]
     attended = attention_call(
         lambda *refs: last_keys_kernel(count, len(last), *refs),
-        jax.ShapeDtypeStruct((owners, HD, width // owners), jnp.bfloat16),
-        [wide, total, query, *last, *first, *near, near_partner],
+        jax.ShapeDtypeStruct((owners, HD, features + width // owners), jnp.bfloat16),
+        [wide, total, projected, output_weight, *last, partner, *near, near_partner],
         count,
         width,
         extra=[pltpu.VMEM(total_shape.shape, jnp.float32)],
     )
-    return attended, output_weight, expert_weights
+    return attended, lane
 
 
 def sum_near(value, axis, distance):
@@ -253,11 +243,28 @@
     return jnp.tanh(TANH_SCALE * (values + CUBE * (values * values * values)))
 
 
-def expert_forward_kernel(rows_ref, in_ref, out_ref, result_ref, total):
+def tile_rows(lane_ref, partner_ref):
+    share, width = lane_ref.shape[1:]
+    return jnp.concatenate(
+        [ref[...].reshape(2 * share, width) for ref in (lane_ref, partner_ref)], axis=0
+    )
+
+
+def weight_specs(weights):
+    _, _, _, share, width = weights.shape
+    return [
+        pl.BlockSpec((None, 2, None, share, width), lambda i, which=which: (i, 0, which, 0, 0))
+        for which in (0, 0, 1, 1)
+    ]
+
+
+def expert_forward_kernel(rows_ref, in_lane, in_partner, out_lane, out_partner, result_ref, total):
     step = pl.program_id(0)
-    pre_act = dot_rows(rows_ref[...], in_ref[...])
+    pre_act = dot_rows(rows_ref[...], tile_rows(in_lane, in_partner))
     hidden = (pre_act * (0.5 * (1.0 + tanh_part(pre_act)))).astype(jnp.bfloat16)
-    part = jnp.dot(hidden, out_ref[...], preferred_element_type=jnp.float32)
+    part = jnp.dot(
+        hidden, tile_rows(out_lane, out_partner), preferred_element_type=jnp.float32
+    )
 
     @pl.when(step == 0)
     def _():
@@ -272,19 +279,14 @@
         result_ref[...] = total[...].astype(result_ref.dtype)
 
 
-def expert_forward(rows, weights):
+def expert_forward(rows, lane, partner):
     count, width = rows.shape
-    hidden = weights.shape[1]
-    tile = 512
+    hidden = lane.size // width
     return pl.pallas_call(
         expert_forward_kernel,
-        grid=(hidden // tile,),
+        grid=(lane.shape[0],),
         out_shape=jax.ShapeDtypeStruct((count, width), jnp.bfloat16),
-        in_specs=[
-            pl.BlockSpec((count, width), lambda i: (0, 0)),
-            pl.BlockSpec((None, tile, width), lambda i: (0, i, 0)),
-            pl.BlockSpec((None, tile, width), lambda i: (1, i, 0)),
-        ],
+        in_specs=[pl.BlockSpec((count, width), lambda i: (0, 0)), *weight_specs(lane)],
         out_specs=pl.BlockSpec((count, width), lambda i: (0, 0)),
         scratch_shapes=[pltpu.VMEM((count, width), jnp.float32)],
         compiler_params=pltpu.CompilerParams(vmem_limit_bytes=VMEM_LIMIT),
@@ -293,14 +295,22 @@
             transcendentals=count * hidden,
             bytes_accessed=4 * hidden * width,
         ),
-    )(rows, weights, weights)
-
-
-def expert_slopes_kernel(place_ref, rows_ref, *refs):
-    ins, outs = refs[:4], refs[4:8]
-    hidden_ref, slope_ref, out_weight_ref, in_weight_ref = refs[8:]
-    weight_in = jnp.concatenate([ref[...] for ref in ins], axis=0)
-    out_weight_ref[...] = jnp.concatenate([ref[...] for ref in outs], axis=0)
+    )(rows, lane, partner, lane, partner)
+
+
+def expert_slopes_kernel(
+    rows_ref,
+    in_lane,
+    in_partner,
+    out_lane,
+    out_partner,
+    hidden_ref,
+    slope_ref,
+    out_weight_ref,
+    in_weight_ref,
+):
+    weight_in = tile_rows(in_lane, in_partner)
+    out_weight_ref[...] = tile_rows(out_lane, out_partner)
     in_weight_ref[...] = weight_in.T
     pre_act = dot_rows(weight_in, rows_ref[...])
     tanh = tanh_part(pre_act)
@@ -311,40 +321,25 @@
     )
 
 
-def expert_slopes(place, rows, weights):
+def expert_slopes(rows, lane, partner):
     count, width = rows.shape
-    hidden = weights.shape[1]
-    share = hidden // 16
-    tile = 4 * share
-
-    def weight_spec(which, quarter):
-        def index(step, place):
-            z = jnp.bitwise_xor(step, place[0])
-            y = jnp.bitwise_xor(quarter // 2, place[1])
-            core = jnp.bitwise_xor(quarter % 2, place[2])
-            return (which, z * 4 + y * 2 + core, 0)
-
-        return pl.BlockSpec((None, share, width), index)
-
-    specs = [weight_spec(which, quarter) for which in range(2) for quarter in range(4)]
+    hidden = lane.size // width
+    tile = hidden // lane.shape[0]
     return pl.pallas_call(
         expert_slopes_kernel,
+        grid=(lane.shape[0],),
         out_shape=(
             jax.ShapeDtypeStruct((hidden, count), jnp.bfloat16),
             jax.ShapeDtypeStruct((hidden, count), jnp.float32),
             jax.ShapeDtypeStruct((hidden, width), jnp.bfloat16),
             jax.ShapeDtypeStruct((width, hidden), jnp.bfloat16),
         ),
-        grid_spec=pltpu.PrefetchScalarGridSpec(
-            num_scalar_prefetch=1,
-            grid=(hidden // tile,),
-            in_specs=[pl.BlockSpec((count, width), lambda i, place: (0, 0)), *specs],
-            out_specs=(
-                pl.BlockSpec((tile, count), lambda i, place: (i, 0)),
-                pl.BlockSpec((tile, count), lambda i, place: (i, 0)),
-                pl.BlockSpec((tile, width), lambda i, place: (i, 0)),
-                pl.BlockSpec((width, tile), lambda i, place: (0, i)),
-            ),
+        in_specs=[pl.BlockSpec((count, width), lambda i: (0, 0)), *weight_specs(lane)],
+        out_specs=(
+            pl.BlockSpec((tile, count), lambda i: (i, 0)),
+            pl.BlockSpec((tile, count), lambda i: (i, 0)),
+            pl.BlockSpec((tile, width), lambda i: (i, 0)),
+            pl.BlockSpec((width, tile), lambda i: (0, i)),
         ),
         compiler_params=pltpu.CompilerParams(vmem_limit_bytes=VMEM_LIMIT),
         cost_estimate=pl.CostEstimate(
@@ -352,15 +347,14 @@
             transcendentals=count * hidden,
             bytes_accessed=6 * count * hidden + 8 * hidden * width,
         ),
-    )(place, rows, *([weights] * 8))
+    )(rows, lane, partner, lane, partner)
 
 
 def store_shares(term, mine_ref, theirs_ref):
     share = mine_ref.shape[2]
     for y in range(2):
-        start = 2 * y * share
-        mine_ref[0, y] = term[start : start + share]
-        theirs_ref[0, y] = term[start + share : start + 2 * share].astype(theirs_ref.dtype)
+        mine_ref[0, y] = term[y * share : (y + 1) * share]
+        theirs_ref[0, y] = term[(y + 2) * share : (y + 3) * share].astype(theirs_ref.dtype)
 
 
 def expert_out_grad_kernel(scale, hidden_ref, grads_ref, mine_ref, theirs_ref):
@@ -372,18 +366,22 @@
     scale,
     slope_ref,
     out_weight_ref,
-    in_weight_ref,
     rows_ref,
     grads_ref,
     mine_ref,
     theirs_ref,
-    back_ref,
-    total,
+    pre_grad_ref,
 ):
-    step = pl.program_id(0)
     hidden_grad = dot_rows(out_weight_ref[...], grads_ref[...])
     pre_grad = (hidden_grad * slope_ref[...]).astype(jnp.bfloat16)
-    part = jnp.dot(in_weight_ref[...], pre_grad, preferred_element_type=jnp.float32)
+    pre_grad_ref[...] = pre_grad
+    term = jnp.dot(pre_grad, rows_ref[...], preferred_element_type=jnp.float32)
+    store_shares(term * scale, mine_ref, theirs_ref)
+
+
+def rows_back_kernel(pre_grad_ref, in_weight_ref, back_ref, total):
+    step = pl.program_id(0)
+    part = jnp.dot(in_weight_ref[...], pre_grad_ref[...], preferred_element_type=jnp.float32)
 
     @pl.when(step == 0)
     def _():
@@ -392,9 +390,6 @@
     @pl.when(step > 0)
     def _():
         total[...] += part
-
-    term = jnp.dot(pre_grad, rows_ref[...], preferred_element_type=jnp.float32)
-    store_shares(term * scale, mine_ref, theirs_ref)
 
     @pl.when(step == pl.num_programs(0) - 1)
     def _():
@@ -431,36 +426,59 @@
     )(hidden, grads)
 
 
-def expert_in_grad(slopes, out_weight, in_weight, rows, grads, scale):
+def expert_in_grad(slopes, out_weight, rows, grads, scale):
     units, count = slopes.shape
     width = grads.shape[1]
     shapes, specs = share_shapes(units, width)
     return pl.pallas_call(
         lambda *refs: expert_in_grad_kernel(scale, *refs),
         grid=(4,),
-        out_shape=(*shapes, jax.ShapeDtypeStruct((count, width), jnp.bfloat16)),
+        out_shape=(*shapes, jax.ShapeDtypeStruct((units, count), jnp.bfloat16)),
         in_specs=[
             pl.BlockSpec((units // 4, count), lambda i: (i, 0)),
             pl.BlockSpec((units // 4, width), lambda i: (i, 0)),
-            pl.BlockSpec((width, units // 4), lambda i: (0, i)),
             pl.BlockSpec((count, width), lambda i: (0, 0)),
             pl.BlockSpec((count, width), lambda i: (0, 0)),
         ],
-        out_specs=(*specs, pl.BlockSpec((count, width), lambda i: (0, 0))),
+        out_specs=(*specs, pl.BlockSpec((units // 4, count), lambda i: (i, 0))),
+        compiler_params=pltpu.CompilerParams(vmem_limit_bytes=VMEM_LIMIT),
+        cost_estimate=pl.CostEstimate(
+            flops=4 * units * count * width, transcendentals=0, bytes_accessed=6 * units * count
+        ),
+    )(slopes, out_weight, rows, grads)
+
+
+def rows_back(pre_grad, in_weight):
+    units, count = pre_grad.shape
+    width = in_weight.shape[0]
+    return pl.pallas_call(
+        rows_back_kernel,
+        grid=(4,),
+        out_shape=jax.ShapeDtypeStruct((count, width), jnp.bfloat16),
+        in_specs=[
+            pl.BlockSpec((units // 4, count), lambda i: (i, 0)),
+            pl.BlockSpec((width, units // 4), lambda i: (0, i)),
+        ],
+        out_specs=pl.BlockSpec((count, width), lambda i: (0, 0)),
         scratch_shapes=[pltpu.VMEM((width, count), jnp.float32)],
         compiler_params=pltpu.CompilerParams(vmem_limit_bytes=VMEM_LIMIT),
         cost_estimate=pl.CostEstimate(
-            flops=6 * units * count * width, transcendentals=0, bytes_accessed=4 * units * count
-        ),
-    )(slopes, out_weight, in_weight, rows, grads)
+            flops=units * count, transcendentals=0, bytes_accessed=count * width
+        ),
+    )(pre_grad, in_weight)
 
 
 def swap(block, distance):
-    return hop(block.astype(jnp.bfloat16), "blk", lambda i: i ^ distance).astype(jnp.float32)
-
-
-def sum_over_z(blocks):
-    return blocks[0] + (swap(blocks[1], 4) + (swap(blocks[2], 8) + swap(blocks[3], 12)))
+    return hop(block.astype(jnp.bfloat16), "blk", lambda i: i ^ distance)
+
+
+def swap_over_z(blocks):
+    return [swap(blocks[d], 4 * d) for d in (1, 2, 3)]
+
+
+def add_swapped(own, swapped):
+    first, second, third = [block.astype(jnp.float32) for block in swapped]
+    return own + (first + (second + third))
 
 
 def local(
@@ -484,27 +502,24 @@
     capacity = 4 * block_rows // (exp_count * exp_count)
     experts = router_weight.shape[0]
     grad_scale = 1.0 / math.sqrt(block_rows * blk_count)
-    block = lax.axis_index("blk")
-    place = jnp.stack([block // 4, (block // 2) % 2, block % 2]).astype(jnp.int32)
-    keys_values = jnp.einsum(
+    projected = jnp.einsum(
         "fd,td->ft",
-        attention_weights[1:].reshape(2 * features, width),
+        attention_weights.reshape(3 * features, width),
         nodes,
         preferred_element_type=jnp.float32,
     ).astype(jnp.bfloat16)
-    query = jnp.einsum(
-        "fd,td->ft", attention_weights[0], nodes, preferred_element_type=jnp.float32
-    ).astype(jnp.bfloat16)
-    attended, full_output_weight, all_weights = attention(
-        query,
-        keys_values,
-        output_weight,
-        jnp.concatenate([expert_in, expert_out], axis=0),
-        exp_count,
-    )
-    by_feature = exchange(attended).reshape(exp_count * features, own_rows)
+    attended, lane_parts = attention(
+        projected, output_weight, jnp.concatenate([expert_in, expert_out], axis=0), exp_count
+    )
+    from_heads = exchange(attended)
+    from_heads, lane_parts = lax.optimization_barrier((from_heads, lane_parts))
+    lane = jnp.stack(lane_parts)
+    lane_partner = hop(lane, "blk", lambda i: i ^ 1)
     attn_out = jnp.einsum(
-        "fr,fd->rd", by_feature, full_output_weight, preferred_element_type=jnp.float32
+        "hfr,hfd->rd",
+        from_heads[:, :, width:],
+        from_heads[:, :, :width],
+        preferred_element_type=jnp.float32,
     )
     own_nodes = lax.dynamic_slice_in_dim(
         nodes, lax.axis_index("exp") * own_rows, own_rows, 0
@@ -534,10 +549,11 @@
     )
     outgoing = outgoing.reshape(experts, capacity, width)
     arrived = exchange(outgoing).reshape(experts * capacity, width)
-    result = expert_forward(arrived, all_weights)
+    result = expert_forward(arrived, lane, lane_partner)
     returned = exchange(result.reshape(experts, capacity, width))
     kept, result = lax.optimization_barrier((arrived, result))
-    hidden, slopes, out_weight, in_weight = expert_slopes(place, kept, all_weights)
+    hidden, slopes, out_weight, in_weight = expert_slopes(kept, lane, lane_partner)
+    returned, hidden, slopes = lax.optimization_barrier((returned, hidden, slopes))
     expert_rows = jnp.einsum(
         "ps,pd->sd",
         dispatch_table,
@@ -557,8 +573,7 @@
     )
     small = jnp.concatenate([router_part, gain_part[None, :]], axis=0) * grad_scale
     small = sum_pair(sum_near(small, "exp", 1), "exp", 4)
-    small = sum_pair(sum_pair(sum_near(small, "blk", 4), "blk", 2), "blk", 1)
-    router_grad, gain_grad = small[:-1], small[-1]
+    small = sum_near(small, "blk", 4)
     assigned_grads = (
         (gates[..., None] * grad_two[:, None, :]).astype(jnp.bfloat16).reshape(2 * own_rows, width)
     )
@@ -568,16 +583,33 @@
     grad_arrived = exchange(grad_outgoing.reshape(experts, capacity, width)).reshape(
         experts * capacity, width
     )
+    grad_arrived, small = lax.optimization_barrier((grad_arrived, small))
     out_mine, out_theirs = expert_out_grad(hidden, grad_arrived, grad_scale)
-    in_mine, in_theirs, rows_back = expert_in_grad(
-        slopes, out_weight, in_weight, kept, grad_arrived, grad_scale
-    )
-    out_sums = out_mine + swap(out_theirs, 1)
-    out_sums = out_sums[:, 0] + swap(out_sums[:, 1], 2)
-    expert_out_grads = sum_over_z(out_sums)[None]
-    in_sums = sum_over_z(in_mine + swap(in_theirs, 1))
-    expert_in_grads = (in_sums[0] + swap(in_sums[1], 2))[None]
-    back_home = exchange(rows_back.reshape(experts, capacity, width))
+    out_sums = out_mine + swap(out_theirs, 1).astype(jnp.float32)
+    out_sent = out_sums[:, 1].astype(jnp.bfloat16)
+    out_beside = swap(out_sent, 2)
+    small = sum_pair(small, "blk", 2)
+    grad_arrived, out_sums, out_sent = lax.optimization_barrier(
+        (grad_arrived, out_sums, out_sent)
+    )
+    in_mine, in_theirs, pre_grad = expert_in_grad(
+        slopes, out_weight, kept, grad_arrived, grad_scale
+    )
+    in_swapped = swap(in_theirs, 1)
+    pre_grad, in_mine, small = lax.optimization_barrier((pre_grad, in_mine, small))
+    row_grads = rows_back(pre_grad, in_weight)
+    small = sum_pair(small, "blk", 1)
+    router_grad, gain_grad = small[:-1], small[-1]
+    in_mine, in_swapped, row_grads, out_beside = lax.optimization_barrier(
+        (in_mine, in_swapped, row_grads, out_beside)
+    )
+    in_sums = in_mine + in_swapped.astype(jnp.float32)
+    in_parts = swap_over_z(in_sums)
+    out_sums = out_sums[:, 0] + out_beside.astype(jnp.float32)
+    expert_out_grads = add_swapped(out_sums[0], swap_over_z(out_sums))[None]
+    in_sums = add_swapped(in_sums[0], in_parts)
+    expert_in_grads = (in_sums[0] + swap(in_sums[1], 2).astype(jnp.float32))[None]
+    back_home = exchange(row_grads.reshape(experts, capacity, width))
     back_rows = jnp.einsum(
         "ps,pd->sd",
         dispatch_table,

time: 327 us -> 317 us (0.969)
  between operations: 14.7 us -> 1.32 us
  local copies, waits for them, and re-layouts: 8.15 us -> 12.2 us
  starting transfers between devices: 56.5 us -> 60.3 us
    all_to_all x5, waiting for transfers between devices: 35.9 us -> 26.5 us  [exchange(): lax.all_to_all(buffer, 'exp', split_axis=0, concat_axis=0, tiled=True)]
    ppermute x30 -> x32, waiting for transfers between devices: 38 us -> 45 us  [hop(): lax.ppermute(value, axis, [(i, target(i) % count) for i in range(count)])]
    pallas_call x2 -> x3, Pallas kernels: 18.3 us -> 23.5 us  [the longest x1 9.63 us: expert_slopes(): pl.pallas_call(expert_slopes_kernel, grid=(lane.shape[0],), out_shape=(ja...]
    unnamed x43 -> x63, local copies, waits for them, and re-layouts: 2.75 us -> 7.8 us
    all_to_all x5, starting transfers between devices: 19.3 us -> 22.8 us  [exchange(): lax.all_to_all(buffer, 'exp', split_axis=0, concat_axis=0, tiled=True)]
    ppermute x30 -> x32, starting transfers between devices: 37.2 us -> 37.5 us  [hop(): lax.ppermute(value, axis, [(i, target(i) % count) for i in range(count)])]
  transfers between devices with their start and end apart: 36 -> 37, of which waited for: 16 -> 15; matrix products, arithmetic and copies ran while one was open for 6% -> 4% of each run, Pallas kernels for 40% -> 41%
where the time goes in v3:
time: 317 us; the launch traced here: 316 us
  Pallas kernels  150 us (47%)
  waiting for transfers between devices  71.6 us (23%)
  starting transfers between devices  60.3 us (19%)
  local copies, waits for them, and re-layouts  12.2 us (4%)
  other arithmetic  10.8 us (3%)
  matrix products  9.08 us (3%)
    pallas_call x4, Pallas kernels, attention_call(): pl.pallas_call(kernel, out_shape=out_shape, in_specs=specs * len(operands...  113 us
    ppermute x32, waiting for transfers between devices, hop(): lax.ppermute(value, axis, [(i, target(i) % count) for i in range(count)])  45 us
    ppermute x32, starting transfers between devices, hop(): lax.ppermute(value, axis, [(i, target(i) % count) for i in range(count)])  37.5 us
    all_to_all x5, waiting for transfers between devices, exchange(): lax.all_to_all(buffer, 'exp', split_axis=0, concat_axis=0, tiled=True)  26.5 us
    all_to_all x5, starting transfers between devices, exchange(): lax.all_to_all(buffer, 'exp', split_axis=0, concat_axis=0, tiled=True)  22.8 us
    pallas_call x1, Pallas kernels, expert_slopes(): pl.pallas_call(expert_slopes_kernel, grid=(lane.shape[0],), out_shape=(ja...  9.63 us
    pallas_call x1, Pallas kernels, expert_in_grad(): pl.pallas_call(lambda *refs: expert_in_grad_kernel(scale, *refs), grid=(4...  8.54 us
    pallas_call x1, Pallas kernels, expert_forward(): pl.pallas_call(expert_forward_kernel, grid=(lane.shape[0],), out_shape=ja...  7.95 us
  transfers between devices with their start and end apart: 37, of which 15 were waited for; matrix products, arithmetic and copies ran while one was open for 4% of the time, Pallas kernels for 41%

profile of v3, /device:TPU:0, one launch (start us, length us, event | category | flops | bytes accessed | tf_op | source)
XLA Modules:
  0.0 315.5 jit_solution(6303822259581075831)
XLA Ops:
  0.7 0.9 copy-done
  1.5 2.0 convolution_convert_fusion.refs_0_.refs_2_
  3.7 4.0 %collective-permute-start.4 = (bf16[64,1536]{1,0:T(8,128)(2,1)S(1)}, bf16[64,1536]{1,0:T(8,128)(2,1)S(1)}, u32[]{:S(2)}, u32[]{:S(2)}) collective-permute-start(bf16[64,1536]{1,0:T(8,128)(2,1)S(1)} %slice.108), channel_id=1, source_target_pairs={{0,64},{8,72},{16,80},{24,88},{32,96},{40,104},{48,112},{56,120},{... | collective-permute-start | bytes 589832 | tf_op jit(solution)/shard_map/ppermute | solution.py:31
  8.7 1.6 collective-permute-start.1
  11.0 6.5 %shard_map.145 = (bf16[128,1536]{1,0:T(8,128)(2,1)}, f32[48,1536]{1,0:T(8,128)}) custom-call(bf16[96,1536]{1,0:T(8,128)(2,1)} %copy-done.7, bf16[64,1536]{1,0:T(8,128)(2,1)} %copy-done.30), custom_call_target="tpu_custom_call" | custom-call | flops 5662310400 | bytes 393216 | tf_op jit(solution)/shard_map/pallas_call | solution.py:149
  18.3 1.7 collective-permute-start.5
  20.1 11.3 %shard_map.146.refs_1_ = f32[48,1536]{1,0:T(8,128)} custom-call(bf16[128,1536]{1,0:T(8,128)(2,1)} %get-tuple-element.48.refs_0_, f32[48,1536]{1,0:T(8,128)} %get-tuple-element.53.refs_1_, bf16[64,1536]{1,0:T(8,128)(2,1)} %copy-done.20, bf16[64,1536]{1,0:T(8,128)(2,1)} %copy-done.10, bf16[64,1536]{1,0:T(8,128)(2,1)} %copy-done.9, ...), custom_call_target="tpu_custom_call", output_to_operand_aliasing={{}: (1, {})} | custom-call | flops 11324620800 | bytes 786432 | tf_op jit(solution)/shard_map/pallas_call | solution.py:149
  31.4 1.8 collective-permute-done.5.refs_4_
  33.2 1.6 collective-permute-start.6
  34.8 0.9 copy-done.27
  35.7 11.3 %shard_map.147.refs_1_ = f32[48,1536]{1,0:T(8,128)} custom-call(bf16[128,1536]{1,0:T(8,128)(2,1)} %get-tuple-element.48.refs_0_, f32[48,1536]{1,0:T(8,128)} %shard_map.146.refs_1_, bf16[256,1536]{1,0:T(8,128)(2,1)} %copy-done.27), custom_call_target="tpu_custom_call", output_to_operand_aliasing={{}: (1, {})} | custom-call | flops 11324620800 | bytes 786432 | tf_op jit(solution)/shard_map/pallas_call | solution.py:149
  47.1 0.8 copy-done.29
  47.9 3.0 collective-permute-start.11
  51.0 1.0 collective-permute-start.9
  52.0 83.7 %shard_map.148 = bf16[8,32,704]{2,1,0:T(8,128)(2,1)} custom-call(bf16[128,1536]{1,0:T(8,128)(2,1)} %get-tuple-element.48.refs_0_, f32[48,1536]{1,0:T(8,128)} %shard_map.147.refs_1_, bf16[96,1536]{1,0:T(8,128)(2,1)} %copy-done.7, bf16[32,512]{1,0:T(8,128)(2,1)} %refs_3_.1, bf16[192,1536]{1,0:T(8,128)(2,1)} %copy-done.28, bf16[192,1536]{1,0:T(8,128)(2,1)} %copy-done.29, ...), custom_call_target="tpu_custom_call" | custom-call | flops 16986931200 | bytes 1179648 | tf_op jit(solution)/shard_map/pallas_call | solution.py:149
  135.7 6.7 %all-to-all-start = ((bf16[8,32,704]{2,1,0:T(8,128)(2,1)}), bf16[8,32,704]{2,1,0:T(8,128)(2,1)S(1)}, u32[]{:S(2)}, u32[]{:S(2)}) async-start(bf16[8,32,704]{2,1,0:T(8,128)(2,1)} %shard_map.148), calls=%async_computation | async-start | bytes 786432 | tf_op jit(solution)/shard_map/all_to_all | solution.py:26
  142.9 0.9 reduce-window.6
  143.7 8.7 %all-to-all-done = bf16[8,32,704]{2,1,0:T(8,128)(2,1)S(1)} async-done(((bf16[8,32,704]{2,1,0:T(8,128)(2,1)}), bf16[8,32,704]{2,1,0:T(8,128)(2,1)S(1)}, u32[]{:S(2)}, u32[]{:S(2)}) %all-to-all-start) | async-done | bytes 360480 | tf_op jit(solution)/shard_map/all_to_all | solution.py:26
  153.6 1.5 pad_maximum_fusion.in_lane.out_lane
  155.5 1.7 multiply_reduce_fusion.2
  157.2 0.7 copy-done.5
  158.5 1.5 convolution_convert_fusion.2
  160.0 3.5 %all-to-all-start.1 = ((bf16[8,96,512]{2,1,0:T(8,128)(2,1)}), bf16[8,96,512]{2,1,0:T(8,128)(2,1)S(1)}, u32[]{:S(2)}, u32[]{:S(2)}) async-start(bf16[8,96,512]{2,1,0:T(8,128)(2,1)} %bitcast.118), calls=%async_computation.1 | async-start | bytes 1572864 | tf_op jit(solution)/shard_map/all_to_all | solution.py:26
  163.8 1.1 eq.74
  165.1 13.5 %all-to-all-done.1 = bf16[8,96,512]{2,1,0:T(8,128)(2,1)S(1)} async-done(((bf16[8,96,512]{2,1,0:T(8,128)(2,1)}), bf16[8,96,512]{2,1,0:T(8,128)(2,1)S(1)}, u32[]{:S(2)}, u32[]{:S(2)}) %all-to-all-start.1) | async-done | bytes 786464 | tf_op jit(solution)/shard_map/all_to_all | solution.py:26
  178.5 0.9 copy-done.2
  179.4 7.9 %shard_map.149 = bf16[768,512]{1,0:T(8,128)(2,1)} custom-call(bf16[768,512]{1,0:T(8,128)(2,1)} %bitcast.107, bf16[4,2,2,128,512]{4,3,2,1,0:T(8,128)(2,1)} %copy-done.1, bf16[4,2,2,128,512]{4,3,2,1,0:T(8,128)(2,1)} %collective-permute-done.12.in_partner.out_partner, bf16[4,2,2,128,512]{4,3,2,1,0:T(8,128)(2,1)} %copy-done.1, ...), custom_call_target="tpu_custom_call" | custom-call | flops 3221225472 | bytes 4194304 | tf_op jit(solution)/shard_map/pallas_call | solution.py:285
  187.3 3.8 %all-to-all-start.2 = ((bf16[8,96,512]{2,1,0:T(8,128)(2,1)}), bf16[8,96,512]{2,1,0:T(8,128)(2,1)S(1)}, u32[]{:S(2)}, u32[]{:S(2)}) async-start(bf16[8,96,512]{2,1,0:T(8,128)(2,1)} %bitcast.117), calls=%async_computation.2 | async-start | bytes 1572864 | tf_op jit(solution)/shard_map/all_to_all | solution.py:26
  191.4 9.6 %shard_map.150 = (bf16[2048,768]{1,0:T(8,128)(2,1)}, f32[2048,768]{1,0:T(8,128)}, bf16[2048,512]{1,0:T(8,128)(2,1)}, bf16[512,2048]{1,0:T(8,128)(2,1)}) custom-call(bf16[768,512]{1,0:T(8,128)(2,1)} %bitcast.108, bf16[4,2,2,128,512]{4,3,2,1,0:T(8,128)(2,1)} %copy-done.1, bf16[4,2,2,128,512]{4,3,2,1,0:T(8,128)(2,1)} %collective-permute-done.12.in_partner.out_partner, ...), custom_call_target="tpu_custom_call" | custom-call | flops 1610612736 | bytes 17825792 | tf_op jit(solution)/shard_map/pallas_call | solution.py:328
  201.1 4.3 %all-to-all-done.2 = bf16[8,96,512]{2,1,0:T(8,128)(2,1)S(1)} async-done(((bf16[8,96,512]{2,1,0:T(8,128)(2,1)}), bf16[8,96,512]{2,1,0:T(8,128)(2,1)S(1)}, u32[]{:S(2)}, u32[]{:S(2)}) %all-to-all-start.2) | async-done | bytes 786464 | tf_op jit(solution)/shard_map/all_to_all | solution.py:26
  206.4 0.8 add_add_fusion
  208.3 1.6 convolution_convert_fusion.1
  209.9 3.5 %all-to-all-start.3 = ((bf16[8,96,512]{2,1,0:T(8,128)(2,1)}), bf16[8,96,512]{2,1,0:T(8,128)(2,1)S(1)}, u32[]{:S(2)}, u32[]{:S(2)}) async-start(bf16[8,96,512]{2,1,0:T(8,128)(2,1)} %bitcast.19), calls=%async_computation.3 | async-start | bytes 1572864 | tf_op jit(solution)/shard_map/all_to_all | solution.py:26
  213.7 3.5 %collective-permute-start.14 = (f32[9,512]{1,0:T(8,128)S(1)}, f32[9,512]{1,0:T(8,128)S(1)}, u32[]{:S(2)}, u32[]{:S(2)}) collective-permute-start(f32[9,512]{1,0:T(8,128)S(1)} %maximum_multiply_fusion), channel_id=1, source_target_pairs={{0,2},{1,3},{2,0},{3,1},{4,6},{5,7},{6,4},{7,5},{8,10},{9,11},{10,... | collective-permute-start | bytes 55304 | tf_op jit(solution)/shard_map/ppermute | solution.py:31
  217.2 1.2 collective-permute-start.15
  218.3 8.6 %collective-permute-done.14 = f32[9,512]{1,0:T(8,128)S(1)} collective-permute-done((f32[9,512]{1,0:T(8,128)S(1)}, f32[9,512]{1,0:T(8,128)S(1)}, u32[]{:S(2)}, u32[]{:S(2)}) %collective-permute-start.14) | collective-permute-done | bytes 18464 | tf_op jit(solution)/shard_map/ppermute | solution.py:31
  226.9 3.1 collective-permute-start.16
  230.0 2.4 collective-permute-done.16
  232.4 3.2 %collective-permute-start.19 = (f32[9,512]{1,0:T(8,128)S(1)}, f32[9,512]{1,0:T(8,128)S(1)}, u32[]{:S(2)}, u32[]{:S(2)}) collective-permute-start(f32[9,512]{1,0:T(8,128)S(1)} %add.120), channel_id=1, source_target_pairs={{0,96},{8,104},{16,112},{24,120},{32,64},{40,72},{48,80},{56,88},{... | collective-permute-start | bytes 55304 | tf_op jit(solution)/shard_map/ppermute | solution.py:31
  235.7 0.9 collective-permute-start.17
  236.6 1.3 collective-permute-done.19
  237.9 3.2 %collective-permute-done.18 = f32[9,512]{1,0:T(8,128)S(1)} collective-permute-done((f32[9,512]{1,0:T(8,128)S(1)}, f32[9,512]{1,0:T(8,128)S(1)}, u32[]{:S(2)}, u32[]{:S(2)}) %collective-permute-start.18) | collective-permute-done | bytes 18464 | tf_op jit(solution)/shard_map/ppermute | solution.py:31
  241.1 0.9 copy-done.11
  242.0 5.4 %shard_map.151 = (f32[4,2,128,512]{3,2,1,0:T(8,128)}, bf16[4,2,128,512]{3,2,1,0:T(8,128)(2,1)}) custom-call(bf16[2048,768]{1,0:T(8,128)(2,1)} %get-tuple-element.73.refs_0_, bf16[768,512]{1,0:T(8,128)(2,1)} %bitcast.114), custom_call_target="tpu_custom_call" | custom-call | flops 1610612736 | bytes 3145728 | tf_op jit(solution)/shard_map/pallas_call | solution.py:413
  247.4 2.9 collective-permute-done.20
  250.3 2.0 convert_add_fusion.1
  252.3 8.5 %shard_map.152 = (f32[4,2,128,512]{3,2,1,0:T(8,128)}, bf16[4,2,128,512]{3,2,1,0:T(8,128)(2,1)}, bf16[2048,768]{1,0:T(8,128)(2,1)}) custom-call(f32[2048,768]{1,0:T(8,128)} %get-tuple-element.70.refs_0_, bf16[2048,512]{1,0:T(8,128)(2,1)} %get-tuple-element.71.refs_1_, bf16[768,512]{1,0:T(8,128)(2,1)} %bitcast.109, bf16[768,512]{1,0:T(8,128)(2,1)} %bitcast.115), custom_call_target="tpu_custom_call" | custom-call | flops 3221225472 | bytes 9437184 | tf_op jit(solution)/shard_map/pallas_call | solution.py:433
  261.2 1.9 collective-permute-start.21
  263.1 12.8 %collective-permute-done.21 = f32[9,512]{1,0:T(8,128)S(1)} collective-permute-done((f32[9,512]{1,0:T(8,128)S(1)}, f32[9,512]{1,0:T(8,128)S(1)}, u32[]{:S(2)}, u32[]{:S(2)}) %collective-permute-start.21) | collective-permute-done | bytes 18464 | tf_op jit(solution)/shard_map/ppermute | solution.py:31
  275.9 5.9 %shard_map.153 = bf16[768,512]{1,0:T(8,128)(2,1)} custom-call(bf16[2048,768]{1,0:T(8,128)(2,1)} %get-tuple-element.82.pre_grad_ref, bf16[512,2048]{1,0:T(8,128)(2,1)} %get-tuple-element.83.in_weight_ref), custom_call_target="tpu_custom_call" | custom-call | flops 1572864 | bytes 393216 | tf_op jit(solution)/shard_map/pallas_call | solution.py:454
  283.0 0.8 copy-done.15
  283.8 5.2 %all-to-all-start.4 = ((bf16[8,96,512]{2,1,0:T(8,128)(2,1)}), bf16[8,96,512]{2,1,0:T(8,128)(2,1)S(1)}, u32[]{:S(2)}, u32[]{:S(2)}) async-start(bf16[8,96,512]{2,1,0:T(8,128)(2,1)} %bitcast.110), calls=%async_computation.4 | async-start | bytes 1572864 | tf_op jit(solution)/shard_map/all_to_all | solution.py:26
  289.0 2.3 fusion.44
  291.5 2.6 collective-permute-start.26
  294.1 1.5 collective-permute-start.25
  296.1 2.5 collective-permute-start.30
  298.6 2.1 collective-permute-done.24
  300.7 2.0 collective-permute-start.29
  302.7 4.9 %collective-permute-done.26 = bf16[2,128,512]{2,1,0:T(8,128)(2,1)S(1)} collective-permute-done((bf16[2,128,512]{2,1,0:T(8,128)(2,1)S(1)}, bf16[2,128,512]{2,1,0:T(8,128)(2,1)S(1)}, u32[]{:S(2)}, u32[]{:S(2)}) %collective-permute-start.26) | collective-permute-done | bytes 262176 | tf_op jit(solution)/shard_map/ppermute | solution.py:31
  308.0 1.1 collective-permute-done.28
  309.1 3.4 %collective-permute-done.30 = bf16[128,512]{1,0:T(8,128)(2,1)S(1)} collective-permute-done((bf16[128,512]{1,0:T(8,128)(2,1)S(1)}, bf16[128,512]{1,0:T(8,128)(2,1)S(1)}, u32[]{:S(2)}, u32[]{:S(2)}) %collective-permute-start.30) | collective-permute-done | bytes 131104 | tf_op jit(solution)/shard_map/ppermute | solution.py:31
  312.5 0.8 fusion.25
  313.2 0.7 fusion.27
  314.5 1.1 fusion.1
  (147 shorter events, 11.2 us)
Async XLA Ops:
  0.6 0.9 copy-start
  0.6 9.7 %copy-start.21 = (bf16[1,128,512]{2,1,0:T(8,128)(2,1)S(1)}, bf16[1,128,512]{2,1,0:T(8,128)(2,1)}, u32[]{:S(2)}) copy-start(bf16[1,128,512]{2,1,0:T(8,128)(2,1)} %param.17) | copy-start | bytes 393220
  0.7 9.7 %copy-start.22 = (bf16[1,128,512]{2,1,0:T(8,128)(2,1)S(1)}, bf16[1,128,512]{2,1,0:T(8,128)(2,1)}, u32[]{:S(2)}) copy-start(bf16[1,128,512]{2,1,0:T(8,128)(2,1)} %param.16) | copy-start | bytes 393220
  3.5 6.8 %copy-start.7 = (bf16[96,1536]{1,0:T(8,128)(2,1)}, bf16[96,1536]{1,0:T(8,128)(2,1)S(1)}, u32[]{:S(2)}) copy-start(bf16[96,1536]{1,0:T(8,128)(2,1)S(1)} %convolution_convert_fusion.refs_0_.refs_2_) | copy-start | bytes 884740
  3.6 6.8 %collective-permute-start = (bf16[64,1536]{1,0:T(8,128)(2,1)S(1)}, bf16[64,1536]{1,0:T(8,128)(2,1)S(1)}, u32[]{:S(2)}, u32[]{:S(2)}) collective-permute-start(bf16[64,1536]{1,0:T(8,128)(2,1)S(1)} %slice.108), channel_id=1, source_target_pairs={{0,8},{8,0},{16,24},{24,16},{32,40},{40,32},{48,56},{56,48},{64,72... | collective-permute-start | bytes 589832 | tf_op jit(solution)/shard_map/ppermute | solution.py:31
  3.7 13.9 %collective-permute-start.4 = (bf16[64,1536]{1,0:T(8,128)(2,1)S(1)}, bf16[64,1536]{1,0:T(8,128)(2,1)S(1)}, u32[]{:S(2)}, u32[]{:S(2)}) collective-permute-start(bf16[64,1536]{1,0:T(8,128)(2,1)S(1)} %slice.108), channel_id=1, source_target_pairs={{0,64},{8,72},{16,80},{24,88},{32,96},{40,104},{48,112},{56,120},{... | collective-permute-start | bytes 589832 | tf_op jit(solution)/shard_map/ppermute | solution.py:31
  7.7 9.9 %collective-permute-start.3 = (bf16[64,1536]{1,0:T(8,128)(2,1)S(1)}, bf16[64,1536]{1,0:T(8,128)(2,1)S(1)}, u32[]{:S(2)}, u32[]{:S(2)}) collective-permute-start(bf16[64,1536]{1,0:T(8,128)(2,1)S(1)} %slice.108), channel_id=1, source_target_pairs={{0,96},{8,104},{16,112},{24,120},{32,64},{40,72},{48,80},{56,88},{... | collective-permute-start | bytes 589832 | tf_op jit(solution)/shard_map/ppermute | solution.py:31
  8.4 9.8 %collective-permute-start.2 = (bf16[64,1536]{1,0:T(8,128)(2,1)S(1)}, bf16[64,1536]{1,0:T(8,128)(2,1)S(1)}, u32[]{:S(2)}, u32[]{:S(2)}) collective-permute-start(bf16[64,1536]{1,0:T(8,128)(2,1)S(1)} %slice.108), channel_id=1, source_target_pairs={{0,32},{8,40},{16,48},{24,56},{32,0},{40,8},{48,16},{56,24},{64,96... | collective-permute-start | bytes 589832 | tf_op jit(solution)/shard_map/ppermute | solution.py:31
  8.7 9.5 %collective-permute-start.1 = (bf16[64,1536]{1,0:T(8,128)(2,1)S(1)}, bf16[64,1536]{1,0:T(8,128)(2,1)S(1)}, u32[]{:S(2)}, u32[]{:S(2)}) collective-permute-start(bf16[64,1536]{1,0:T(8,128)(2,1)S(1)} %slice.108), channel_id=1, source_target_pairs={{0,16},{8,24},{16,0},{24,8},{32,48},{40,56},{48,32},{56,40},{64,80... | collective-permute-start | bytes 589832 | tf_op jit(solution)/shard_map/ppermute | solution.py:31
  17.6 2.5 copy-start.8
  17.6 2.5 copy-start.9
  18.2 1.9 copy-start.10
  18.2 1.9 copy-start.20
  18.3 15.0 %collective-permute-start.5 = (bf16[192,1536]{1,0:T(8,128)(2,1)S(1)}, bf16[192,1536]{1,0:T(8,128)(2,1)S(1)}, u32[]{:S(2)}, u32[]{:S(2)}) collective-permute-start(bf16[192,1536]{1,0:T(8,128)(2,1)S(1)} %pad_maximum_fusion.2), channel_id=1, source_target_pairs={{0,16},{8,24},{16,0},{24,8},{32,48},{40,56},{48,32},{56,40},{64,80... | collective-permute-start | bytes 1769480 | tf_op jit(solution)/shard_map/ppermute | solution.py:31
  20.0 14.8 %collective-permute-start.8 = (bf16[256,1536]{1,0:T(8,128)(2,1)S(1)}, bf16[256,1536]{1,0:T(8,128)(2,1)S(1)}, u32[]{:S(2)}, u32[]{:S(2)}) collective-permute-start(bf16[256,1536]{1,0:T(8,128)(2,1)S(1)} %pad_maximum_fusion.1), channel_id=1, source_target_pairs={{0,8},{8,0},{16,24},{24,16},{32,40},{40,32},{48,56},{56,48},{64,72... | collective-permute-start | bytes 2359304 | tf_op jit(solution)/shard_map/ppermute | solution.py:31
  33.2 13.8 %copy-start.28 = (bf16[192,1536]{1,0:T(8,128)(2,1)}, bf16[192,1536]{1,0:T(8,128)(2,1)S(1)}, u32[]{:S(2)}) copy-start(bf16[192,1536]{1,0:T(8,128)(2,1)S(1)} %collective-permute-done.5.refs_4_) | copy-start | bytes 1769476
  33.2 13.8 %collective-permute-start.6 = (bf16[2,128,512]{2,1,0:T(8,128)(2,1)S(1)}, bf16[2,128,512]{2,1,0:T(8,128)(2,1)S(1)}, u32[]{:S(2)}, u32[]{:S(2)}) collective-permute-start(bf16[2,128,512]{2,1,0:T(8,128)(2,1)S(1)} %pad_maximum_fusion.4), channel_id=1, source_target_pairs={{0,16},{8,24},{16,0},{24,8},{32,48},{40,56},{48,32},{56,40},{64,80... | collective-permute-start | bytes 786440 | tf_op jit(solution)/shard_map/ppermute | solution.py:31
  34.8 12.3 %collective-permute-start.7 = (bf16[192,1536]{1,0:T(8,128)(2,1)S(1)}, bf16[192,1536]{1,0:T(8,128)(2,1)S(1)}, u32[]{:S(2)}, u32[]{:S(2)}) collective-permute-start(bf16[192,1536]{1,0:T(8,128)(2,1)S(1)} %collective-permute-done.5.refs_4_), channel_id=1, source_target_pairs={{0,8},{8,0},{16,24},{24,16},{32,40},{40,32},{48,56},{56,48},{64,72... | collective-permute-start | bytes 1769480 | tf_op jit(solution)/shard_map/ppermute | solution.py:31
  34.8 0.9 copy-start.27
  47.0 0.8 copy-start.29
  47.9 94.6 %copy-start.24 = (s32[192,2]{0,1:T(2,128)S(1)}, s32[192,2]{0,1:T(2,128)}, u32[]{:S(2)}) copy-start(s32[192,2]{0,1:T(2,128)} %param.18) | copy-start | bytes 4612
  47.9 104.6 %collective-permute-start.11 = (bf16[2,2,128,512]{3,2,1,0:T(8,128)(2,1)S(1)}, bf16[2,2,128,512]{3,2,1,0:T(8,128)(2,1)S(1)}, u32[]{:S(2)}, u32[]{:S(2)}) collective-permute-start(bf16[2,2,128,512]{3,2,1,0:T(8,128)(2,1)S(1)} %pad_maximum_fusion.3), channel_id=1, source_target_pairs={{0,96},{8,104},{16,112},{24,120},{32,64},{40,72},{48,80},{56,88},{... | collective-permute-start | bytes 1572872 | tf_op jit(solution)/shard_map/ppermute | solution.py:31
  50.9 101.6 %collective-permute-start.10 = (bf16[2,2,128,512]{3,2,1,0:T(8,128)(2,1)S(1)}, bf16[2,2,128,512]{3,2,1,0:T(8,128)(2,1)S(1)}, u32[]{:S(2)}, u32[]{:S(2)}) collective-permute-start(bf16[2,2,128,512]{3,2,1,0:T(8,128)(2,1)S(1)} %pad_maximum_fusion.3), channel_id=1, source_target_pairs={{0,64},{8,72},{16,80},{24,88},{32,96},{40,104},{48,112},{56,120},{... | collective-permute-start | bytes 1572872 | tf_op jit(solution)/shard_map/ppermute | solution.py:31
  51.0 101.5 %collective-permute-start.9 = (bf16[2,2,128,512]{3,2,1,0:T(8,128)(2,1)S(1)}, bf16[2,2,128,512]{3,2,1,0:T(8,128)(2,1)S(1)}, u32[]{:S(2)}, u32[]{:S(2)}) collective-permute-start(bf16[2,2,128,512]{3,2,1,0:T(8,128)(2,1)S(1)} %pad_maximum_fusion.3), channel_id=1, source_target_pairs={{0,32},{8,40},{16,48},{24,56},{32,0},{40,8},{48,16},{56,24},{64,96... | collective-permute-start | bytes 1572872 | tf_op jit(solution)/shard_map/ppermute | solution.py:31
  135.7 16.8 %all-to-all-start = ((bf16[8,32,704]{2,1,0:T(8,128)(2,1)}), bf16[8,32,704]{2,1,0:T(8,128)(2,1)S(1)}, u32[]{:S(2)}, u32[]{:S(2)}) async-start(bf16[8,32,704]{2,1,0:T(8,128)(2,1)} %shard_map.148), calls=%async_computation | async-start | bytes 786432 | tf_op jit(solution)/shard_map/all_to_all | solution.py:26
  152.5 0.9 copy-start.17
  152.5 1.1 copy-start.18
  153.6 4.4 %copy-start.25 = (f32[512]{0:T(512)S(1)}, f32[512]{0:T(512)}, u32[]{:S(2)}) copy-start(f32[512]{0:T(512)} %param.14) | copy-start | bytes 6148
  155.1 4.9 %copy-start.1 = (bf16[4,2,2,128,512]{4,3,2,1,0:T(8,128)(2,1)}, bf16[4,2,2,128,512]{4,3,2,1,0:T(8,128)(2,1)S(1)}, u32[]{:S(2)}) copy-start(bf16[4,2,2,128,512]{4,3,2,1,0:T(8,128)(2,1)S(1)} %pad_maximum_fusion.in_lane.out_lane) | copy-start | bytes 6291460
  155.1 23.4 %collective-permute-start.12 = (bf16[4,2,2,128,512]{4,3,2,1,0:T(8,128)(2,1)S(1)}, bf16[4,2,2,128,512]{4,3,2,1,0:T(8,128)(2,1)}, u32[]{:S(2)}, u32[]{:S(2)}) collective-permute-start(bf16[4,2,2,128,512]{4,3,2,1,0:T(8,128)(2,1)S(1)} %pad_maximum_fusion.in_lane.out_lane), channel_id=1, source_target_pairs={{0,8},{8,0},{16,24},{24,16},{32,40},{40,32},{48,56},{56,48},{64,72... | collective-permute-start | bytes 6291464 | tf_op jit(solution)/shard_map/ppermute | solution.py:31
  158.1 6.8 %copy-start.3 = (bf16[192,512]{1,0:T(8,128)(2,1)}, bf16[192,512]{1,0:T(8,128)(2,1)S(1)}, u32[]{:S(2)}) copy-start(bf16[192,512]{1,0:T(8,128)(2,1)S(1)} %multiply_convert_fusion.3) | copy-start | bytes 589828
  158.5 6.4 %copy-start.23 = (bf16[8,512]{1,0:T(8,128)(2,1)S(1)}, bf16[8,512]{1,0:T(8,128)(2,1)}, u32[]{:S(2)}) copy-start(bf16[8,512]{1,0:T(8,128)(2,1)} %param.13) | copy-start | bytes 24580
  160.0 18.5 %all-to-all-start.1 = ((bf16[8,96,512]{2,1,0:T(8,128)(2,1)}), bf16[8,96,512]{2,1,0:T(8,128)(2,1)S(1)}, u32[]{:S(2)}, u32[]{:S(2)}) async-start(bf16[8,96,512]{2,1,0:T(8,128)(2,1)} %bitcast.118), calls=%async_computation.1 | async-start | bytes 1572864 | tf_op jit(solution)/shard_map/all_to_all | solution.py:26
  178.5 0.9 copy-start.2
  187.3 18.1 %all-to-all-start.2 = ((bf16[8,96,512]{2,1,0:T(8,128)(2,1)}), bf16[8,96,512]{2,1,0:T(8,128)(2,1)S(1)}, u32[]{:S(2)}, u32[]{:S(2)}) async-start(bf16[8,96,512]{2,1,0:T(8,128)(2,1)} %bitcast.117), calls=%async_computation.2 | async-start | bytes 1572864 | tf_op jit(solution)/shard_map/all_to_all | solution.py:26
  191.4 14.0 %copy-start.13 = (pred[192,2,768]{2,1,0:T(4,128)(4,1)S(1)}, pred[192,2,768]{2,1,0:T(4,128)(4,1)}, u32[]{:S(2)}) copy-start(pred[192,2,768]{2,1,0:T(4,128)(4,1)} %eq.74) | copy-start | bytes 884740
  201.1 4.9 %copy-start.6 = (f32[192,512]{1,0:T(8,128)S(1)}, f32[192,512]{1,0:T(8,128)}, u32[]{:S(2)}) copy-start(f32[192,512]{1,0:T(8,128)} %copy-done.5) | copy-start | bytes 1179652
  201.1 5.1 %copy-start.12 = (bf16[192,512]{1,0:T(8,128)(2,1)S(1)}, bf16[192,512]{1,0:T(8,128)(2,1)}, u32[]{:S(2)}) copy-start(bf16[192,512]{1,0:T(8,128)(2,1)} %param.19) | copy-start | bytes 589828
  201.1 5.1 %copy-start.26 = (f32[512]{0:T(512)S(1)}, f32[512]{0:T(512)}, u32[]{:S(2)}) copy-start(f32[512]{0:T(512)} %param.15) | copy-start | bytes 6148
  207.8 5.7 %copy-start.4 = (bf16[192,512]{1,0:T(8,128)(2,1)S(1)}, bf16[192,512]{1,0:T(8,128)(2,1)}, u32[]{:S(2)}) copy-start(bf16[192,512]{1,0:T(8,128)(2,1)} %copy-done.3) | copy-start | bytes 589828
  209.9 31.2 %all-to-all-start.3 = ((bf16[8,96,512]{2,1,0:T(8,128)(2,1)}), bf16[8,96,512]{2,1,0:T(8,128)(2,1)S(1)}, u32[]{:S(2)}, u32[]{:S(2)}) async-start(bf16[8,96,512]{2,1,0:T(8,128)(2,1)} %bitcast.19), calls=%async_computation.3 | async-start | bytes 1572864 | tf_op jit(solution)/shard_map/all_to_all | solution.py:26
  213.7 13.2 %collective-permute-start.14 = (f32[9,512]{1,0:T(8,128)S(1)}, f32[9,512]{1,0:T(8,128)S(1)}, u32[]{:S(2)}, u32[]{:S(2)}) collective-permute-start(f32[9,512]{1,0:T(8,128)S(1)} %maximum_multiply_fusion), channel_id=1, source_target_pairs={{0,2},{1,3},{2,0},{3,1},{4,6},{5,7},{6,4},{7,5},{8,10},{9,11},{10,... | collective-permute-start | bytes 55304 | tf_op jit(solution)/shard_map/ppermute | solution.py:31
  217.2 9.7 %collective-permute-start.15 = (f32[9,512]{1,0:T(8,128)S(1)}, f32[9,512]{1,0:T(8,128)S(1)}, u32[]{:S(2)}, u32[]{:S(2)}) collective-permute-start(f32[9,512]{1,0:T(8,128)S(1)} %maximum_multiply_fusion), channel_id=1, source_target_pairs={{0,3},{1,2},{2,1},{3,0},{4,7},{5,6},{6,5},{7,4},{8,11},{9,10},{10,... | collective-permute-start | bytes 55304 | tf_op jit(solution)/shard_map/ppermute | solution.py:31
  218.3 8.6 %collective-permute-start.13 = (f32[9,512]{1,0:T(8,128)S(1)}, f32[9,512]{1,0:T(8,128)S(1)}, u32[]{:S(2)}, u32[]{:S(2)}) collective-permute-start(f32[9,512]{1,0:T(8,128)S(1)} %maximum_multiply_fusion), channel_id=1, source_target_pairs={{0,1},{1,0},{2,3},{3,2},{4,5},{5,4},{6,7},{7,6},{8,9},{9,8},{10,11... | collective-permute-start | bytes 55304 | tf_op jit(solution)/shard_map/ppermute | solution.py:31
  226.9 5.5 %collective-permute-start.16 = (f32[9,512]{1,0:T(8,128)S(1)}, f32[9,512]{1,0:T(8,128)S(1)}, u32[]{:S(2)}, u32[]{:S(2)}) collective-permute-start(f32[9,512]{1,0:T(8,128)S(1)} %add_add_fusion.2), channel_id=1, source_target_pairs={{0,4},{1,5},{2,6},{3,7},{4,0},{5,1},{6,2},{7,3},{8,12},{9,13},{10,... | collective-permute-start | bytes 55304 | tf_op jit(solution)/shard_map/ppermute | solution.py:31
  232.4 5.5 %collective-permute-start.19 = (f32[9,512]{1,0:T(8,128)S(1)}, f32[9,512]{1,0:T(8,128)S(1)}, u32[]{:S(2)}, u32[]{:S(2)}) collective-permute-start(f32[9,512]{1,0:T(8,128)S(1)} %add.120), channel_id=1, source_target_pairs={{0,96},{8,104},{16,112},{24,120},{32,64},{40,72},{48,80},{56,88},{... | collective-permute-start | bytes 55304 | tf_op jit(solution)/shard_map/ppermute | solution.py:31
  235.7 5.4 %collective-permute-start.18 = (f32[9,512]{1,0:T(8,128)S(1)}, f32[9,512]{1,0:T(8,128)S(1)}, u32[]{:S(2)}, u32[]{:S(2)}) collective-permute-start(f32[9,512]{1,0:T(8,128)S(1)} %add.120), channel_id=1, source_target_pairs={{0,64},{8,72},{16,80},{24,88},{32,96},{40,104},{48,112},{56,120},{... | collective-permute-start | bytes 55304 | tf_op jit(solution)/shard_map/ppermute | solution.py:31
  235.7 5.4 %collective-permute-start.17 = (f32[9,512]{1,0:T(8,128)S(1)}, f32[9,512]{1,0:T(8,128)S(1)}, u32[]{:S(2)}, u32[]{:S(2)}) collective-permute-start(f32[9,512]{1,0:T(8,128)S(1)} %add.120), channel_id=1, source_target_pairs={{0,32},{8,40},{16,48},{24,56},{32,0},{40,8},{48,16},{56,24},{64,96... | collective-permute-start | bytes 55304 | tf_op jit(solution)/shard_map/ppermute | solution.py:31
  241.1 0.9 copy-start.11
  247.4 2.9 collective-permute-start.20
  260.9 22.2 %collective-permute-start.22 = (bf16[4,2,128,512]{3,2,1,0:T(8,128)(2,1)}, bf16[4,2,128,512]{3,2,1,0:T(8,128)(2,1)}, u32[]{:S(2)}, u32[]{:S(2)}) collective-permute-start(bf16[4,2,128,512]{3,2,1,0:T(8,128)(2,1)} %get-tuple-element.81), channel_id=1, source_target_pairs={{0,8},{8,0},{16,24},{24,16},{32,40},{40,32},{48,56},{56,48},{64,72... | collective-permute-start | bytes 3145736 | tf_op jit(solution)/shard_map/ppermute | solution.py:31
  261.0 22.0 %collective-permute-start.23 = (bf16[4,128,512]{2,1,0:T(8,128)(2,1)S(1)}, bf16[4,128,512]{2,1,0:T(8,128)(2,1)S(1)}, u32[]{:S(2)}, u32[]{:S(2)}) collective-permute-start(bf16[4,128,512]{2,1,0:T(8,128)(2,1)S(1)} %fusion.7), channel_id=1, source_target_pairs={{0,16},{8,24},{16,0},{24,8},{32,48},{40,56},{48,32},{56,40},{64,80... | collective-permute-start | bytes 1572872 | tf_op jit(solution)/shard_map/ppermute | solution.py:31
  261.2 14.8 %collective-permute-start.21 = (f32[9,512]{1,0:T(8,128)S(1)}, f32[9,512]{1,0:T(8,128)S(1)}, u32[]{:S(2)}, u32[]{:S(2)}) collective-permute-start(f32[9,512]{1,0:T(8,128)S(1)} %add_add_fusion.1), channel_id=1, source_target_pairs={{0,16},{8,24},{16,0},{24,8},{32,48},{40,56},{48,32},{56,40},{64,80... | collective-permute-start | bytes 55304 | tf_op jit(solution)/shard_map/ppermute | solution.py:31
  275.9 5.9 %collective-permute-start.31 = (f32[9,512]{1,0:T(8,128)S(1)}, f32[9,512]{1,0:T(8,128)S(1)}, u32[]{:S(2)}, u32[]{:S(2)}) collective-permute-start(f32[9,512]{1,0:T(8,128)S(1)} %add.125), channel_id=1, source_target_pairs={{0,8},{8,0},{16,24},{24,16},{32,40},{40,32},{48,56},{56,48},{64,72... | collective-permute-start | bytes 55304 | tf_op jit(solution)/shard_map/ppermute | solution.py:31
  283.8 30.1 %all-to-all-start.4 = ((bf16[8,96,512]{2,1,0:T(8,128)(2,1)}), bf16[8,96,512]{2,1,0:T(8,128)(2,1)S(1)}, u32[]{:S(2)}, u32[]{:S(2)}) async-start(bf16[8,96,512]{2,1,0:T(8,128)(2,1)} %bitcast.110), calls=%async_computation.4 | async-start | bytes 1572864 | tf_op jit(solution)/shard_map/all_to_all | solution.py:26
  289.0 6.6 %copy-start.16 = (bf16[4,128,512]{2,1,0:T(8,128)(2,1)S(1)}, bf16[4,128,512]{2,1,0:T(8,128)(2,1)}, u32[]{:S(2)}) copy-start(bf16[4,128,512]{2,1,0:T(8,128)(2,1)} %copy-done.15) | copy-start | bytes 1572868
  291.4 9.2 %collective-permute-start.24 = (bf16[2,128,512]{2,1,0:T(8,128)(2,1)S(1)}, bf16[2,128,512]{2,1,0:T(8,128)(2,1)S(1)}, u32[]{:S(2)}, u32[]{:S(2)}) collective-permute-start(bf16[2,128,512]{2,1,0:T(8,128)(2,1)S(1)} %get-tuple-element.100), channel_id=1, source_target_pairs={{0,32},{8,40},{16,48},{24,56},{32,0},{40,8},{48,16},{56,24},{64,96... | collective-permute-start | bytes 786440 | tf_op jit(solution)/shard_map/ppermute | solution.py:31
  291.5 16.0 %collective-permute-start.26 = (bf16[2,128,512]{2,1,0:T(8,128)(2,1)S(1)}, bf16[2,128,512]{2,1,0:T(8,128)(2,1)S(1)}, u32[]{:S(2)}, u32[]{:S(2)}) collective-permute-start(bf16[2,128,512]{2,1,0:T(8,128)(2,1)S(1)} %get-tuple-element.101), channel_id=1, source_target_pairs={{0,96},{8,104},{16,112},{24,120},{32,64},{40,72},{48,80},{56,88},{... | collective-permute-start | bytes 786440 | tf_op jit(solution)/shard_map/ppermute | solution.py:31
  294.1 13.5 %collective-permute-start.25 = (bf16[2,128,512]{2,1,0:T(8,128)(2,1)S(1)}, bf16[2,128,512]{2,1,0:T(8,128)(2,1)S(1)}, u32[]{:S(2)}, u32[]{:S(2)}) collective-permute-start(bf16[2,128,512]{2,1,0:T(8,128)(2,1)S(1)} %get-tuple-element.102), channel_id=1, source_target_pairs={{0,64},{8,72},{16,80},{24,88},{32,96},{40,104},{48,112},{56,120},{... | collective-permute-start | bytes 786440 | tf_op jit(solution)/shard_map/ppermute | solution.py:31
  295.8 18.1 %copy-start.14 = (pred[192,2,768]{2,1,0:T(4,128)(4,1)S(1)}, pred[192,2,768]{2,1,0:T(4,128)(4,1)}, u32[]{:S(2)}) copy-start(pred[192,2,768]{2,1,0:T(4,128)(4,1)} %eq.74) | copy-start | bytes 884740
  295.9 13.2 %collective-permute-start.28 = (bf16[128,512]{1,0:T(8,128)(2,1)S(1)}, bf16[128,512]{1,0:T(8,128)(2,1)S(1)}, u32[]{:S(2)}, u32[]{:S(2)}) collective-permute-start(bf16[128,512]{1,0:T(8,128)(2,1)S(1)} %get-tuple-element.103), channel_id=1, source_target_pairs={{0,32},{8,40},{16,48},{24,56},{32,0},{40,8},{48,16},{56,24},{64,96... | collective-permute-start | bytes 393224 | tf_op jit(solution)/shard_map/ppermute | solution.py:31
  296.1 16.4 %collective-permute-start.30 = (bf16[128,512]{1,0:T(8,128)(2,1)S(1)}, bf16[128,512]{1,0:T(8,128)(2,1)S(1)}, u32[]{:S(2)}, u32[]{:S(2)}) collective-permute-start(bf16[128,512]{1,0:T(8,128)(2,1)S(1)} %get-tuple-element.104), channel_id=1, source_target_pairs={{0,96},{8,104},{16,112},{24,120},{32,64},{40,72},{48,80},{56,88},{... | collective-permute-start | bytes 393224 | tf_op jit(solution)/shard_map/ppermute | solution.py:31
  300.7 11.8 %collective-permute-start.29 = (bf16[128,512]{1,0:T(8,128)(2,1)S(1)}, bf16[128,512]{1,0:T(8,128)(2,1)S(1)}, u32[]{:S(2)}, u32[]{:S(2)}) collective-permute-start(bf16[128,512]{1,0:T(8,128)(2,1)S(1)} %get-tuple-element.105), channel_id=1, source_target_pairs={{0,64},{8,72},{16,80},{24,88},{32,96},{40,104},{48,112},{56,120},{... | collective-permute-start | bytes 393224 | tf_op jit(solution)/shard_map/ppermute | solution.py:31
  307.7 5.5 %collective-permute-start.27 = (bf16[128,512]{1,0:T(8,128)(2,1)S(1)}, bf16[128,512]{1,0:T(8,128)(2,1)S(1)}, u32[]{:S(2)}, u32[]{:S(2)}) collective-permute-start(bf16[128,512]{1,0:T(8,128)(2,1)S(1)} %fusion.29), channel_id=1, source_target_pairs={{0,16},{8,24},{16,0},{24,8},{32,48},{40,56},{48,32},{56,40},{64,80... | collective-permute-start | bytes 393224 | tf_op jit(solution)/shard_map/ppermute | solution.py:31
  (4 other events, 3.0 us)
